TPU v7x, 32 devices: a whole 2x2x4 slice. The times are simulated.
32 devices in a mesh: seq: 4 (over y, core), fsdp: 8 (over z, x).
Axes of the slice: x: 2, y: 2, z: 4, core: 2. Of those that a mesh axis runs over, the one named last changes fastest.
Arguments:
- activations: bfloat16 [24, 1024, 768], P('fsdp', 'seq'), may hold values from -6 to 6
- cotangent: bfloat16 [24, 1024, 768], P('fsdp', 'seq'), may hold values from -6 to 6
- lengths: int32 [24], P('fsdp'), may hold values from 512 to 1024, as said below
- w_qkv: bfloat16 [768, 2304], P('fsdp'), may hold values from -0.21875 to 0.21875
- w_out: bfloat16 [768, 768], P('fsdp'), may hold values from -0.375 to 0.375
- w_fc1: bfloat16 [768, 3072], P('fsdp'), may hold values from -0.21875 to 0.21875
- w_fc2: bfloat16 [3072, 768], P('fsdp'), may hold values from -0.1875 to 0.1875
- d_gains: bfloat16 [768, 3], P('fsdp'), may hold values from 0.5 to 1.5
- d_biases: bfloat16 [768, 7], P('fsdp'), may hold values from -3 to 3
- ff_gain: bfloat16 [3072], P('fsdp'), may hold values from 0.5 to 1.5
- ff_biases: bfloat16 [3072, 2], P('fsdp'), may hold values from -3 to 3
Outputs:
- block_out: bfloat16 [24, 1024, 768], P('fsdp', 'seq')
- input_grad: float32 [24, 1024, 768], P('fsdp', 'seq')
- w_qkv_grad: float32 [768, 2304], P('fsdp')
- w_out_grad: float32 [768, 768], P('fsdp')
- w_fc1_grad: float32 [768, 3072], P('fsdp')
- w_fc2_grad: float32 [3072, 768], P('fsdp')
- d_gains_grad: float32 [768, 3], P('fsdp')
- d_biases_grad: float32 [768, 7], P('fsdp')
- ff_gain_grad: float32 [3072], P('fsdp')
- ff_biases_grad: float32 [3072, 2], P('fsdp')
Inputs may be any that keep to these rules, and one draw needn't show every extreme that they name: `lengths`: slots of a sequence from its length on are padding. One sequence has exactly 1024 live tokens and one exactly 512.
All inputs are finite; a program needn't handle non-finite values.
Results may differ from a plain program's by a relative error of at most 0.0085.
Values may be sent and summed in bfloat16 or wider, within the bound.
No kernel may reach another device: no remote copies, remote signals or barrier semaphores. Data moves between devices by JAX's collectives and lax.ppermute only.
A program may use at most 192 MiB of HBM per device.

v0:
```python
import functools

import jax
import jax.numpy as jnp
from jax import lax
from jax.experimental import pallas as pl
from jax.experimental.pallas import tpu as pltpu
from jax.sharding import PartitionSpec as P


HD = 64
eps = 1e-05
F32 = jnp.float32
BF16 = jnp.bfloat16
NT = (((1,), (1,)), ((), ()))


def mm(left, right):
    return jnp.dot(left, right, preferred_element_type=F32)


def mm_nt(left, right):
    return lax.dot_general(left, right, NT, preferred_element_type=F32)


def mm_tn(left, right):
    return lax.dot_general(left, right, (((0,), (0,)), ((), ())), preferred_element_type=F32)


def centred(values):
    center = values - jnp.mean(values, axis=-1, keepdims=True)
    spread = jnp.mean(center * center, axis=-1, keepdims=True)
    scale = lax.rsqrt(spread + eps)
    return center * scale, scale


def norm_back(grad, unit, scale):
    return scale * (
        grad
        - jnp.mean(grad, axis=-1, keepdims=True)
        - unit * jnp.mean(grad * unit, axis=-1, keepdims=True)
    )


def key_mask(block, live_rows):
    rows = lax.broadcasted_iota(jnp.int32, block.shape, 0)
    return jnp.where(rows < live_rows, block, -1e30)


def attend_kernel(parts, heads, rows, info, *refs):
    xs = refs[:parts]
    w, gain, shift, bias = refs[parts : parts + 4]
    stored = refs[parts + 4 : parts + 9]
    outs = refs[parts + 9 : 2 * parts + 9]
    lse, nrm, q, k, v, kt, vt, ot, sems = refs[2 * parts + 9 :]
    me, live = info[0], info[1]
    span = heads * HD
    for j in range(parts):
        g = me ^ j
        at = pl.ds(pl.multiple_of(g * rows, rows), rows)
        unit, _ = centred(xs[j][...].astype(F32))
        normed = (unit * gain[...] + shift[...]).astype(BF16)
        nrm[j] = normed
        qkv = mm(normed, w[...]) + bias[...]
        for h in range(heads):
            cols = slice(h * HD, (h + 1) * HD)
            kk = qkv[:, span + h * HD : span + (h + 1) * HD]
            vv = qkv[:, 2 * span + h * HD : 2 * span + (h + 1) * HD]
            q[h, at, :] = (qkv[:, cols].astype(BF16).astype(F32) * 0.125).astype(BF16)
            k[h, at, :] = kk.astype(BF16)
            v[h, at, :] = vv.astype(BF16)
            kt[h, g] = kk.T.astype(BF16)
            vt[h, g] = vv.T.astype(BF16)
    copies = [
        pltpu.make_async_copy(source, target, sems.at[index])
        for index, (source, target) in enumerate(zip((nrm, q, k, v, kt), stored))
    ]
    for copy in copies:
        copy.start()

    def variant(count):
        def step(t, carry):
            h, j = t // parts, t % parts
            g = me ^ j

            @pl.when(g < count)
            def _():
                qb = q[h, pl.ds(pl.multiple_of(g * rows, rows), rows), :]
                scores = [
                    mm_nt(k[h, c * rows : (c + 1) * rows, :], qb) for c in range(count)
                ]
                scores[-1] = key_mask(scores[-1], live - (count - 1) * rows)
                top = functools.reduce(
                    jnp.maximum, [jnp.max(s, axis=0, keepdims=True) for s in scores]
                )
                total, mixed = 0.0, 0.0
                for c in range(count):
                    e = jnp.exp(scores[c] - top)
                    total = total + jnp.sum(e, axis=0, keepdims=True)
                    mixed = mixed + mm(vt[h, c], e.astype(BF16))
                ot[t] = mixed / total
                lse[t] = jnp.broadcast_to(top + jnp.log(total), (8, rows))

            @pl.when(g >= count)
            def _():
                ot[t] = jnp.zeros((HD, rows), F32)
                lse[t] = jnp.zeros((8, rows), F32)

            return carry

        lax.fori_loop(0, heads * parts, step, 0)

    blocks = (live + rows - 1) // rows
    for count in range(1, parts + 1):
        pl.when(blocks == count)(functools.partial(variant, count))
    for j in range(parts):
        stacked = jnp.concatenate([ot[h * parts + j] for h in range(heads)], axis=0)
        outs[j][...] = stacked.T.astype(BF16)
    for copy in copies:
        copy.wait()


def whole(*arrays):
    return [pl.BlockSpec(a.shape, lambda i, n=a.ndim: (0,) * n) for a in arrays]


def attend_forward(place, live, xs, w, gain, shift, bias):
    parts, (rows, width) = len(xs), xs[0].shape
    span = w.shape[1] // 3
    heads, full = span // HD, parts * rows
    shape = jax.ShapeDtypeStruct
    kept = [(parts, rows, width)] + [(heads, full, HD)] * 3 + [(heads, parts, HD, rows)]
    outs_like, lse_like = shape((rows, span), BF16), shape((heads * parts, 8, rows), F32)
    outs = pl.pallas_call(
        functools.partial(attend_kernel, parts, heads, rows),
        grid=(1,),
        in_specs=[pl.BlockSpec(memory_space=pltpu.SMEM)] + whole(*xs, w, gain, shift, bias),
        out_specs=[pl.BlockSpec(memory_space=pltpu.HBM)] * 5
        + whole(*[outs_like] * parts, lse_like),
        out_shape=[shape(dims, BF16) for dims in kept]
        + [outs_like] * parts
        + [lse_like],
        scratch_shapes=[pltpu.VMEM(dims, BF16) for dims in kept]
        + [
            pltpu.VMEM((heads, parts, HD, rows), BF16),
            pltpu.VMEM((heads * parts, HD, rows), F32),
            pltpu.SemaphoreType.DMA((5,)),
        ],
        cost_estimate=pl.CostEstimate(
            flops=2 * full * width * 3 * span + 4 * full * full * span,
            bytes_accessed=2 * (2 * full * width + width * 3 * span + 6 * full * span),
            transcendentals=heads * full * full,
        ),
        compiler_params=pltpu.CompilerParams(vmem_limit_bytes=60 << 20),
        name="attend_forward",
    )(jnp.stack([place, live]), *xs, w, gain, shift, bias)
    return outs[0], outs[1:5], outs[5 : 5 + parts], outs[5 + parts]


def attend_back_kernel(parts, heads, rows, info, *refs):
    xs, grads = refs[:parts], refs[parts : 2 * parts]
    w, q, k, v, kt, lse = refs[2 * parts : 2 * parts + 6]
    dqkv = refs[2 * parts + 6]
    dns = refs[2 * parts + 7 : 3 * parts + 7]
    sums, cols = refs[3 * parts + 7 : 3 * parts + 9]
    do, dk, dv, dqt = refs[3 * parts + 9 :]
    me, live = info[0], info[1]
    for j in range(parts):
        block = grads[j][...].astype(F32)
        for h in range(heads):
            do[h * parts + j] = block[:, h * HD : (h + 1) * HD].astype(BF16)
    dk[...] = jnp.zeros_like(dk)
    dv[...] = jnp.zeros_like(dv)

    def variant(count):
        def step(t, carry):
            h, j = t // parts, t % parts
            g = me ^ j

            @pl.when(g < count)
            def _():
                qb = q[h, pl.ds(pl.multiple_of(g * rows, rows), rows), :]
                dob = do[t]
                shift = lse[t][0:1, :]
                probs, dps, inner = [], [], 0.0
                for c in range(count):
                    span = slice(c * rows, (c + 1) * rows)
                    s = mm_nt(k[h, span, :], qb)
                    if c == count - 1:
                        s = key_mask(s, live - c * rows)
                    p = jnp.exp(s - shift)
                    dp = mm_nt(v[h, span, :], dob)
                    inner = inner + jnp.sum(p * dp, axis=0, keepdims=True)
                    dv[h, c] += mm(p.astype(BF16), dob)
                    probs.append(p)
                    dps.append(dp)
                dq = 0.0
                for c in range(count):
                    ds = (probs[c] * (dps[c] - inner)).astype(BF16)
                    dk[h, c] += mm(ds, qb)
                    dq = dq + mm(kt[h, c], ds)
                dqt[t] = dq * 0.125

            @pl.when(g >= count)
            def _():
                dqt[t] = jnp.zeros((HD, rows), F32)

            return carry

        lax.fori_loop(0, heads * parts, step, 0)

    blocks = (live + rows - 1) // rows
    for count in range(1, parts + 1):
        pl.when(blocks == count)(functools.partial(variant, count))
    shift_sum, gain_sum, col_sum = 0.0, 0.0, 0.0
    for j in range(parts):
        g = me ^ j
        dq = jnp.concatenate([dqt[h * parts + j] for h in range(heads)], axis=0).T
        pieces = [dq] + [dk[h, g] for h in range(heads)] + [dv[h, g] for h in range(heads)]
        block = jnp.concatenate(pieces, axis=1).astype(BF16)
        dqkv[j] = block
        col_sum = col_sum + jnp.sum(block.astype(F32), axis=0, keepdims=True)
        dn = mm_nt(block, w[...])
        unit, _ = centred(xs[j][...].astype(F32))
        shift_sum = shift_sum + jnp.sum(dn, axis=0, keepdims=True)
        gain_sum = gain_sum + jnp.sum(dn * unit, axis=0, keepdims=True)
        dns[j][...] = dn.astype(BF16)
    sums[0:1, :] = gain_sum
    sums[1:2, :] = shift_sum
    cols[0:1, :] = col_sum


def attend_backward(place, live, xs, grads, w, saved, lse):
    parts, (rows, width) = len(xs), xs[0].shape
    span = w.shape[1] // 3
    heads, full = span // HD, parts * rows
    shape = jax.ShapeDtypeStruct
    out_shape = [
        shape((parts, rows, 3 * span), BF16),
        *[shape((rows, width), BF16)] * parts,
        shape((2, width), F32),
        shape((1, 3 * span), F32),
    ]
    outs = pl.pallas_call(
        functools.partial(attend_back_kernel, parts, heads, rows),
        grid=(1,),
        in_specs=[pl.BlockSpec(memory_space=pltpu.SMEM)] + whole(*xs, *grads, w, *saved, lse),
        out_specs=whole(*out_shape),
        out_shape=out_shape,
        scratch_shapes=[
            pltpu.VMEM((heads * parts, rows, HD), BF16),
            pltpu.VMEM((heads, parts, rows, HD), F32),
            pltpu.VMEM((heads, parts, rows, HD), F32),
            pltpu.VMEM((heads * parts, HD, rows), F32),
        ],
        cost_estimate=pl.CostEstimate(
            flops=2 * full * width * 3 * span + 10 * full * full * span,
            bytes_accessed=2 * (3 * full * width + width * 3 * span + 9 * full * span),
            transcendentals=heads * full * full,
        ),
        compiler_params=pltpu.CompilerParams(vmem_limit_bytes=60 << 20),
        name="attend_backward",
    )(jnp.stack([place, live]), *xs, *grads, w, *saved, lse)
    return outs[0], outs[1 : 1 + parts], outs[1 + parts], outs[2 + parts]


def live_only(values, first, live):
    rows = first + lax.broadcasted_iota(jnp.int32, values.shape, 0)
    return jnp.where(rows < live, values, jnp.zeros_like(values))


def folded(values):
    return functools.reduce(
        jnp.add, [values[r : r + 8] for r in range(0, values.shape[0], 8)]
    )


def token_kernel(plan, seqs, parts, info, *refs):
    refs = list(refs)
    take = lambda count: [refs.pop(0) for _ in range(count)]
    sources = take(max(p[0] for p in plan) + 1)
    pieces = take(seqs * parts)
    x, cot, dvec, mgain, mshift, fvec = take(6)
    block_out, resid_grad, fnorm, branch, og, anorm = take(6)
    hid, pg = take(2)
    mds = take(seqs * parts)
    dsum, msum, fsum = take(3)
    wo, w1, w2, ob, munit, mscale, res, runit, rscale = take(9)
    pre, cdf, act, hg, fscale, ngs, dacc, macc, facc, sems = take(10)
    step = pl.program_id(0)
    me, core = info[seqs], info[seqs + 1]
    live = info[step] - me * x.shape[0]
    rows, width = x.shape
    span, units = width // parts, pre.shape[1]
    tile, wide = 16, 384
    quarters = units // width

    def place(quarter):
        turned = quarter + quarters // 2 * core
        return jnp.where(turned >= quarters, turned - quarters, turned)

    targets = {"out": wo, "fc1": w1, "fc2": w2}

    @pl.when(step == 0)
    def _():
        copies = []
        for index, (src, k, start, count, name, at, at_step, col, col_step) in enumerate(plan):
            source = sources[src] if k is None else sources[src].at[k]
            target = targets[name]
            turn = core if src == 0 else 1 - core
            if at_step:
                at = pl.multiple_of(at + at_step * turn, 16)
            if col_step:
                col = pl.multiple_of(col + col_step * turn, 128)
            target = target.at[pl.ds(at, count), pl.ds(col, source.shape[1])]
            copies.append(
                pltpu.make_async_copy(source.at[pl.ds(start, count)], target, sems.at[index])
            )
        for copy in copies:
            copy.start()
        dacc[...] = jnp.zeros_like(dacc)
        macc[...] = jnp.zeros_like(macc)
        facc[...] = jnp.zeros_like(facc)
        for copy in copies:
            copy.wait()

    for i in range(seqs):

        @pl.when(step == i)
        def _(i=i):
            for j in range(parts):
                ob[j] = pieces[i * parts + j][...]

    def tiles(size):
        def decorate(body):
            def run(t, carry):
                body(pl.ds(pl.multiple_of(t * size, size), size), t * size)
                return carry

            lax.fori_loop(0, rows // size, run, 0)

        return decorate

    @tiles(32)
    def _(at, first):
        blocks = [ob[j, at, :].astype(F32) for j in range(parts)]
        mean = sum(jnp.sum(b, axis=1, keepdims=True) for b in blocks) / width
        blocks = [b - mean for b in blocks]
        var = sum(jnp.sum(b * b, axis=1, keepdims=True) for b in blocks) / width
        scale = lax.rsqrt(var + eps)
        mscale[at, :] = jnp.broadcast_to(scale, (32, 128))
        for j in range(parts):
            g = me ^ j
            unit = blocks[j] * scale
            munit[j, at, :] = unit
            anorm[g, at, :] = (unit * mgain[g] + mshift[g]).astype(BF16)

    mixed = sum(mm(anorm[g], wo[g * span : (g + 1) * span, :]) for g in range(parts))
    res[...] = x[...].astype(F32) + mixed + dvec[2:3, :]

    @tiles(32)
    def _(at, first):
        unit, scale = centred(res[at, :])
        runit[at, :] = unit
        rscale[at, :] = jnp.broadcast_to(scale, (32, 128))
        fnorm[at, :] = (unit * dvec[0:1, :] + dvec[1:2, :]).astype(BF16)

    for c in range(units // width):
        cols = slice(c * width, (c + 1) * width)
        pre[:, cols] = mm(fnorm[...], w1[:, cols])
    chunks = [slice(c, c + wide) for c in range(0, units, wide)]

    @tiles(tile)
    def _(at, first):
        total, square = 0.0, 0.0
        for c in chunks:
            v = pre[at, c] + fvec[1:2, c]
            below = 0.5 * (1.0 + lax.erf(v * 0.7071067811865476))
            a = v * below
            pre[at, c] = v
            cdf[at, c] = below
            act[at, c] = a
            total = total + a
        mean = jnp.sum(total, axis=1, keepdims=True) / units
        for c in chunks:
            d = act[at, c] - mean
            act[at, c] = d
            square = square + d * d
        scale = lax.rsqrt(jnp.sum(square, axis=1, keepdims=True) / units + eps)
        fscale[at, :] = jnp.broadcast_to(scale, (tile, 128))
        for c in chunks:
            unit = act[at, c] * scale
            act[at, c] = unit
            value = (unit * fvec[0:1, c] + fvec[2:3, c]).astype(BF16)
            hid[at, c] = value

    out = res[...] + mm(hid[...], w2[...]) + dvec[3:4, :]
    block_out[...] = live_only(out, 0, live).astype(BF16)
    kept = live_only(cot[...].astype(F32), 0, live)
    og[...] = kept.astype(BF16)
    dacc[24:32, :] += folded(kept)
    for c in range(units // width):
        cols = slice(c * width, (c + 1) * width)
        hg[:, cols] = mm_nt(og[...], w2[cols, :])

    @tiles(tile)
    def _(at, first):
        one, two = 0.0, 0.0
        for c in chunks:
            unit, grad = act[at, c], hg[at, c]
            both = grad * unit
            facc[0:8, c] += folded(both)
            facc[16:24, c] += folded(grad)
            gain = fvec[0:1, c]
            hg[at, c] = grad * gain
            one = one + grad * gain
            two = two + both * gain
        one = jnp.sum(one, axis=1, keepdims=True) / units
        two = jnp.sum(two, axis=1, keepdims=True) / units
        scale = fscale[at, 0:1]
        for c in chunks:
            v = pre[at, c]
            slope = cdf[at, c] + v * (jnp.exp(-0.5 * v * v) * 0.3989422804014327)
            grad = scale * (hg[at, c] - one - act[at, c] * two) * slope
            low = grad.astype(BF16)
            pg[place(c.start // width), at, c.start % width : c.start % width + wide] = low
            facc[8:16, c] += folded(low.astype(F32))

    fg = hg.at[:, 0:width]
    fg[...] = sum(
        mm_nt(pg[place(c)], w1[:, c * width : (c + 1) * width]) for c in range(units // width)
    )

    @tiles(32)
    def _(at, first):
        grad, unit = fg[at, :], runit[at, :]
        dacc[0:8, :] += folded(grad * unit)
        dacc[8:16, :] += folded(grad)
        total = og[at, :].astype(F32) + norm_back(grad * dvec[0:1, :], unit, rscale[at, 0:1])
        resid_grad[at, :] = total
        branch[at, :] = total.astype(BF16)
        dacc[16:24, :] += folded(total)

    for g in range(parts):
        ngs[g] = mm_nt(branch[...], wo[g * span : (g + 1) * span, :])

    @tiles(32)
    def _(at, first):
        one, two, scaled = 0.0, 0.0, []
        for j in range(parts):
            g = me ^ j
            grad, unit = ngs[g, at, :], munit[j, at, :]
            macc[g, 0:8, :] += folded(grad * unit)
            macc[g, 8:16, :] += folded(grad)
            m = grad * mgain[g]
            one = one + jnp.sum(m, axis=1, keepdims=True)
            two = two + jnp.sum(m * unit, axis=1, keepdims=True)
            scaled.append(m)
        one, two, scale = one / width, two / width, mscale[at, 0:1]
        for j in range(parts):
            value = scale * (scaled[j] - one - munit[j, at, :] * two)
            ob[j, at, :] = value.astype(BF16)

    for i in range(seqs):

        @pl.when(step == i)
        def _(i=i):
            for j in range(parts):
                mds[i * parts + j][...] = ob[j]

    @pl.when(step == seqs - 1)
    def _():
        for r in range(4):
            dsum[r : r + 1, :] = jnp.sum(dacc[8 * r : 8 * r + 8, :], axis=0, keepdims=True)
        for r in range(3):
            fsum[r : r + 1, :] = jnp.sum(facc[8 * r : 8 * r + 8, :], axis=0, keepdims=True)
        for g in range(parts):
            for r in range(2):
                part = macc[g, 8 * r : 8 * r + 8, :]
                msum[g, r : r + 1, :] = jnp.sum(part, axis=0, keepdims=True)


def token_stage(info, plan, sources, pieces, x, cot, dvec, mgain, mshift, fvec):
    seqs, rows, width = x.shape
    parts, units = len(pieces[0]), fvec.shape[1]
    span = width // parts
    shape = jax.ShapeDtypeStruct
    full = lambda *dims: pl.BlockSpec(dims, lambda i: (0,) * len(dims))
    by_seq = pl.BlockSpec((None, rows, width), lambda i: (i, 0, 0))
    by_rows = lambda cols: pl.BlockSpec((rows, cols), lambda i: (i, 0))
    n = seqs * rows
    outs = pl.pallas_call(
        functools.partial(token_kernel, plan, seqs, parts),
        grid=(seqs,),
        in_specs=[pl.BlockSpec(memory_space=pltpu.SMEM)]
        + [pl.BlockSpec(memory_space=pl.ANY)] * len(sources)
        + [full(rows, span)] * (seqs * parts)
        + [
            by_seq,
            by_seq,
            full(*dvec.shape),
            full(*mgain.shape),
            full(*mshift.shape),
            full(*fvec.shape),
        ],
        out_specs=[by_seq, by_seq]
        + [by_rows(width)] * 3
        + [pl.BlockSpec((parts, rows, span), lambda i: (0, i, 0))]
        + [by_rows(units)]
        + [pl.BlockSpec((units // width, rows, width), lambda i: (0, i, 0))]
        + [full(rows, span)] * (seqs * parts)
        + [full(4, width), full(parts, 2, span), full(3, units)],
        out_shape=[shape((seqs, rows, width), BF16), shape((seqs, rows, width), F32)]
        + [shape((n, width), BF16)] * 3
        + [shape((parts, n, span), BF16)]
        + [shape((n, units), BF16), shape((units // width, n, width), BF16)]
        + [shape((rows, span), BF16)] * (seqs * parts)
        + [shape((4, width), F32), shape((parts, 2, span), F32), shape((3, units), F32)],
        scratch_shapes=[
            pltpu.VMEM((width, width), BF16),
            pltpu.VMEM((width, units), BF16),
            pltpu.VMEM((units, width), BF16),
            pltpu.VMEM((parts, rows, span), BF16),
            pltpu.VMEM((parts, rows, span), F32),
            pltpu.VMEM((rows, 128), F32),
            pltpu.VMEM((rows, width), F32),
            pltpu.VMEM((rows, width), F32),
            pltpu.VMEM((rows, 128), F32),
        ]
        + [pltpu.VMEM((rows, units), F32)] * 4
        + [
            pltpu.VMEM((rows, 128), F32),
            pltpu.VMEM((parts, rows, span), F32),
            pltpu.VMEM((32, width), F32),
            pltpu.VMEM((parts, 16, span), F32),
            pltpu.VMEM((24, units), F32),
            pltpu.SemaphoreType.DMA((len(plan),)),
        ],
        cost_estimate=pl.CostEstimate(
            flops=2 * n * width * (4 * units + 2 * width),
            bytes_accessed=2 * width * (2 * units + width) + 2 * n * (4 * units + 12 * width),
            transcendentals=2 * n * units,
        ),
        compiler_params=pltpu.CompilerParams(vmem_limit_bytes=60 << 20),
        name="token_stage",
    )(info, *sources, *[p for group in pieces for p in group], x, cot, dvec, mgain, mshift, fvec)
    outs = list(outs)
    mds = outs[8 : 8 + seqs * parts]
    mds = [mds[i * parts : (i + 1) * parts] for i in range(seqs)]
    return outs[:6], outs[6], outs[7], mds, outs[8 + seqs * parts :]


def swap(values, axis, mask):
    count = lax.axis_size(axis)
    return lax.ppermute(values, axis, [(i, i ^ mask) for i in range(count)])


def pick(values, index, axis):
    return lax.dynamic_index_in_dim(values, index, axis, keepdims=False)


def after(values, others):
    return lax.optimization_barrier((values, others))[0]


def spread_blocks(block, axis):
    count, me = lax.axis_size(axis), lax.axis_index(axis)
    held = {0: block}
    bit = count // 2
    while bit:
        held |= {mask | bit: swap(part, axis, bit) for mask, part in held.items()}
        bit //= 2
    whole = jnp.zeros((count,) + block.shape, block.dtype)
    for mask, part in held.items():
        whole = lax.dynamic_update_index_in_dim(whole, part, me ^ mask, 0)
    return whole


def sum_blocks(blocks, axis, kind):
    blocks = lax.all_to_all(blocks.astype(kind), axis, split_axis=0, concat_axis=0, tiled=True)
    return jnp.sum(blocks.astype(F32), axis=0)


def shards(
    activations,
    cotangent,
    lengths,
    w_qkv,
    w_out,
    w_fc1,
    w_fc2,
    d_gains,
    d_biases,
    ff_gain,
    ff_biases,
):
    seqs, rows, width = activations.shape
    parts, owners = lax.axis_size("seq"), lax.axis_size("fsdp")
    s = lax.axis_index("seq")
    core = s % 2
    span = width // parts
    own_rows = w_qkv.shape[0]
    own_ff = w_fc2.shape[0]
    half_ff, half_rows = own_ff // 2, own_rows // 2
    ff_half = half_ff * owners
    quarter = own_ff // own_rows

    own_w = pick(w_qkv.reshape(own_rows, 3, parts, span), s, 2).reshape(own_rows, 3 * span)
    ff_small = jnp.concatenate([ff_gain[:, None], ff_biases], axis=1).T.reshape(
        3 * quarter, own_rows
    )
    small = jnp.concatenate([d_gains.T, d_biases.T, ff_small], axis=0)
    kinds = small.shape[0]
    small_rows = 32
    small = jnp.pad(small, ((0, small_rows - kinds), (0, 3 * span - own_rows)))
    block = jnp.concatenate([own_w, small], axis=0)
    first = spread_blocks(block, "fsdp")
    my_qkv = first[:, :own_rows].reshape(width, 3 * span)
    small = first[:, own_rows : own_rows + kinds, :own_rows].astype(F32)
    d_small = small[:, :10].transpose(1, 0, 2).reshape(10, width)
    gains, biases = d_small[:3], d_small[3:]
    ff_small = small[:, 10:].reshape(owners, 3, own_ff).transpose(1, 0, 2).reshape(3, 2 * ff_half)

    w_out, w_fc1, w_fc2 = after((w_out, w_fc1, w_fc2), block)
    fc1_half = lax.dynamic_slice(w_fc1, (0, core * ff_half), (own_rows, ff_half))
    columns = range(0, ff_half, width)
    rest = jnp.concatenate(
        [pick(w_out.reshape(2, half_rows, width), core, 0)]
        + [fc1_half[:, c : c + width] for c in columns]
        + [pick(w_fc2.reshape(2, half_ff, width), core, 0)],
        axis=0,
    )
    rest_rows = rest.shape[0]
    rest = lax.all_gather(rest, "fsdp", axis=0, tiled=False)

    qkv_bias = pick(
        jnp.stack([biases[1], jnp.zeros_like(biases[1]), biases[2]]).reshape(3, parts, span), s, 1
    ).reshape(1, 3 * span)
    x_parts, mixed_parts, kept = [], [], []
    for i in range(seqs):
        mine = activations[i]
        across = swap(mine, "seq", 2)
        x_parts.append([mine, swap(mine, "seq", 1), across, swap(across, "seq", 1)])
    for i in range(seqs):
        if i > 0:
            x_parts[i] = after(x_parts[i], [kept[i - 1][2], mixed_parts[:-1]])
        normed, saved, outs, lse = attend_forward(
            s, lengths[i], x_parts[i], my_qkv, gains[0:1], biases[0:1], qkv_bias
        )
        kept.append((normed, saved, lse))
        mixed_parts.append([outs[0]] + [swap(outs[j], "seq", j) for j in range(1, parts)])
    rest = after(rest, [lse for _, _, lse in kept])
    rest_other = swap(rest, "seq", 1)

    plan, sources = [], [rest, rest_other]
    if half_rows % 16 == 0 and half_ff % 16 == 0:
        for src in range(2):
            for k in range(owners):
                plan.append((src, k, 0, half_rows, "out", k * own_rows, half_rows, 0, 0))
                for at, c in enumerate(columns):
                    start = half_rows + at * own_rows
                    plan.append((src, k, start, own_rows, "fc1", k * own_rows, 0, c, ff_half))
                start = rest_rows - half_ff
                plan.append((src, k, start, half_ff, "fc2", k * own_ff, half_ff, 0, 0))
    else:
        pair = [jnp.where(core == 0, rest, rest_other), jnp.where(core == 0, rest_other, rest)]
        blocks = [
            buf[:, half_rows + at * own_rows : half_rows + (at + 1) * own_rows].reshape(width, width)
            for buf in pair
            for at in range(len(columns))
        ]
        sources = [
            jnp.concatenate([buf[:, :half_rows] for buf in pair], axis=1).reshape(width, width),
            jnp.concatenate(blocks, axis=1),
            jnp.concatenate([buf[:, rest_rows - half_ff :] for buf in pair], axis=1).reshape(
                2 * ff_half, width
            ),
        ]
        names = ("out", "fc1", "fc2")
        plan = [(i, None, 0, sources[i].shape[0], names[i], 0, 0, 0, 0) for i in range(3)]
    info = jnp.concatenate([lengths, jnp.stack([s, core]).astype(jnp.int32)])
    dvec = jnp.stack([gains[2], biases[5], biases[4], biases[6]])
    tokens = token_stage(
        info,
        plan,
        sources,
        mixed_parts,
        activations,
        cotangent,
        dvec,
        gains[1].reshape(parts, 1, span),
        biases[3].reshape(parts, 1, span),
        ff_small,
    )
    (block_out, resid_grad, fnorm, branch, og, anorm), hid, pg, mixed_grads, sums = tokens
    dsum, msum, fsum = sums

    grad_out = jnp.einsum("gnk,nd->gkd", anorm, branch, preferred_element_type=F32)
    grad_out = grad_out.reshape(owners, 2, half_rows, width)
    grad_fc2 = mm_tn(hid, og).reshape(owners, 2, half_ff, width)
    mixed_grads = [[g[0]] + [swap(g[j], "seq", j) for j in range(1, parts)] for g in mixed_grads]
    grads = []
    for src in (1, 0):
        turn = core if src == 0 else 1 - core
        pieces = [pick(grad_out, turn, 1)]
        pieces += [
            mm_tn(fnorm, pg[len(columns) * src + at]).reshape(owners, own_rows, width)
            for at in range(len(columns))
        ]
        pieces.append(pick(grad_fc2, turn, 1))
        grads.append(jnp.concatenate([p.astype(BF16) for p in pieces], axis=1))
    rest_sum = grads[1].astype(F32) + swap(grads[0], "seq", 1).astype(F32)
    rest_sum = rest_sum.astype(BF16).reshape(owners * rest_rows, width)
    mixed_grads[0], rest_sum = lax.optimization_barrier((mixed_grads[0], rest_sum))
    rest_sum = lax.psum_scatter(rest_sum, "fsdp", scatter_dimension=0, tiled=True)

    grad_own, summed, head_sums, unit_sums, near = 0.0, [], 0.0, 0.0, []
    for i in range(seqs):
        pieces = mixed_grads[i]
        if i > 0:
            pieces = after(pieces, [sums, near[:-1]])
        normed, saved, lse = kept[i]
        dqkv, dns, sums, cols = attend_backward(
            s, lengths[i], x_parts[i], pieces, my_qkv, saved, lse
        )
        grad_own = grad_own + mm_tn(
            normed.reshape(parts * rows, width), dqkv.reshape(parts * rows, 3 * span)
        )
        unit_sums, head_sums = unit_sums + sums, head_sums + cols
        near.append([swap(dns[j], "seq", 1) for j in (1, 3)])
        far = (dns[2].astype(F32) + near[i][1].astype(F32)).astype(BF16)
        far = swap(far, "seq", 2).astype(F32)
        summed.append(dns[0].astype(F32) + near[i][0].astype(F32) + far)
    first_grad = jnp.stack(summed)
    first_unit, first_scale = centred(activations.astype(F32))
    input_grad = resid_grad + norm_back(first_grad * gains[0], first_unit, first_scale)

    def head_columns(values):
        blank = jnp.zeros((parts, span), F32)
        return lax.dynamic_update_slice(blank, values[None], (s, 0)).reshape(width)

    small_grads = jnp.stack(
        [
            unit_sums[0],
            msum[:, 0].reshape(width),
            dsum[0],
            unit_sums[1],
            head_columns(head_sums[0, :span]),
            head_columns(head_sums[0, 2 * span :]),
            msum[:, 1].reshape(width),
            dsum[2],
            dsum[1],
            dsum[3],
        ]
    )
    feed_grads = fsum.reshape(3, owners, quarter, own_rows)
    small_blocks = jnp.concatenate(
        [
            small_grads.reshape(10, owners, own_rows).transpose(1, 0, 2),
            feed_grads.transpose(1, 0, 2, 3).reshape(owners, 3 * quarter, own_rows),
        ],
        axis=1,
    )
    small_blocks = jnp.pad(small_blocks, ((0, 0), (0, small_rows - kinds), (0, 0)))
    small_sum = sum_blocks(small_blocks, "fsdp", F32)
    own_sum = sum_blocks(grad_own.reshape(owners, own_rows, 3 * span), "fsdp", BF16).astype(BF16)
    rest_sum = after(rest_sum, own_sum)
    rest_sum = rest_sum.astype(F32) + swap(rest_sum, "seq", 2).astype(F32)
    small_sum = [small_sum] + [swap(small_sum, "seq", j) for j in range(1, parts)]
    small_sum = (small_sum[0] + small_sum[1]) + (small_sum[2] + small_sum[3])
    feed_sum = small_sum[10:kinds].reshape(3, own_ff)
    group = jnp.stack([own_sum] + [swap(own_sum, "seq", j) for j in range(1, parts)])
    w_qkv_grad = jnp.concatenate(
        [
            pick(group, s ^ g, 0)[:, p * span : (p + 1) * span]
            for p in range(3)
            for g in range(parts)
        ],
        axis=1,
    ).astype(F32)

    other_sum = swap(rest_sum, "seq", 1)
    pair = [
        jnp.where(core == 0, rest_sum, other_sum),
        jnp.where(core == 0, other_sum, rest_sum),
    ]
    w_out_grad = jnp.concatenate([p[:half_rows] for p in pair], axis=0)
    w_fc1_grad = jnp.concatenate(
        [
            p[half_rows + at * own_rows : half_rows + (at + 1) * own_rows]
            for p in pair
            for at in range(len(columns))
        ],
        axis=1,
    )
    w_fc2_grad = jnp.concatenate([p[rest_rows - half_ff :] for p in pair], axis=0)
    return (
        block_out,
        input_grad,
        w_qkv_grad,
        w_out_grad,
        w_fc1_grad,
        w_fc2_grad,
        small_sum[:3].T,
        small_sum[3:10].T,
        feed_sum[0],
        feed_sum[1:].T,
    )


def solution(mesh):
    return jax.shard_map(
        shards,
        mesh=mesh,
        in_specs=(
            P("fsdp", "seq", None),
            P("fsdp", "seq", None),
            P("fsdp"),
            P("fsdp", None),
            P("fsdp", None),
            P("fsdp", None),
            P("fsdp", None),
            P("fsdp", None),
            P("fsdp", None),
            P("fsdp"),
            P("fsdp", None),
        ),
        out_specs=(
            P("fsdp", "seq", None),
            P("fsdp", "seq", None),
            P("fsdp", None),
            P("fsdp", None),
            P("fsdp", None),
            P("fsdp", None),
            P("fsdp", None),
            P("fsdp", None),
            P("fsdp"),
            P("fsdp", None),
        ),
        check_vma=False,
    )
```

profile of v0, /device:TPU:0, one launch (start us, length us, event | category | flops | bytes accessed | tf_op | source)
XLA Modules:
  0.0 386.9 jit_solution(13501410724280352417)
XLA Ops:
  7.3 1.7 reshape.146
  11.1 4.1 %collective-permute-start.3 = (bf16[128,576]{0,1:T(8,128)(2,1)S(1)}, bf16[128,576]{0,1:T(8,128)(2,1)S(1)}, u32[]{:S(2)}, u32[]{:S(2)}) collective-permute-start(bf16[128,576]{0,1:T(8,128)(2,1)S(1)} %fusion.26), channel_id=1, source_target_pairs={{0,4},{1,5},{2,6},{3,7},{4,0},{5,1},{6,2},{7,3},{8,12},{9,13},{10,... | collective-permute-start | bytes 442376 | tf_op jit(solution)/shard_map/ppermute | solution.py:555
  15.2 1.6 collective-permute-start.4
  16.8 1.5 collective-permute-start.6
  18.4 1.6 collective-permute-start.1
  21.0 2.0 pad_add_fusion.2
  23.0 1.2 pad_add_fusion.1.info
  26.7 13.1 %collective-permute-done.5 = bf16[128,576]{0,1:T(8,128)(2,1)} collective-permute-done((bf16[128,576]{0,1:T(8,128)(2,1)S(1)}, bf16[128,576]{0,1:T(8,128)(2,1)}, u32[]{:S(2)}, u32[]{:S(2)}) %collective-permute-start.5) | collective-permute-done | bytes 147488 | tf_op jit(solution)/shard_map/ppermute | solution.py:555
  41.2 2.1 collective-permute-start.9
  43.3 3.3 collective-permute-done.8
  47.5 1.4 collective-permute-done.9
  50.0 8.4 %collective-permute-done.14.refs_2_ = bf16[256,768]{1,0:T(8,128)(2,1)S(1)} collective-permute-done((bf16[256,768]{1,0:T(8,128)(2,1)S(1)}, bf16[256,768]{1,0:T(8,128)(2,1)S(1)}, u32[]{:S(2)}, u32[]{:S(2)}) %collective-permute-start.14) | collective-permute-done | bytes 393248 | tf_op jit(solution)/shard_map/ppermute | solution.py:555
  61.6 15.6 %attend_forward.3 = (bf16[4,256,768]{2,1,0:T(8,128)(2,1)}, bf16[3,1024,64]{2,1,0:T(8,128)(2,1)}, bf16[3,1024,64]{2,1,0:T(8,128)(2,1)}, bf16[3,1024,64]{2,1,0:T(8...) custom-call(s32[2]{0:T(128)} %pad_add_fusion.1.info, ...), custom_call_target="tpu_custom_call" | custom-call | flops 1711276032 | bytes 6389760 | tf_op jit(solution)/shard_map/attend_forward/pallas_call | solution.py:134
  78.1 1.2 collective-permute-start.18
  79.2 15.5 %attend_forward.4 = (bf16[4,256,768]{2,1,0:T(8,128)(2,1)}, bf16[3,1024,64]{2,1,0:T(8,128)(2,1)}, bf16[3,1024,64]{2,1,0:T(8,128)(2,1)}, bf16[3,1024,64]{2,1,0:T(8...) custom-call(s32[2]{0:T(128)} %get-tuple-element.267.info, ...), custom_call_target="tpu_custom_call" | custom-call | flops 1711276032 | bytes 6389760 | tf_op jit(solution)/shard_map/attend_forward/pallas_call | solution.py:134
  95.5 9.2 %attend_forward.5 = (bf16[4,256,768]{2,1,0:T(8,128)(2,1)}, bf16[3,1024,64]{2,1,0:T(8,128)(2,1)}, bf16[3,1024,64]{2,1,0:T(8,128)(2,1)}, bf16[3,1024,64]{2,1,0:T(8...) custom-call(s32[2]{0:T(128)} %get-tuple-element.268.info, ...), custom_call_target="tpu_custom_call" | custom-call | flops 1711276032 | bytes 6389760 | tf_op jit(solution)/shard_map/attend_forward/pallas_call | solution.py:134
  109.0 1.4 collective-permute-start.22
  110.8 3.6 collective-permute-done.20.refs_7_
  114.7 1.4 collective-permute-start.25
  116.7 4.2 %collective-permute-done.24.refs_12_ = bf16[256,192]{1,0:T(8,128)(2,1)S(1)} collective-permute-done((bf16[256,192]{1,0:T(8,128)(2,1)}, bf16[256,192]{1,0:T(8,128)(2,1)S(1)}, u32[]{:S(2)}, u32[]{:S(2)}) %collective-permute-start.24) | collective-permute-done | bytes 98336 | tf_op jit(solution)/shard_map/ppermute | solution.py:555
  120.9 1.6 collective-permute-done.25.refs_13_
  123.2 69.7 %token_stage.1 = (bf16[3,256,768]{2,1,0:T(8,128)(2,1)}, f32[3,256,768]{2,1,0:T(8,128)}, bf16[768,768]{1,0:T(8,128)(2,1)}, bf16[768,768]{1,0:T(8,128)(2,1)}, bf16...) custom-call(s32[5]{0:T(128)} %pad_add_fusion.info, ...), custom_call_target="tpu_custom_call" | custom-call | flops 16307453952 | bytes 43646976 | tf_op jit(solution)/shard_map/token_stage/pallas_call | solution.py:492
  192.9 1.6 copy.90
  194.5 2.5 convolution_convert_fusion.1
  201.4 4.4 %fusion.37 = bf16[3072,768]{1,0:T(8,128)(2,1)S(1)} fusion(bf16[768,3072]{1,0:T(8,128)(2,1)S(1)} %bitcast.164, bf16[768,768]{1,0:T(8,128)(2,1)S(1)} %copy-done.72), kind=kOutput, calls=%fused_computation.136 | convolution fusion | flops 3623878656 | bytes 10616832 | tf_op jit(solution)/shard_map/dot_general | solution.py:27
  211.3 4.3 %collective-permute-done.29 = bf16[8,432,768]{2,1,0:T(8,128)(2,1)S(1)} collective-permute-done((bf16[8,432,768]{2,1,0:T(8,128)(2,1)S(1)}, bf16[8,432,768]{2,1,0:T(8,128)(2,1)S(1)}, u32[]{:S(2)}, u32[]{:S(2)}) %collective-permute-start.29) | collective-permute-done | bytes 5308448 | tf_op jit(solution)/shard_map/ppermute | solution.py:555
  215.6 3.6 add_convert_fusion
  224.9 21.1 %attend_backward.3 = (bf16[4,256,576]{2,1,0:T(8,128)(2,1)}, bf16[256,768]{1,0:T(8,128)(2,1)}, bf16[256,768]{1,0:T(8,128)(2,1)}, bf16[256,768]{1,0:T(8,128)(2,1)}...) custom-call(s32[2]{0:T(128)} %pad_add_fusion.1.info, bf16[256,768]{1,0:T(8,128)(2,1)} %copy-done.12, ...), custom_call_target="tpu_custom_call" | custom-call | flops 2919235584 | bytes 9142272 | tf_op jit(solution)/shard_map/attend_backward/pallas_call | solution.py:244
  248.1 21.1 %attend_backward.4 = (bf16[4,256,576]{2,1,0:T(8,128)(2,1)}, bf16[256,768]{1,0:T(8,128)(2,1)}, bf16[256,768]{1,0:T(8,128)(2,1)}, bf16[256,768]{1,0:T(8,128)(2,1)}...) custom-call(s32[2]{0:T(128)} %get-tuple-element.267.info, bf16[256,768]{1,0:T(8,128)(2,1)} %copy-done.11, ...), custom_call_target="tpu_custom_call" | custom-call | flops 2919235584 | bytes 9142272 | tf_op jit(solution)/shard_map/attend_backward/pallas_call | solution.py:244
  269.2 4.2 %fusion.38 = f32[768,576,1]{0,1,2:T(8,128)} fusion(bf16[4,256,768]{2,1,0:T(8,128)(2,1)} %get-tuple-element.197, bf16[4,256,576]{2,1,0:T(8,128)(2,1)} %get-tuple-element.198), kind=kOutput, calls=%fused_computation.137 | convolution fusion | flops 905969664 | bytes 4521984 | tf_op jit(solution)/shard_map/dot_general | solution.py:27
  274.6 11.4 %attend_backward.5 = (bf16[4,256,576]{2,1,0:T(8,128)(2,1)}, bf16[256,768]{1,0:T(8,128)(2,1)}, bf16[256,768]{1,0:T(8,128)(2,1)}, bf16[256,768]{1,0:T(8,128)(2,1)}...) custom-call(s32[2]{0:T(128)} %get-tuple-element.268.info, bf16[256,768]{1,0:T(8,128)(2,1)} %copy-done.10, ...), custom_call_target="tpu_custom_call" | custom-call | flops 2919235584 | bytes 9142272 | tf_op jit(solution)/shard_map/attend_backward/pallas_call | solution.py:244
  288.7 17.9 %all-to-all-start.1 = ((f32[8,32,96]{2,1,0:T(8,128)}), f32[8,32,96]{2,1,0:T(8,128)S(1)}, u32[]{:S(2)}, u32[]{:S(2)}) async-start(f32[8,32,96]{2,1,0:T(8,128)} %pad.9.clone), calls=%async_computation.2 | async-start | bytes 262144 | tf_op jit(solution)/shard_map/all_to_all | solution.py:580
  306.6 3.1 fusion.39
  309.8 1.3 fusion.11
  311.1 1.3 copy.95
  314.1 3.2 all-to-all-done.1
  317.4 4.4 %all-to-all-start = ((bf16[8,96,576]{2,1,0:T(8,128)(2,1)}), bf16[8,96,576]{2,1,0:T(8,128)(2,1)}, u32[]{:S(2)}, u32[]{:S(2)}) async-start(bf16[8,96,576]{2,1,0:T(8,128)(2,1)} %bitcast.50), calls=%async_computation | async-start | bytes 1966080 | tf_op jit(solution)/shard_map/all_to_all | solution.py:580
  330.4 1.3 add_bitcast_fusion.2
  331.7 4.3 %collective-permute-done.38 = bf16[256,768]{1,0:T(8,128)(2,1)} collective-permute-done((bf16[256,768]{1,0:T(8,128)(2,1)S(1)}, bf16[256,768]{1,0:T(8,128)(2,1)}, u32[]{:S(2)}, u32[]{:S(2)}) %collective-permute-start.38) | collective-permute-done | bytes 393248 | tf_op jit(solution)/shard_map/ppermute | solution.py:555
  336.0 1.2 add_bitcast_fusion.1
  337.3 6.5 %collective-permute-done.44 = bf16[256,768]{1,0:T(8,128)(2,1)S(1)} collective-permute-done((bf16[256,768]{1,0:T(8,128)(2,1)S(1)}, bf16[256,768]{1,0:T(8,128)(2,1)S(1)}, u32[]{:S(2)}, u32[]{:S(2)}) %collective-permute-start.44) | collective-permute-done | bytes 393248 | tf_op jit(solution)/shard_map/ppermute | solution.py:555
  344.8 4.9 %all-to-all-done = bf16[8,96,576]{2,1,0:T(8,128)(2,1)} async-done(((bf16[8,96,576]{2,1,0:T(8,128)(2,1)}), bf16[8,96,576]{2,1,0:T(8,128)(2,1)}, u32[]{:S(2)}, u32[]{:S(2)}) %all-to-all-start) | async-done | bytes 884768 | tf_op jit(solution)/shard_map/all_to_all | solution.py:580
  349.7 2.0 reduce_sum.61
  351.7 1.4 collective-permute-start.48
  355.9 13.8 %collective-permute-done.48 = bf16[432,768]{1,0:T(8,128)(2,1)S(1)} collective-permute-done((bf16[432,768]{1,0:T(8,128)(2,1)}, bf16[432,768]{1,0:T(8,128)(2,1)S(1)}, u32[]{:S(2)}, u32[]{:S(2)}) %collective-permute-start.48) | collective-permute-done | bytes 663584 | tf_op jit(solution)/shard_map/ppermute | solution.py:555
  369.7 1.3 convert_add_fusion
  371.0 1.9 fusion.7
  374.8 1.6 broadcast_select_fusion.1
  (375 shorter events, 60.1 us)
Async XLA Ops:
  7.2 97.6 %all-gather.3.cloned.1.call-start = ((), (), s32[]{:S(2)}) async-start(), calls=%async_computation.4 | async-start | bytes 5971968 | tf_op jit(solution)/shard_map/all_gather | solution.py:634
  11.1 340.7 %reduce-scatter.2.cloned.1.call-start = ((), (), s32[]{:S(2)}) async-start(), calls=%async_computation.3 | async-start | bytes 5971968 | tf_op jit(solution)/shard_map/reduce_scatter | solution.py:715
  11.1 13.2 %collective-permute-start.3 = (bf16[128,576]{0,1:T(8,128)(2,1)S(1)}, bf16[128,576]{0,1:T(8,128)(2,1)S(1)}, u32[]{:S(2)}, u32[]{:S(2)}) collective-permute-start(bf16[128,576]{0,1:T(8,128)(2,1)S(1)} %fusion.26), channel_id=1, source_target_pairs={{0,4},{1,5},{2,6},{3,7},{4,0},{5,1},{6,2},{7,3},{8,12},{9,13},{10,... | collective-permute-start | bytes 442376 | tf_op jit(solution)/shard_map/ppermute | solution.py:555
  15.2 9.7 %collective-permute-start.4 = (bf16[128,576]{0,1:T(8,128)(2,1)S(1)}, bf16[128,576]{0,1:T(8,128)(2,1)S(1)}, u32[]{:S(2)}, u32[]{:S(2)}) collective-permute-start(bf16[128,576]{0,1:T(8,128)(2,1)S(1)} %fusion.26), channel_id=1, source_target_pairs={{0,2},{1,3},{2,0},{3,1},{4,6},{5,7},{6,4},{7,5},{8,10},{9,11},{10,... | collective-permute-start | bytes 442376 | tf_op jit(solution)/shard_map/ppermute | solution.py:555
  16.8 8.9 %collective-permute-start.6 = (bf16[128,576]{0,1:T(8,128)(2,1)S(1)}, bf16[128,576]{0,1:T(8,128)(2,1)S(1)}, u32[]{:S(2)}, u32[]{:S(2)}) collective-permute-start(bf16[128,576]{0,1:T(8,128)(2,1)S(1)} %fusion.26), channel_id=1, source_target_pairs={{0,1},{1,0},{2,3},{3,2},{4,5},{5,4},{6,7},{7,6},{8,9},{9,8},{10,11... | collective-permute-start | bytes 442376 | tf_op jit(solution)/shard_map/ppermute | solution.py:555
  18.4 28.4 %collective-permute-start.1 = (bf16[256,768]{1,0:T(8,128)(2,1)S(1)}, bf16[256,768]{1,0:T(8,128)(2,1)}, u32[]{:S(2)}, u32[]{:S(2)}) collective-permute-start(bf16[256,768]{1,0:T(8,128)(2,1)S(1)} %get-tuple-element.242.refs_0_), channel_id=1, source_target_pairs={{0,16},{8,24},{16,0},{24,8},{1,17},{9,25},{17,1},{25,9},{2,18},{10... | collective-permute-start | bytes 1179656 | tf_op jit(solution)/shard_map/ppermute | solution.py:555
  20.0 29.4 %collective-permute-start = (bf16[256,768]{1,0:T(8,128)(2,1)S(1)}, bf16[256,768]{1,0:T(8,128)(2,1)}, u32[]{:S(2)}, u32[]{:S(2)}) collective-permute-start(bf16[256,768]{1,0:T(8,128)(2,1)S(1)} %get-tuple-element.242.refs_0_), channel_id=1, source_target_pairs={{0,8},{8,0},{16,24},{24,16},{1,9},{9,1},{17,25},{25,17},{2,10},{10... | collective-permute-start | bytes 1179656 | tf_op jit(solution)/shard_map/ppermute | solution.py:555
  24.4 15.4 %collective-permute-start.5 = (bf16[128,576]{0,1:T(8,128)(2,1)S(1)}, bf16[128,576]{0,1:T(8,128)(2,1)}, u32[]{:S(2)}, u32[]{:S(2)}) collective-permute-start(bf16[128,576]{0,1:T(8,128)(2,1)S(1)} %collective-permute-done.3), channel_id=1, source_target_pairs={{0,2},{1,3},{2,0},{3,1},{4,6},{5,7},{6,4},{7,5},{8,10},{9,11},{10,... | collective-permute-start | bytes 442376 | tf_op jit(solution)/shard_map/ppermute | solution.py:555
  25.0 21.9 %collective-permute-start.11 = (bf16[256,768]{1,0:T(8,128)(2,1)S(1)}, bf16[256,768]{1,0:T(8,128)(2,1)}, u32[]{:S(2)}, u32[]{:S(2)}) collective-permute-start(bf16[256,768]{1,0:T(8,128)(2,1)S(1)} %get-tuple-element.114.refs_0_), channel_id=1, source_target_pairs={{0,16},{8,24},{16,0},{24,8},{1,17},{9,25},{17,1},{25,9},{2,18},{10... | collective-permute-start | bytes 1179656 | tf_op jit(solution)/shard_map/ppermute | solution.py:555
  25.9 15.1 %collective-permute-start.7 = (bf16[128,576]{0,1:T(8,128)(2,1)S(1)}, bf16[128,576]{0,1:T(8,128)(2,1)S(1)}, u32[]{:S(2)}, u32[]{:S(2)}) collective-permute-start(bf16[128,576]{0,1:T(8,128)(2,1)S(1)} %collective-permute-done.3), channel_id=1, source_target_pairs={{0,1},{1,0},{2,3},{3,2},{4,5},{5,4},{6,7},{7,6},{8,9},{9,8},{10,11... | collective-permute-start | bytes 442376 | tf_op jit(solution)/shard_map/ppermute | solution.py:555
  41.2 7.7 %collective-permute-start.9 = (bf16[128,576]{0,1:T(8,128)(2,1)}, bf16[128,576]{0,1:T(8,128)(2,1)S(1)}, u32[]{:S(2)}, u32[]{:S(2)}) collective-permute-start(bf16[128,576]{0,1:T(8,128)(2,1)} %collective-permute-done.5), channel_id=1, source_target_pairs={{0,1},{1,0},{2,3},{3,2},{4,5},{5,4},{6,7},{7,6},{8,9},{9,8},{10,11... | collective-permute-start | bytes 442376 | tf_op jit(solution)/shard_map/ppermute | solution.py:555
  46.6 30.6 %collective-permute-start.10 = (bf16[256,768]{1,0:T(8,128)(2,1)S(1)}, bf16[256,768]{1,0:T(8,128)(2,1)}, u32[]{:S(2)}, u32[]{:S(2)}) collective-permute-start(bf16[256,768]{1,0:T(8,128)(2,1)S(1)} %get-tuple-element.114.refs_0_), channel_id=1, source_target_pairs={{0,8},{8,0},{16,24},{24,16},{1,9},{9,1},{17,25},{25,17},{2,10},{10... | collective-permute-start | bytes 1179656 | tf_op jit(solution)/shard_map/ppermute | solution.py:555
  46.8 11.6 %collective-permute-start.14 = (bf16[256,768]{1,0:T(8,128)(2,1)S(1)}, bf16[256,768]{1,0:T(8,128)(2,1)S(1)}, u32[]{:S(2)}, u32[]{:S(2)}) collective-permute-start(bf16[256,768]{1,0:T(8,128)(2,1)S(1)} %get-tuple-element.123.refs_0_), channel_id=1, source_target_pairs={{0,16},{8,24},{16,0},{24,8},{1,17},{9,25},{17,1},{25,9},{2,18},{10... | collective-permute-start | bytes 1179656 | tf_op jit(solution)/shard_map/ppermute | solution.py:555
  46.9 14.7 %collective-permute-start.2 = (bf16[256,768]{1,0:T(8,128)(2,1)}, bf16[256,768]{1,0:T(8,128)(2,1)}, u32[]{:S(2)}, u32[]{:S(2)}) collective-permute-start(bf16[256,768]{1,0:T(8,128)(2,1)} %collective-permute-done.1.refs_2_), channel_id=1, source_target_pairs={{0,8},{8,0},{16,24},{24,16},{1,9},{9,1},{17,25},{25,17},{2,10},{10... | collective-permute-start | bytes 1179656 | tf_op jit(solution)/shard_map/ppermute | solution.py:555
  48.9 28.3 %collective-permute-start.12 = (bf16[256,768]{1,0:T(8,128)(2,1)}, bf16[256,768]{1,0:T(8,128)(2,1)}, u32[]{:S(2)}, u32[]{:S(2)}) collective-permute-start(bf16[256,768]{1,0:T(8,128)(2,1)} %collective-permute-done.11.refs_2_), channel_id=1, source_target_pairs={{0,8},{8,0},{16,24},{24,16},{1,9},{9,1},{17,25},{25,17},{2,10},{10... | collective-permute-start | bytes 1179656 | tf_op jit(solution)/shard_map/ppermute | solution.py:555
  49.4 45.3 %collective-permute-start.13 = (bf16[256,768]{1,0:T(8,128)(2,1)S(1)}, bf16[256,768]{1,0:T(8,128)(2,1)S(1)}, u32[]{:S(2)}, u32[]{:S(2)}) collective-permute-start(bf16[256,768]{1,0:T(8,128)(2,1)S(1)} %get-tuple-element.123.refs_0_), channel_id=1, source_target_pairs={{0,8},{8,0},{16,24},{24,16},{1,9},{9,1},{17,25},{25,17},{2,10},{10... | collective-permute-start | bytes 1179656 | tf_op jit(solution)/shard_map/ppermute | solution.py:555
  58.4 36.3 %collective-permute-start.15 = (bf16[256,768]{1,0:T(8,128)(2,1)S(1)}, bf16[256,768]{1,0:T(8,128)(2,1)}, u32[]{:S(2)}, u32[]{:S(2)}) collective-permute-start(bf16[256,768]{1,0:T(8,128)(2,1)S(1)} %collective-permute-done.14.refs_2_), channel_id=1, source_target_pairs={{0,8},{8,0},{16,24},{24,16},{1,9},{9,1},{17,25},{25,17},{2,10},{10... | collective-permute-start | bytes 1179656 | tf_op jit(solution)/shard_map/ppermute | solution.py:555
  77.2 17.5 %collective-permute-start.16 = (bf16[256,192]{1,0:T(8,128)(2,1)}, bf16[256,192]{1,0:T(8,128)(2,1)S(1)}, u32[]{:S(2)}, u32[]{:S(2)}) collective-permute-start(bf16[256,192]{1,0:T(8,128)(2,1)} %get-tuple-element.120), channel_id=1, source_target_pairs={{0,8},{8,0},{16,24},{24,16},{1,9},{9,1},{17,25},{25,17},{2,10},{10... | collective-permute-start | bytes 294920 | tf_op jit(solution)/shard_map/ppermute | solution.py:555
  77.8 16.9 %collective-permute-start.17 = (bf16[256,192]{1,0:T(8,128)(2,1)}, bf16[256,192]{1,0:T(8,128)(2,1)S(1)}, u32[]{:S(2)}, u32[]{:S(2)}) collective-permute-start(bf16[256,192]{1,0:T(8,128)(2,1)} %get-tuple-element.121), channel_id=1, source_target_pairs={{0,16},{8,24},{16,0},{24,8},{1,17},{9,25},{17,1},{25,9},{2,18},{10... | collective-permute-start | bytes 294920 | tf_op jit(solution)/shard_map/ppermute | solution.py:555
  78.1 16.7 %collective-permute-start.18 = (bf16[256,192]{1,0:T(8,128)(2,1)}, bf16[256,192]{1,0:T(8,128)(2,1)S(1)}, u32[]{:S(2)}, u32[]{:S(2)}) collective-permute-start(bf16[256,192]{1,0:T(8,128)(2,1)} %get-tuple-element.122), channel_id=1, source_target_pairs={{0,24},{8,16},{16,8},{24,0},{1,25},{9,17},{17,9},{25,1},{2,26},{10... | collective-permute-start | bytes 294920 | tf_op jit(solution)/shard_map/ppermute | solution.py:555
  104.8 17.7 %collective-permute-start.19 = (bf16[8,432,768]{2,1,0:T(8,128)(2,1)}, bf16[8,432,768]{2,1,0:T(8,128)(2,1)}, u32[]{:S(2)}, u32[]{:S(2)}) collective-permute-start(bf16[8,432,768]{2,1,0:T(8,128)(2,1)} %bitcast.161), channel_id=1, source_target_pairs={{0,8},{8,0},{16,24},{24,16},{1,9},{9,1},{17,25},{25,17},{2,10},{10... | collective-permute-start | bytes 15925256 | tf_op jit(solution)/shard_map/ppermute | solution.py:555
  105.5 8.8 %collective-permute-start.20 = (bf16[256,192]{1,0:T(8,128)(2,1)S(1)}, bf16[256,192]{1,0:T(8,128)(2,1)S(1)}, u32[]{:S(2)}, u32[]{:S(2)}) collective-permute-start(bf16[256,192]{1,0:T(8,128)(2,1)S(1)} %copy-done.61), channel_id=1, source_target_pairs={{0,8},{8,0},{16,24},{24,16},{1,9},{9,1},{17,25},{25,17},{2,10},{10... | collective-permute-start | bytes 294920 | tf_op jit(solution)/shard_map/ppermute | solution.py:555
  105.6 9.0 %collective-permute-start.21 = (bf16[256,192]{1,0:T(8,128)(2,1)S(1)}, bf16[256,192]{1,0:T(8,128)(2,1)S(1)}, u32[]{:S(2)}, u32[]{:S(2)}) collective-permute-start(bf16[256,192]{1,0:T(8,128)(2,1)S(1)} %copy-done.56), channel_id=1, source_target_pairs={{0,16},{8,24},{16,0},{24,8},{1,17},{9,25},{17,1},{25,9},{2,18},{10... | collective-permute-start | bytes 294920 | tf_op jit(solution)/shard_map/ppermute | solution.py:555
  114.7 7.8 %collective-permute-start.25 = (bf16[256,192]{1,0:T(8,128)(2,1)}, bf16[256,192]{1,0:T(8,128)(2,1)S(1)}, u32[]{:S(2)}, u32[]{:S(2)}) collective-permute-start(bf16[256,192]{1,0:T(8,128)(2,1)} %get-tuple-element.136), channel_id=1, source_target_pairs={{0,24},{8,16},{16,8},{24,0},{1,25},{9,17},{17,9},{25,1},{2,26},{10... | collective-permute-start | bytes 294920 | tf_op jit(solution)/shard_map/ppermute | solution.py:555
  206.7 8.9 %collective-permute-start.29 = (bf16[8,432,768]{2,1,0:T(8,128)(2,1)S(1)}, bf16[8,432,768]{2,1,0:T(8,128)(2,1)S(1)}, u32[]{:S(2)}, u32[]{:S(2)}) collective-permute-start(bf16[8,432,768]{2,1,0:T(8,128)(2,1)S(1)} %pad_maximum_fusion), channel_id=1, source_target_pairs={{0,8},{8,0},{16,24},{24,16},{1,9},{9,1},{17,25},{25,17},{2,10},{10... | collective-permute-start | bytes 15925256 | tf_op jit(solution)/shard_map/ppermute | solution.py:555
  207.2 11.9 %collective-permute-start.26 = (bf16[256,192]{1,0:T(8,128)(2,1)S(1)}, bf16[256,192]{1,0:T(8,128)(2,1)S(1)}, u32[]{:S(2)}, u32[]{:S(2)}) collective-permute-start(bf16[256,192]{1,0:T(8,128)(2,1)S(1)} %copy-done.59), channel_id=1, source_target_pairs={{0,8},{8,0},{16,24},{24,16},{1,9},{9,1},{17,25},{25,17},{2,10},{10... | collective-permute-start | bytes 294920 | tf_op jit(solution)/shard_map/ppermute | solution.py:555
  207.6 11.5 %collective-permute-start.27 = (bf16[256,192]{1,0:T(8,128)(2,1)S(1)}, bf16[256,192]{1,0:T(8,128)(2,1)S(1)}, u32[]{:S(2)}, u32[]{:S(2)}) collective-permute-start(bf16[256,192]{1,0:T(8,128)(2,1)S(1)} %copy-done.58), channel_id=1, source_target_pairs={{0,16},{8,24},{16,0},{24,8},{1,17},{9,25},{17,1},{25,9},{2,18},{10... | collective-permute-start | bytes 294920 | tf_op jit(solution)/shard_map/ppermute | solution.py:555
  208.0 11.2 %collective-permute-start.28 = (bf16[256,192]{1,0:T(8,128)(2,1)S(1)}, bf16[256,192]{1,0:T(8,128)(2,1)S(1)}, u32[]{:S(2)}, u32[]{:S(2)}) collective-permute-start(bf16[256,192]{1,0:T(8,128)(2,1)S(1)} %copy-done.55), channel_id=1, source_target_pairs={{0,24},{8,16},{16,8},{24,0},{1,25},{9,17},{17,9},{25,1},{2,26},{10... | collective-permute-start | bytes 294920 | tf_op jit(solution)/shard_map/ppermute | solution.py:555
  221.4 24.7 %collective-permute-start.33 = (bf16[256,192]{1,0:T(8,128)(2,1)S(1)}, bf16[256,192]{1,0:T(8,128)(2,1)S(1)}, u32[]{:S(2)}, u32[]{:S(2)}) collective-permute-start(bf16[256,192]{1,0:T(8,128)(2,1)S(1)} %copy-done.41), channel_id=1, source_target_pairs={{0,8},{8,0},{16,24},{24,16},{1,9},{9,1},{17,25},{25,17},{2,10},{10... | collective-permute-start | bytes 294920 | tf_op jit(solution)/shard_map/ppermute | solution.py:555
  221.8 25.5 %collective-permute-start.34 = (bf16[256,192]{1,0:T(8,128)(2,1)S(1)}, bf16[256,192]{1,0:T(8,128)(2,1)S(1)}, u32[]{:S(2)}, u32[]{:S(2)}) collective-permute-start(bf16[256,192]{1,0:T(8,128)(2,1)S(1)} %copy-done.40), channel_id=1, source_target_pairs={{0,16},{8,24},{16,0},{24,8},{1,17},{9,25},{17,1},{25,9},{2,18},{10... | collective-permute-start | bytes 294920 | tf_op jit(solution)/shard_map/ppermute | solution.py:555
  222.1 25.1 %collective-permute-start.35 = (bf16[256,192]{1,0:T(8,128)(2,1)S(1)}, bf16[256,192]{1,0:T(8,128)(2,1)S(1)}, u32[]{:S(2)}, u32[]{:S(2)}) collective-permute-start(bf16[256,192]{1,0:T(8,128)(2,1)S(1)} %copy-done.39), channel_id=1, source_target_pairs={{0,24},{8,16},{16,8},{24,0},{1,25},{9,17},{17,9},{25,1},{2,26},{10... | collective-permute-start | bytes 294920 | tf_op jit(solution)/shard_map/ppermute | solution.py:555
  223.3 50.1 %collective-permute-start.39 = (bf16[256,192]{1,0:T(8,128)(2,1)S(1)}, bf16[256,192]{1,0:T(8,128)(2,1)S(1)}, u32[]{:S(2)}, u32[]{:S(2)}) collective-permute-start(bf16[256,192]{1,0:T(8,128)(2,1)S(1)} %copy-done.38), channel_id=1, source_target_pairs={{0,8},{8,0},{16,24},{24,16},{1,9},{9,1},{17,25},{25,17},{2,10},{10... | collective-permute-start | bytes 294920 | tf_op jit(solution)/shard_map/ppermute | solution.py:555
  223.9 49.9 %collective-permute-start.40 = (bf16[256,192]{1,0:T(8,128)(2,1)S(1)}, bf16[256,192]{1,0:T(8,128)(2,1)S(1)}, u32[]{:S(2)}, u32[]{:S(2)}) collective-permute-start(bf16[256,192]{1,0:T(8,128)(2,1)S(1)} %copy-done.37), channel_id=1, source_target_pairs={{0,16},{8,24},{16,0},{24,8},{1,17},{9,25},{17,1},{25,9},{2,18},{10... | collective-permute-start | bytes 294920 | tf_op jit(solution)/shard_map/ppermute | solution.py:555
  246.1 27.9 %collective-permute-start.41 = (bf16[256,192]{1,0:T(8,128)(2,1)S(1)}, bf16[256,192]{1,0:T(8,128)(2,1)S(1)}, u32[]{:S(2)}, u32[]{:S(2)}) collective-permute-start(bf16[256,192]{1,0:T(8,128)(2,1)S(1)} %copy-done.36), channel_id=1, source_target_pairs={{0,24},{8,16},{16,8},{24,0},{1,25},{9,17},{17,9},{25,1},{2,26},{10... | collective-permute-start | bytes 294920 | tf_op jit(solution)/shard_map/ppermute | solution.py:555
  247.3 26.7 %collective-permute-start.30 = (bf16[256,768]{1,0:T(8,128)(2,1)}, bf16[256,768]{1,0:T(8,128)(2,1)S(1)}, u32[]{:S(2)}, u32[]{:S(2)}) collective-permute-start(bf16[256,768]{1,0:T(8,128)(2,1)} %get-tuple-element.158), channel_id=1, source_target_pairs={{0,8},{8,0},{16,24},{24,16},{1,9},{9,1},{17,25},{25,17},{2,10},{10... | collective-permute-start | bytes 1179656 | tf_op jit(solution)/shard_map/ppermute | solution.py:555
  248.0 25.9 %collective-permute-start.31 = (bf16[256,768]{1,0:T(8,128)(2,1)}, bf16[256,768]{1,0:T(8,128)(2,1)S(1)}, u32[]{:S(2)}, u32[]{:S(2)}) collective-permute-start(bf16[256,768]{1,0:T(8,128)(2,1)} %get-tuple-element.160), channel_id=1, source_target_pairs={{0,8},{8,0},{16,24},{24,16},{1,9},{9,1},{17,25},{25,17},{2,10},{10... | collective-permute-start | bytes 1179656 | tf_op jit(solution)/shard_map/ppermute | solution.py:555
  273.4 49.6 %collective-permute-start.37 = (bf16[256,768]{1,0:T(8,128)(2,1)}, bf16[256,768]{1,0:T(8,128)(2,1)S(1)}, u32[]{:S(2)}, u32[]{:S(2)}) collective-permute-start(bf16[256,768]{1,0:T(8,128)(2,1)} %get-tuple-element.177), channel_id=1, source_target_pairs={{0,8},{8,0},{16,24},{24,16},{1,9},{9,1},{17,25},{25,17},{2,10},{10... | collective-permute-start | bytes 1179656 | tf_op jit(solution)/shard_map/ppermute | solution.py:555
  273.9 57.8 %collective-permute-start.36 = (bf16[256,768]{1,0:T(8,128)(2,1)}, bf16[256,768]{1,0:T(8,128)(2,1)}, u32[]{:S(2)}, u32[]{:S(2)}) collective-permute-start(bf16[256,768]{1,0:T(8,128)(2,1)} %get-tuple-element.175), channel_id=1, source_target_pairs={{0,8},{8,0},{16,24},{24,16},{1,9},{9,1},{17,25},{25,17},{2,10},{10... | collective-permute-start | bytes 1179656 | tf_op jit(solution)/shard_map/ppermute | solution.py:555
  288.7 28.7 %all-to-all-start.1 = ((f32[8,32,96]{2,1,0:T(8,128)}), f32[8,32,96]{2,1,0:T(8,128)S(1)}, u32[]{:S(2)}, u32[]{:S(2)}) async-start(f32[8,32,96]{2,1,0:T(8,128)} %pad.9.clone), calls=%async_computation.2 | async-start | bytes 262144 | tf_op jit(solution)/shard_map/all_to_all | solution.py:580
  313.3 17.1 %collective-permute-start.32 = (bf16[256,768]{1,0:T(8,128)(2,1)}, bf16[256,768]{1,0:T(8,128)(2,1)}, u32[]{:S(2)}, u32[]{:S(2)}) collective-permute-start(bf16[256,768]{1,0:T(8,128)(2,1)} %add_convert_fusion.3), channel_id=1, source_target_pairs={{0,16},{8,24},{16,0},{24,8},{1,17},{9,25},{17,1},{25,9},{2,18},{10... | collective-permute-start | bytes 1179656 | tf_op jit(solution)/shard_map/ppermute | solution.py:555
  317.4 32.3 %all-to-all-start = ((bf16[8,96,576]{2,1,0:T(8,128)(2,1)}), bf16[8,96,576]{2,1,0:T(8,128)(2,1)}, u32[]{:S(2)}, u32[]{:S(2)}) async-start(bf16[8,96,576]{2,1,0:T(8,128)(2,1)} %bitcast.50), calls=%async_computation | async-start | bytes 1966080 | tf_op jit(solution)/shard_map/all_to_all | solution.py:580
  323.8 12.2 %collective-permute-start.38 = (bf16[256,768]{1,0:T(8,128)(2,1)S(1)}, bf16[256,768]{1,0:T(8,128)(2,1)}, u32[]{:S(2)}, u32[]{:S(2)}) collective-permute-start(bf16[256,768]{1,0:T(8,128)(2,1)S(1)} %add_convert_fusion.2), channel_id=1, source_target_pairs={{0,16},{8,24},{16,0},{24,8},{1,17},{9,25},{17,1},{25,9},{2,18},{10... | collective-permute-start | bytes 1179656 | tf_op jit(solution)/shard_map/ppermute | solution.py:555
  326.1 11.1 %collective-permute-start.42 = (bf16[256,768]{1,0:T(8,128)(2,1)}, bf16[256,768]{1,0:T(8,128)(2,1)}, u32[]{:S(2)}, u32[]{:S(2)}) collective-permute-start(bf16[256,768]{1,0:T(8,128)(2,1)} %get-tuple-element.192), channel_id=1, source_target_pairs={{0,8},{8,0},{16,24},{24,16},{1,9},{9,1},{17,25},{25,17},{2,10},{10... | collective-permute-start | bytes 1179656 | tf_op jit(solution)/shard_map/ppermute | solution.py:555
  329.3 14.4 %collective-permute-start.44 = (bf16[256,768]{1,0:T(8,128)(2,1)S(1)}, bf16[256,768]{1,0:T(8,128)(2,1)S(1)}, u32[]{:S(2)}, u32[]{:S(2)}) collective-permute-start(bf16[256,768]{1,0:T(8,128)(2,1)S(1)} %add_convert_fusion.1), channel_id=1, source_target_pairs={{0,16},{8,24},{16,0},{24,8},{1,17},{9,25},{17,1},{25,9},{2,18},{10... | collective-permute-start | bytes 1179656 | tf_op jit(solution)/shard_map/ppermute | solution.py:555
  351.7 18.0 %collective-permute-start.48 = (bf16[432,768]{1,0:T(8,128)(2,1)}, bf16[432,768]{1,0:T(8,128)(2,1)S(1)}, u32[]{:S(2)}, u32[]{:S(2)}) collective-permute-start(bf16[432,768]{1,0:T(8,128)(2,1)} %reduce-scatter.2.cloned.1.call-done), channel_id=1, source_target_pairs={{0,16},{8,24},{16,0},{24,8},{1,17},{9,25},{17,1},{25,9},{2,18},{10... | collective-permute-start | bytes 1990664 | tf_op jit(solution)/shard_map/ppermute | solution.py:555
  354.0 19.0 %collective-permute-start.45 = (bf16[96,576]{1,0:T(8,128)(2,1)S(1)}, bf16[96,576]{1,0:T(8,128)(2,1)S(1)}, u32[]{:S(2)}, u32[]{:S(2)}) collective-permute-start(bf16[96,576]{1,0:T(8,128)(2,1)S(1)} %copy-done.9), channel_id=1, source_target_pairs={{0,8},{8,0},{16,24},{24,16},{1,9},{9,1},{17,25},{25,17},{2,10},{10... | collective-permute-start | bytes 331784 | tf_op jit(solution)/shard_map/ppermute | solution.py:555
  354.1 18.9 %collective-permute-start.46 = (bf16[96,576]{1,0:T(8,128)(2,1)S(1)}, bf16[96,576]{1,0:T(8,128)(2,1)S(1)}, u32[]{:S(2)}, u32[]{:S(2)}) collective-permute-start(bf16[96,576]{1,0:T(8,128)(2,1)S(1)} %copy-done.9), channel_id=1, source_target_pairs={{0,16},{8,24},{16,0},{24,8},{1,17},{9,25},{17,1},{25,9},{2,18},{10... | collective-permute-start | bytes 331784 | tf_op jit(solution)/shard_map/ppermute | solution.py:555
  354.8 18.3 %collective-permute-start.47 = (bf16[96,576]{1,0:T(8,128)(2,1)S(1)}, bf16[96,576]{1,0:T(8,128)(2,1)S(1)}, u32[]{:S(2)}, u32[]{:S(2)}) collective-permute-start(bf16[96,576]{1,0:T(8,128)(2,1)S(1)} %copy-done.9), channel_id=1, source_target_pairs={{0,24},{8,16},{16,8},{24,0},{1,25},{9,17},{17,9},{25,1},{2,26},{10... | collective-permute-start | bytes 331784 | tf_op jit(solution)/shard_map/ppermute | solution.py:555
  (84 other events, 491.9 us)
Sparse Core Ops, SparseCore 0:
  11.2 92.5 all-gather.2
  219.4 111.9 reduce-scatter.1
where the time goes:
time: 395 us; the launch traced here: 387 us
  Pallas kernels  164 us (42%)
  waiting for transfers between devices  74.1 us (19%)
  starting transfers between devices  59.6 us (15%)
  other arithmetic  28 us (7%)
  local copies, waits for them, and re-layouts  25.7 us (7%)
  matrix products  19.9 us (5%)
  between operations  15.8 us (4%)
    pallas_call x1, Pallas kernels, token_stage(): pl.pallas_call(functools.partial(token_kernel, plan, seqs, parts), grid=(...  69.7 us
    ppermute x53, waiting for transfers between devices, swap(): return lax.ppermute(values, axis, [(i, i ^ mask) for i in range(count)])  66 us
    pallas_call x3, Pallas kernels, attend_backward(): pl.pallas_call(functools.partial(attend_back_kernel, parts, heads, rows),...  53.6 us
    pallas_call x3, Pallas kernels, attend_forward(): pl.pallas_call(functools.partial(attend_kernel, parts, heads, rows), grid...  40.3 us
    ppermute x53, starting transfers between devices, swap(): return lax.ppermute(values, axis, [(i, i ^ mask) for i in range(count)])  37.3 us
    all_to_all x2, starting transfers between devices, sum_blocks(): lax.all_to_all(blocks.astype(kind), axis, split_axis=0, concat_axis=0, ti...  22.2 us
    dot_general x8, matrix products, mm_tn(): lax.dot_general(left, right, (((0,), (0,)), ((), ())), preferred_element_...  18.8 us
    all_to_all x2, waiting for transfers between devices, sum_blocks(): lax.all_to_all(blocks.astype(kind), axis, split_axis=0, concat_axis=0, ti...  8.08 us
  transfers between devices with their start and end apart: 57, of which 16 were waited for; matrix products, arithmetic and copies ran while one was open for 12% of the time, Pallas kernels for 24%

commit v1 on v0

--- a/solution.py
+++ b/solution.py
@@ -286,13 +286,13 @@
     mds = take(seqs * parts)
     dsum, msum, fsum = take(3)
     wo, w1, w2, ob, munit, mscale, res, runit, rscale = take(9)
-    pre, cdf, act, hg, fscale, ngs, dacc, macc, facc, sems = take(10)
+    pre, slope, act, hg, ngs, dacc, macc, facc, sems = take(9)
     step = pl.program_id(0)
     me, core = info[seqs], info[seqs + 1]
     live = info[step] - me * x.shape[0]
     rows, width = x.shape
     span, units = width // parts, pre.shape[1]
-    tile, wide = 16, 384
+    band, wide = 64, 256
     quarters = units // width
 
     def place(quarter):
@@ -301,10 +301,10 @@
 
     targets = {"out": wo, "fc1": w1, "fc2": w2}
 
-    @pl.when(step == 0)
-    def _():
-        copies = []
+    def copies(wanted):
         for index, (src, k, start, count, name, at, at_step, col, col_step) in enumerate(plan):
+            if name not in wanted:
+                continue
             source = sources[src] if k is None else sources[src].at[k]
             target = targets[name]
             turn = core if src == 0 else 1 - core
@@ -313,16 +313,21 @@
             if col_step:
                 col = pl.multiple_of(col + col_step * turn, 128)
             target = target.at[pl.ds(at, count), pl.ds(col, source.shape[1])]
-            copies.append(
-                pltpu.make_async_copy(source.at[pl.ds(start, count)], target, sems.at[index])
-            )
-        for copy in copies:
+            yield pltpu.make_async_copy(source.at[pl.ds(start, count)], target, sems.at[index])
+
+    def arrived(name):
+        @pl.when(step == 0)
+        def _():
+            for copy in copies((name,)):
+                copy.wait()
+
+    @pl.when(step == 0)
+    def _():
+        for copy in copies(("out", "fc1", "fc2")):
             copy.start()
         dacc[...] = jnp.zeros_like(dacc)
         macc[...] = jnp.zeros_like(macc)
         facc[...] = jnp.zeros_like(facc)
-        for copy in copies:
-            copy.wait()
 
     for i in range(seqs):
 
@@ -355,6 +360,7 @@
             munit[j, at, :] = unit
             anorm[g, at, :] = (unit * mgain[g] + mshift[g]).astype(BF16)
 
+    arrived("out")
     mixed = sum(mm(anorm[g], wo[g * span : (g + 1) * span, :]) for g in range(parts))
     res[...] = x[...].astype(F32) + mixed + dvec[2:3, :]
 
@@ -365,71 +371,83 @@
         rscale[at, :] = jnp.broadcast_to(scale, (32, 128))
         fnorm[at, :] = (unit * dvec[0:1, :] + dvec[1:2, :]).astype(BF16)
 
-    for c in range(units // width):
-        cols = slice(c * width, (c + 1) * width)
-        pre[:, cols] = mm(fnorm[...], w1[:, cols])
-    chunks = [slice(c, c + wide) for c in range(0, units, wide)]
-
-    @tiles(tile)
-    def _(at, first):
-        total, square = 0.0, 0.0
-        for c in chunks:
-            v = pre[at, c] + fvec[1:2, c]
-            below = 0.5 * (1.0 + lax.erf(v * 0.7071067811865476))
-            a = v * below
-            pre[at, c] = v
-            cdf[at, c] = below
-            act[at, c] = a
-            total = total + a
-        mean = jnp.sum(total, axis=1, keepdims=True) / units
-        for c in chunks:
-            d = act[at, c] - mean
-            act[at, c] = d
-            square = square + d * d
-        scale = lax.rsqrt(jnp.sum(square, axis=1, keepdims=True) / units + eps)
-        fscale[at, :] = jnp.broadcast_to(scale, (tile, 128))
-        for c in chunks:
-            unit = act[at, c] * scale
-            act[at, c] = unit
-            value = (unit * fvec[0:1, c] + fvec[2:3, c]).astype(BF16)
-            hid[at, c] = value
-
-    out = res[...] + mm(hid[...], w2[...]) + dvec[3:4, :]
-    block_out[...] = live_only(out, 0, live).astype(BF16)
     kept = live_only(cot[...].astype(F32), 0, live)
     og[...] = kept.astype(BF16)
     dacc[24:32, :] += folded(kept)
-    for c in range(units // width):
-        cols = slice(c * width, (c + 1) * width)
-        hg[:, cols] = mm_nt(og[...], w2[cols, :])
-
-    @tiles(tile)
-    def _(at, first):
-        one, two = 0.0, 0.0
-        for c in chunks:
-            unit, grad = act[at, c], hg[at, c]
-            both = grad * unit
-            facc[0:8, c] += folded(both)
-            facc[16:24, c] += folded(grad)
+    chunks = [slice(c, c + wide) for c in range(0, units, wide)]
+    bands = [slice(r, r + band) for r in range(0, rows, band)]
+
+    def lanes(chunk):
+        return [slice(c, c + 128) for c in range(chunk.start, chunk.stop, 128)]
+
+    def row_mean(parts_of):
+        return [jnp.sum(v, axis=1, keepdims=True) / units for v in parts_of]
+
+    arrived("fc1")
+    arrived("fc2")
+    total = [jnp.zeros((band, 128), F32) for _ in bands]
+    pre[:, chunks[0]] = mm(fnorm[...], w1[:, chunks[0]])
+    for index, chunk in enumerate(chunks):
+        if index + 1 < len(chunks):
+            after_it = chunks[index + 1]
+            pre[:, after_it] = mm(fnorm[...], w1[:, after_it])
+        for c in lanes(chunk):
+            for b, r in enumerate(bands):
+                v = pre[r, c] + fvec[1:2, c]
+                below = 0.5 * (1.0 + lax.erf(v * 0.7071067811865476))
+                a = v * below
+                slope[r, c] = below + v * (jnp.exp(-0.5 * v * v) * 0.3989422804014327)
+                act[r, c] = a
+                total[b] = total[b] + a
+    mean = row_mean(total)
+    total = [jnp.zeros((band, 128), F32) for _ in bands]
+    for chunk in chunks:
+        hg[:, chunk] = mm_nt(og[...], w2[chunk, :])
+        for c in lanes(chunk):
+            for b, r in enumerate(bands):
+                d = act[r, c] - mean[b]
+                total[b] = total[b] + d * d
+    scale = [lax.rsqrt(v + eps) for v in row_mean(total)]
+    one = [jnp.zeros((band, 128), F32) for _ in bands]
+    two = [jnp.zeros((band, 128), F32) for _ in bands]
+    out = res[...] + dvec[3:4, :]
+    for chunk in chunks:
+        for c in lanes(chunk):
             gain = fvec[0:1, c]
-            hg[at, c] = grad * gain
-            one = one + grad * gain
-            two = two + both * gain
-        one = jnp.sum(one, axis=1, keepdims=True) / units
-        two = jnp.sum(two, axis=1, keepdims=True) / units
-        scale = fscale[at, 0:1]
-        for c in chunks:
-            v = pre[at, c]
-            slope = cdf[at, c] + v * (jnp.exp(-0.5 * v * v) * 0.3989422804014327)
-            grad = scale * (hg[at, c] - one - act[at, c] * two) * slope
-            low = grad.astype(BF16)
-            pg[place(c.start // width), at, c.start % width : c.start % width + wide] = low
-            facc[8:16, c] += folded(low.astype(F32))
-
-    fg = hg.at[:, 0:width]
-    fg[...] = sum(
-        mm_nt(pg[place(c)], w1[:, c * width : (c + 1) * width]) for c in range(units // width)
-    )
+            gain_sum, shift_sum = 0.0, 0.0
+            for b, r in enumerate(bands):
+                unit = (act[r, c] - mean[b]) * scale[b]
+                act[r, c] = unit
+                hid[r, c] = (unit * gain + fvec[2:3, c]).astype(BF16)
+                grad = hg[r, c]
+                gain_sum = gain_sum + folded(grad * unit)
+                shift_sum = shift_sum + folded(grad)
+                grad = grad * gain
+                hg[r, c] = grad
+                one[b] = one[b] + grad
+                two[b] = two[b] + grad * unit
+            facc[0:8, c] += gain_sum
+            facc[16:24, c] += shift_sum
+        if chunk.stop % width == 0:
+            ready = slice(chunk.stop - width, chunk.stop)
+            out = out + mm(hid[:, ready], w2[ready, :])
+    block_out[...] = live_only(out, 0, live).astype(BF16)
+    one, two = row_mean(one), row_mean(two)
+    total = 0.0
+    for chunk in chunks:
+        quarter, base = chunk.start // width, chunk.start // width * width
+        for c in lanes(chunk):
+            low_sum = 0.0
+            for b, r in enumerate(bands):
+                grad = scale[b] * (hg[r, c] - one[b] - act[r, c] * two[b]) * slope[r, c]
+                low = grad.astype(BF16)
+                pg[place(quarter), r, c.start - base : c.stop - base] = low
+                low_sum = low_sum + folded(low.astype(F32))
+            facc[8:16, c] += low_sum
+        if chunk.stop % width == 0:
+            total = total + mm_nt(pg[place(quarter)], w1[:, base : base + width])
+    fg = res
+    fg[...] = total
 
     @tiles(32)
     def _(at, first):
@@ -529,7 +547,6 @@
         ]
         + [pltpu.VMEM((rows, units), F32)] * 4
         + [
-            pltpu.VMEM((rows, 128), F32),
             pltpu.VMEM((parts, rows, span), F32),
             pltpu.VMEM((32, width), F32),
             pltpu.VMEM((parts, 16, span), F32),

time: 395 us -> 382 us (0.967)
  the two profiles are of different devices: /device:TPU:0 before, /device:TPU:1 now
where the time goes in v1:
time: 382 us; the launch traced here: 375 us
  Pallas kernels  151 us (40%)
  waiting for transfers between devices  70.9 us (19%)
  starting transfers between devices  62.8 us (16%)
  other arithmetic  28 us (7%)
  local copies, waits for them, and re-layouts  26.3 us (7%)
  matrix products  19.7 us (5%)
  between operations  15.9 us (4%)
    ppermute x53, waiting for transfers between devices, swap(): return lax.ppermute(values, axis, [(i, i ^ mask) for i in range(count)])  62.4 us
    pallas_call x1, Pallas kernels, token_stage(): pl.pallas_call(functools.partial(token_kernel, plan, seqs, parts), grid=(...  57.4 us
    pallas_call x3, Pallas kernels, attend_backward(): pl.pallas_call(functools.partial(attend_back_kernel, parts, heads, rows),...  53.5 us
    ppermute x53, starting transfers between devices, swap(): return lax.ppermute(values, axis, [(i, i ^ mask) for i in range(count)])  40.6 us
    pallas_call x3, Pallas kernels, attend_forward(): pl.pallas_call(functools.partial(attend_kernel, parts, heads, rows), grid...  40.3 us
    all_to_all x2, starting transfers between devices, sum_blocks(): lax.all_to_all(blocks.astype(kind), axis, split_axis=0, concat_axis=0, ti...  22.1 us
    dot_general x8, matrix products, mm_tn(): lax.dot_general(left, right, (((0,), (0,)), ((), ())), preferred_element_...  18.6 us
    all_to_all x2, waiting for transfers between devices, sum_blocks(): lax.all_to_all(blocks.astype(kind), axis, split_axis=0, concat_axis=0, ti...  8.52 us
  transfers between devices with their start and end apart: 57, of which 16 were waited for; matrix products, arithmetic and copies ran while one was open for 13% of the time, Pallas kernels for 25%

profile of v1, /device:TPU:1, one launch (start us, length us, event | category | flops | bytes accessed | tf_op | source)
XLA Modules:
  0.0 374.8 jit_solution(12408079549076547924)
XLA Ops:
  7.3 1.7 reshape.146
  11.1 3.2 collective-permute-start.3
  14.3 1.3 collective-permute-start.4
  16.9 1.3 collective-permute-start.1
  18.2 1.8 collective-permute-start
  21.0 2.0 pad_add_fusion.2
  25.7 13.8 %collective-permute-done.5 = bf16[128,576]{0,1:T(8,128)(2,1)} collective-permute-done((bf16[128,576]{0,1:T(8,128)(2,1)S(1)}, bf16[128,576]{0,1:T(8,128)(2,1)}, u32[]{:S(2)}, u32[]{:S(2)}) %collective-permute-start.5) | collective-permute-done | bytes 147488 | tf_op jit(solution)/shard_map/ppermute | solution.py:572
  40.8 1.5 collective-permute-start.9
  42.4 2.3 collective-permute-done.8
  44.6 2.0 collective-permute-start.10
  49.5 8.1 %collective-permute-done.14.refs_2_ = bf16[256,768]{1,0:T(8,128)(2,1)S(1)} collective-permute-done((bf16[256,768]{1,0:T(8,128)(2,1)S(1)}, bf16[256,768]{1,0:T(8,128)(2,1)S(1)}, u32[]{:S(2)}, u32[]{:S(2)}) %collective-permute-start.14) | collective-permute-done | bytes 393248 | tf_op jit(solution)/shard_map/ppermute | solution.py:572
  61.6 15.6 %attend_forward.3 = (bf16[4,256,768]{2,1,0:T(8,128)(2,1)}, bf16[3,1024,64]{2,1,0:T(8,128)(2,1)}, bf16[3,1024,64]{2,1,0:T(8,128)(2,1)}, bf16[3,1024,64]{2,1,0:T(8...) custom-call(s32[2]{0:T(128)} %pad_add_fusion.1.info, ...), custom_call_target="tpu_custom_call" | custom-call | flops 1711276032 | bytes 6389760 | tf_op jit(solution)/shard_map/attend_forward/pallas_call | solution.py:134
  77.4 2.1 collective-permute-start.18
  79.5 15.4 %attend_forward.4 = (bf16[4,256,768]{2,1,0:T(8,128)(2,1)}, bf16[3,1024,64]{2,1,0:T(8,128)(2,1)}, bf16[3,1024,64]{2,1,0:T(8,128)(2,1)}, bf16[3,1024,64]{2,1,0:T(8...) custom-call(s32[2]{0:T(128)} %get-tuple-element.267.info, ...), custom_call_target="tpu_custom_call" | custom-call | flops 1711276032 | bytes 6389760 | tf_op jit(solution)/shard_map/attend_forward/pallas_call | solution.py:134
  95.7 9.2 %attend_forward.5 = (bf16[4,256,768]{2,1,0:T(8,128)(2,1)}, bf16[3,1024,64]{2,1,0:T(8,128)(2,1)}, bf16[3,1024,64]{2,1,0:T(8,128)(2,1)}, bf16[3,1024,64]{2,1,0:T(8...) custom-call(s32[2]{0:T(128)} %get-tuple-element.268.info, ...), custom_call_target="tpu_custom_call" | custom-call | flops 1711276032 | bytes 6389760 | tf_op jit(solution)/shard_map/attend_forward/pallas_call | solution.py:134
  108.6 1.7 collective-permute-start.22
  110.4 3.8 %collective-permute-done.20.refs_7_ = bf16[256,192]{1,0:T(8,128)(2,1)S(1)} collective-permute-done((bf16[256,192]{1,0:T(8,128)(2,1)S(1)}, bf16[256,192]{1,0:T(8,128)(2,1)S(1)}, u32[]{:S(2)}, u32[]{:S(2)}) %collective-permute-start.20) | collective-permute-done | bytes 98336 | tf_op jit(solution)/shard_map/ppermute | solution.py:572
  114.3 1.7 collective-permute-start.25
  116.6 2.7 collective-permute-done.24.refs_12_
  119.3 3.1 collective-permute-done.25.refs_13_
  123.1 57.4 %token_stage.1 = (bf16[3,256,768]{2,1,0:T(8,128)(2,1)}, f32[3,256,768]{2,1,0:T(8,128)}, bf16[768,768]{1,0:T(8,128)(2,1)}, bf16[768,768]{1,0:T(8,128)(2,1)}, bf16...) custom-call(s32[5]{0:T(128)} %pad_add_fusion.info, ...), custom_call_target="tpu_custom_call" | custom-call | flops 16307453952 | bytes 43646976 | tf_op jit(solution)/shard_map/token_stage/pallas_call | solution.py:510
  180.4 1.7 copy.90
  182.2 2.5 convolution_convert_fusion.1
  189.1 4.3 %fusion.37 = bf16[3072,768]{1,0:T(8,128)(2,1)S(1)} fusion(bf16[768,3072]{1,0:T(8,128)(2,1)S(1)} %bitcast.164, bf16[768,768]{1,0:T(8,128)(2,1)S(1)} %copy-done.72), kind=kOutput, calls=%fused_computation.136 | convolution fusion | flops 3623878656 | bytes 10616832 | tf_op jit(solution)/shard_map/dot_general | solution.py:27
  194.9 2.0 collective-permute-start.28
  199.1 4.0 %collective-permute-done.29 = bf16[8,432,768]{2,1,0:T(8,128)(2,1)S(1)} collective-permute-done((bf16[8,432,768]{2,1,0:T(8,128)(2,1)S(1)}, bf16[8,432,768]{2,1,0:T(8,128)(2,1)S(1)}, u32[]{:S(2)}, u32[]{:S(2)}) %collective-permute-start.29) | collective-permute-done | bytes 5308448 | tf_op jit(solution)/shard_map/ppermute | solution.py:572
  203.1 3.6 add_convert_fusion
  209.1 1.9 collective-permute-start.35
  211.9 21.1 %attend_backward.3 = (bf16[4,256,576]{2,1,0:T(8,128)(2,1)}, bf16[256,768]{1,0:T(8,128)(2,1)}, bf16[256,768]{1,0:T(8,128)(2,1)}, bf16[256,768]{1,0:T(8,128)(2,1)}...) custom-call(s32[2]{0:T(128)} %pad_add_fusion.1.info, bf16[256,768]{1,0:T(8,128)(2,1)} %copy-done.12, ...), custom_call_target="tpu_custom_call" | custom-call | flops 2919235584 | bytes 9142272 | tf_op jit(solution)/shard_map/attend_backward/pallas_call | solution.py:244
  233.1 2.0 collective-permute-start.41
  235.8 21.0 %attend_backward.4 = (bf16[4,256,576]{2,1,0:T(8,128)(2,1)}, bf16[256,768]{1,0:T(8,128)(2,1)}, bf16[256,768]{1,0:T(8,128)(2,1)}, bf16[256,768]{1,0:T(8,128)(2,1)}...) custom-call(s32[2]{0:T(128)} %get-tuple-element.267.info, bf16[256,768]{1,0:T(8,128)(2,1)} %copy-done.11, ...), custom_call_target="tpu_custom_call" | custom-call | flops 2919235584 | bytes 9142272 | tf_op jit(solution)/shard_map/attend_backward/pallas_call | solution.py:244
  256.8 4.2 %fusion.38 = f32[768,576,1]{0,1,2:T(8,128)} fusion(bf16[4,256,768]{2,1,0:T(8,128)(2,1)} %get-tuple-element.197, bf16[4,256,576]{2,1,0:T(8,128)(2,1)} %get-tuple-element.198), kind=kOutput, calls=%fused_computation.137 | convolution fusion | flops 905969664 | bytes 4521984 | tf_op jit(solution)/shard_map/dot_general | solution.py:27
  262.2 11.3 %attend_backward.5 = (bf16[4,256,576]{2,1,0:T(8,128)(2,1)}, bf16[256,768]{1,0:T(8,128)(2,1)}, bf16[256,768]{1,0:T(8,128)(2,1)}, bf16[256,768]{1,0:T(8,128)(2,1)}...) custom-call(s32[2]{0:T(128)} %get-tuple-element.268.info, bf16[256,768]{1,0:T(8,128)(2,1)} %copy-done.10, ...), custom_call_target="tpu_custom_call" | custom-call | flops 2919235584 | bytes 9142272 | tf_op jit(solution)/shard_map/attend_backward/pallas_call | solution.py:244
  276.2 17.7 %all-to-all-start.1 = ((f32[8,32,96]{2,1,0:T(8,128)}), f32[8,32,96]{2,1,0:T(8,128)S(1)}, u32[]{:S(2)}, u32[]{:S(2)}) async-start(f32[8,32,96]{2,1,0:T(8,128)} %pad.9.clone), calls=%async_computation.2 | async-start | bytes 262144 | tf_op jit(solution)/shard_map/all_to_all | solution.py:597
  293.9 3.1 fusion.39
  297.1 1.3 fusion.11
  298.4 1.3 copy.95
  301.2 3.3 all-to-all-done.1
  304.5 4.4 %all-to-all-start = ((bf16[8,96,576]{2,1,0:T(8,128)(2,1)}), bf16[8,96,576]{2,1,0:T(8,128)(2,1)}, u32[]{:S(2)}, u32[]{:S(2)}) async-start(bf16[8,96,576]{2,1,0:T(8,128)(2,1)} %bitcast.50), calls=%async_computation | async-start | bytes 1966080 | tf_op jit(solution)/shard_map/all_to_all | solution.py:597
  318.5 3.5 collective-permute-done.38
  323.3 7.2 %collective-permute-done.44 = bf16[256,768]{1,0:T(8,128)(2,1)S(1)} collective-permute-done((bf16[256,768]{1,0:T(8,128)(2,1)S(1)}, bf16[256,768]{1,0:T(8,128)(2,1)S(1)}, u32[]{:S(2)}, u32[]{:S(2)}) %collective-permute-start.44) | collective-permute-done | bytes 393248 | tf_op jit(solution)/shard_map/ppermute | solution.py:572
  331.6 5.3 %all-to-all-done = bf16[8,96,576]{2,1,0:T(8,128)(2,1)} async-done(((bf16[8,96,576]{2,1,0:T(8,128)(2,1)}), bf16[8,96,576]{2,1,0:T(8,128)(2,1)}, u32[]{:S(2)}, u32[]{:S(2)}) %all-to-all-start) | async-done | bytes 884768 | tf_op jit(solution)/shard_map/all_to_all | solution.py:597
  336.8 2.0 reduce_sum.61
  342.0 1.4 collective-permute-start.47
  343.4 11.7 %collective-permute-done.48 = bf16[432,768]{1,0:T(8,128)(2,1)S(1)} collective-permute-done((bf16[432,768]{1,0:T(8,128)(2,1)}, bf16[432,768]{1,0:T(8,128)(2,1)S(1)}, u32[]{:S(2)}, u32[]{:S(2)}) %collective-permute-start.48) | collective-permute-done | bytes 663584 | tf_op jit(solution)/shard_map/ppermute | solution.py:572
  356.3 2.3 collective-permute-start.49
  358.6 1.9 fusion.7
  362.7 1.6 broadcast_select_fusion.1
  (375 shorter events, 59.7 us)
Async XLA Ops:
  7.2 97.7 %all-gather.3.cloned.1.call-start = ((), (), s32[]{:S(2)}) async-start(), calls=%async_computation.4 | async-start | bytes 5971968 | tf_op jit(solution)/shard_map/all_gather | solution.py:651
  11.1 327.8 %reduce-scatter.2.cloned.1.call-start = ((), (), s32[]{:S(2)}) async-start(), calls=%async_computation.3 | async-start | bytes 5971968 | tf_op jit(solution)/shard_map/reduce_scatter | solution.py:732
  11.1 13.2 %collective-permute-start.3 = (bf16[128,576]{0,1:T(8,128)(2,1)S(1)}, bf16[128,576]{0,1:T(8,128)(2,1)S(1)}, u32[]{:S(2)}, u32[]{:S(2)}) collective-permute-start(bf16[128,576]{0,1:T(8,128)(2,1)S(1)} %fusion.26), channel_id=1, source_target_pairs={{0,4},{1,5},{2,6},{3,7},{4,0},{5,1},{6,2},{7,3},{8,12},{9,13},{10,... | collective-permute-start | bytes 442376 | tf_op jit(solution)/shard_map/ppermute | solution.py:572
  14.3 10.4 %collective-permute-start.4 = (bf16[128,576]{0,1:T(8,128)(2,1)S(1)}, bf16[128,576]{0,1:T(8,128)(2,1)S(1)}, u32[]{:S(2)}, u32[]{:S(2)}) collective-permute-start(bf16[128,576]{0,1:T(8,128)(2,1)S(1)} %fusion.26), channel_id=1, source_target_pairs={{0,2},{1,3},{2,0},{3,1},{4,6},{5,7},{6,4},{7,5},{8,10},{9,11},{10,... | collective-permute-start | bytes 442376 | tf_op jit(solution)/shard_map/ppermute | solution.py:572
  15.6 9.6 %collective-permute-start.6 = (bf16[128,576]{0,1:T(8,128)(2,1)S(1)}, bf16[128,576]{0,1:T(8,128)(2,1)S(1)}, u32[]{:S(2)}, u32[]{:S(2)}) collective-permute-start(bf16[128,576]{0,1:T(8,128)(2,1)S(1)} %fusion.26), channel_id=1, source_target_pairs={{0,1},{1,0},{2,3},{3,2},{4,5},{5,4},{6,7},{7,6},{8,9},{9,8},{10,11... | collective-permute-start | bytes 442376 | tf_op jit(solution)/shard_map/ppermute | solution.py:572
  16.9 29.9 %collective-permute-start.1 = (bf16[256,768]{1,0:T(8,128)(2,1)S(1)}, bf16[256,768]{1,0:T(8,128)(2,1)}, u32[]{:S(2)}, u32[]{:S(2)}) collective-permute-start(bf16[256,768]{1,0:T(8,128)(2,1)S(1)} %get-tuple-element.242.refs_0_), channel_id=1, source_target_pairs={{0,16},{8,24},{16,0},{24,8},{1,17},{9,25},{17,1},{25,9},{2,18},{10... | collective-permute-start | bytes 1179656 | tf_op jit(solution)/shard_map/ppermute | solution.py:572
  18.2 31.2 %collective-permute-start = (bf16[256,768]{1,0:T(8,128)(2,1)S(1)}, bf16[256,768]{1,0:T(8,128)(2,1)}, u32[]{:S(2)}, u32[]{:S(2)}) collective-permute-start(bf16[256,768]{1,0:T(8,128)(2,1)S(1)} %get-tuple-element.242.refs_0_), channel_id=1, source_target_pairs={{0,8},{8,0},{16,24},{24,16},{1,9},{9,1},{17,25},{25,17},{2,10},{10... | collective-permute-start | bytes 1179656 | tf_op jit(solution)/shard_map/ppermute | solution.py:572
  24.5 15.0 %collective-permute-start.5 = (bf16[128,576]{0,1:T(8,128)(2,1)S(1)}, bf16[128,576]{0,1:T(8,128)(2,1)}, u32[]{:S(2)}, u32[]{:S(2)}) collective-permute-start(bf16[128,576]{0,1:T(8,128)(2,1)S(1)} %collective-permute-done.3), channel_id=1, source_target_pairs={{0,2},{1,3},{2,0},{3,1},{4,6},{5,7},{6,4},{7,5},{8,10},{9,11},{10,... | collective-permute-start | bytes 442376 | tf_op jit(solution)/shard_map/ppermute | solution.py:572
  24.7 22.2 %collective-permute-start.11 = (bf16[256,768]{1,0:T(8,128)(2,1)S(1)}, bf16[256,768]{1,0:T(8,128)(2,1)}, u32[]{:S(2)}, u32[]{:S(2)}) collective-permute-start(bf16[256,768]{1,0:T(8,128)(2,1)S(1)} %get-tuple-element.114.refs_0_), channel_id=1, source_target_pairs={{0,16},{8,24},{16,0},{24,8},{1,17},{9,25},{17,1},{25,9},{2,18},{10... | collective-permute-start | bytes 1179656 | tf_op jit(solution)/shard_map/ppermute | solution.py:572
  25.4 15.3 %collective-permute-start.7 = (bf16[128,576]{0,1:T(8,128)(2,1)S(1)}, bf16[128,576]{0,1:T(8,128)(2,1)S(1)}, u32[]{:S(2)}, u32[]{:S(2)}) collective-permute-start(bf16[128,576]{0,1:T(8,128)(2,1)S(1)} %collective-permute-done.3), channel_id=1, source_target_pairs={{0,1},{1,0},{2,3},{3,2},{4,5},{5,4},{6,7},{7,6},{8,9},{9,8},{10,11... | collective-permute-start | bytes 442376 | tf_op jit(solution)/shard_map/ppermute | solution.py:572
  44.6 32.6 %collective-permute-start.10 = (bf16[256,768]{1,0:T(8,128)(2,1)S(1)}, bf16[256,768]{1,0:T(8,128)(2,1)}, u32[]{:S(2)}, u32[]{:S(2)}) collective-permute-start(bf16[256,768]{1,0:T(8,128)(2,1)S(1)} %get-tuple-element.114.refs_0_), channel_id=1, source_target_pairs={{0,8},{8,0},{16,24},{24,16},{1,9},{9,1},{17,25},{25,17},{2,10},{10... | collective-permute-start | bytes 1179656 | tf_op jit(solution)/shard_map/ppermute | solution.py:572
  46.8 10.8 %collective-permute-start.14 = (bf16[256,768]{1,0:T(8,128)(2,1)S(1)}, bf16[256,768]{1,0:T(8,128)(2,1)S(1)}, u32[]{:S(2)}, u32[]{:S(2)}) collective-permute-start(bf16[256,768]{1,0:T(8,128)(2,1)S(1)} %get-tuple-element.123.refs_0_), channel_id=1, source_target_pairs={{0,16},{8,24},{16,0},{24,8},{1,17},{9,25},{17,1},{25,9},{2,18},{10... | collective-permute-start | bytes 1179656 | tf_op jit(solution)/shard_map/ppermute | solution.py:572
  46.9 14.7 %collective-permute-start.2 = (bf16[256,768]{1,0:T(8,128)(2,1)}, bf16[256,768]{1,0:T(8,128)(2,1)}, u32[]{:S(2)}, u32[]{:S(2)}) collective-permute-start(bf16[256,768]{1,0:T(8,128)(2,1)} %collective-permute-done.1.refs_2_), channel_id=1, source_target_pairs={{0,8},{8,0},{16,24},{24,16},{1,9},{9,1},{17,25},{25,17},{2,10},{10... | collective-permute-start | bytes 1179656 | tf_op jit(solution)/shard_map/ppermute | solution.py:572
  47.8 29.5 %collective-permute-start.12 = (bf16[256,768]{1,0:T(8,128)(2,1)}, bf16[256,768]{1,0:T(8,128)(2,1)}, u32[]{:S(2)}, u32[]{:S(2)}) collective-permute-start(bf16[256,768]{1,0:T(8,128)(2,1)} %collective-permute-done.11.refs_2_), channel_id=1, source_target_pairs={{0,8},{8,0},{16,24},{24,16},{1,9},{9,1},{17,25},{25,17},{2,10},{10... | collective-permute-start | bytes 1179656 | tf_op jit(solution)/shard_map/ppermute | solution.py:572
  49.4 45.4 %collective-permute-start.13 = (bf16[256,768]{1,0:T(8,128)(2,1)S(1)}, bf16[256,768]{1,0:T(8,128)(2,1)S(1)}, u32[]{:S(2)}, u32[]{:S(2)}) collective-permute-start(bf16[256,768]{1,0:T(8,128)(2,1)S(1)} %get-tuple-element.123.refs_0_), channel_id=1, source_target_pairs={{0,8},{8,0},{16,24},{24,16},{1,9},{9,1},{17,25},{25,17},{2,10},{10... | collective-permute-start | bytes 1179656 | tf_op jit(solution)/shard_map/ppermute | solution.py:572
  57.7 37.2 %collective-permute-start.15 = (bf16[256,768]{1,0:T(8,128)(2,1)S(1)}, bf16[256,768]{1,0:T(8,128)(2,1)}, u32[]{:S(2)}, u32[]{:S(2)}) collective-permute-start(bf16[256,768]{1,0:T(8,128)(2,1)S(1)} %collective-permute-done.14.refs_2_), channel_id=1, source_target_pairs={{0,8},{8,0},{16,24},{24,16},{1,9},{9,1},{17,25},{25,17},{2,10},{10... | collective-permute-start | bytes 1179656 | tf_op jit(solution)/shard_map/ppermute | solution.py:572
  77.3 17.7 %collective-permute-start.16 = (bf16[256,192]{1,0:T(8,128)(2,1)}, bf16[256,192]{1,0:T(8,128)(2,1)S(1)}, u32[]{:S(2)}, u32[]{:S(2)}) collective-permute-start(bf16[256,192]{1,0:T(8,128)(2,1)} %get-tuple-element.120), channel_id=1, source_target_pairs={{0,8},{8,0},{16,24},{24,16},{1,9},{9,1},{17,25},{25,17},{2,10},{10... | collective-permute-start | bytes 294920 | tf_op jit(solution)/shard_map/ppermute | solution.py:572
  77.3 17.6 %collective-permute-start.17 = (bf16[256,192]{1,0:T(8,128)(2,1)}, bf16[256,192]{1,0:T(8,128)(2,1)S(1)}, u32[]{:S(2)}, u32[]{:S(2)}) collective-permute-start(bf16[256,192]{1,0:T(8,128)(2,1)} %get-tuple-element.121), channel_id=1, source_target_pairs={{0,16},{8,24},{16,0},{24,8},{1,17},{9,25},{17,1},{25,9},{2,18},{10... | collective-permute-start | bytes 294920 | tf_op jit(solution)/shard_map/ppermute | solution.py:572
  77.4 17.5 %collective-permute-start.18 = (bf16[256,192]{1,0:T(8,128)(2,1)}, bf16[256,192]{1,0:T(8,128)(2,1)S(1)}, u32[]{:S(2)}, u32[]{:S(2)}) collective-permute-start(bf16[256,192]{1,0:T(8,128)(2,1)} %get-tuple-element.122), channel_id=1, source_target_pairs={{0,24},{8,16},{16,8},{24,0},{1,25},{9,17},{17,9},{25,1},{2,26},{10... | collective-permute-start | bytes 294920 | tf_op jit(solution)/shard_map/ppermute | solution.py:572
  105.0 17.5 %collective-permute-start.19 = (bf16[8,432,768]{2,1,0:T(8,128)(2,1)}, bf16[8,432,768]{2,1,0:T(8,128)(2,1)}, u32[]{:S(2)}, u32[]{:S(2)}) collective-permute-start(bf16[8,432,768]{2,1,0:T(8,128)(2,1)} %bitcast.161), channel_id=1, source_target_pairs={{0,8},{8,0},{16,24},{24,16},{1,9},{9,1},{17,25},{25,17},{2,10},{10... | collective-permute-start | bytes 15925256 | tf_op jit(solution)/shard_map/ppermute | solution.py:572
  105.1 9.1 %collective-permute-start.20 = (bf16[256,192]{1,0:T(8,128)(2,1)S(1)}, bf16[256,192]{1,0:T(8,128)(2,1)S(1)}, u32[]{:S(2)}, u32[]{:S(2)}) collective-permute-start(bf16[256,192]{1,0:T(8,128)(2,1)S(1)} %copy-done.61), channel_id=1, source_target_pairs={{0,8},{8,0},{16,24},{24,16},{1,9},{9,1},{17,25},{25,17},{2,10},{10... | collective-permute-start | bytes 294920 | tf_op jit(solution)/shard_map/ppermute | solution.py:572
  105.6 8.7 %collective-permute-start.21 = (bf16[256,192]{1,0:T(8,128)(2,1)S(1)}, bf16[256,192]{1,0:T(8,128)(2,1)S(1)}, u32[]{:S(2)}, u32[]{:S(2)}) collective-permute-start(bf16[256,192]{1,0:T(8,128)(2,1)S(1)} %copy-done.56), channel_id=1, source_target_pairs={{0,16},{8,24},{16,0},{24,8},{1,17},{9,25},{17,1},{25,9},{2,18},{10... | collective-permute-start | bytes 294920 | tf_op jit(solution)/shard_map/ppermute | solution.py:572
  108.6 8.0 %collective-permute-start.22 = (bf16[256,192]{1,0:T(8,128)(2,1)S(1)}, bf16[256,192]{1,0:T(8,128)(2,1)S(1)}, u32[]{:S(2)}, u32[]{:S(2)}) collective-permute-start(bf16[256,192]{1,0:T(8,128)(2,1)S(1)} %copy-done.50), channel_id=1, source_target_pairs={{0,24},{8,16},{16,8},{24,0},{1,25},{9,17},{17,9},{25,1},{2,26},{10... | collective-permute-start | bytes 294920 | tf_op jit(solution)/shard_map/ppermute | solution.py:572
  114.3 8.2 %collective-permute-start.25 = (bf16[256,192]{1,0:T(8,128)(2,1)}, bf16[256,192]{1,0:T(8,128)(2,1)S(1)}, u32[]{:S(2)}, u32[]{:S(2)}) collective-permute-start(bf16[256,192]{1,0:T(8,128)(2,1)} %get-tuple-element.136), channel_id=1, source_target_pairs={{0,24},{8,16},{16,8},{24,0},{1,25},{9,17},{17,9},{25,1},{2,26},{10... | collective-permute-start | bytes 294920 | tf_op jit(solution)/shard_map/ppermute | solution.py:572
  194.3 8.8 %collective-permute-start.29 = (bf16[8,432,768]{2,1,0:T(8,128)(2,1)S(1)}, bf16[8,432,768]{2,1,0:T(8,128)(2,1)S(1)}, u32[]{:S(2)}, u32[]{:S(2)}) collective-permute-start(bf16[8,432,768]{2,1,0:T(8,128)(2,1)S(1)} %pad_maximum_fusion), channel_id=1, source_target_pairs={{0,8},{8,0},{16,24},{24,16},{1,9},{9,1},{17,25},{25,17},{2,10},{10... | collective-permute-start | bytes 15925256 | tf_op jit(solution)/shard_map/ppermute | solution.py:572
  194.7 11.9 %collective-permute-start.26 = (bf16[256,192]{1,0:T(8,128)(2,1)S(1)}, bf16[256,192]{1,0:T(8,128)(2,1)S(1)}, u32[]{:S(2)}, u32[]{:S(2)}) collective-permute-start(bf16[256,192]{1,0:T(8,128)(2,1)S(1)} %copy-done.59), channel_id=1, source_target_pairs={{0,8},{8,0},{16,24},{24,16},{1,9},{9,1},{17,25},{25,17},{2,10},{10... | collective-permute-start | bytes 294920 | tf_op jit(solution)/shard_map/ppermute | solution.py:572
  194.9 11.8 %collective-permute-start.27 = (bf16[256,192]{1,0:T(8,128)(2,1)S(1)}, bf16[256,192]{1,0:T(8,128)(2,1)S(1)}, u32[]{:S(2)}, u32[]{:S(2)}) collective-permute-start(bf16[256,192]{1,0:T(8,128)(2,1)S(1)} %copy-done.58), channel_id=1, source_target_pairs={{0,16},{8,24},{16,0},{24,8},{1,17},{9,25},{17,1},{25,9},{2,18},{10... | collective-permute-start | bytes 294920 | tf_op jit(solution)/shard_map/ppermute | solution.py:572
  194.9 11.8 %collective-permute-start.28 = (bf16[256,192]{1,0:T(8,128)(2,1)S(1)}, bf16[256,192]{1,0:T(8,128)(2,1)S(1)}, u32[]{:S(2)}, u32[]{:S(2)}) collective-permute-start(bf16[256,192]{1,0:T(8,128)(2,1)S(1)} %copy-done.55), channel_id=1, source_target_pairs={{0,24},{8,16},{16,8},{24,0},{1,25},{9,17},{17,9},{25,1},{2,26},{10... | collective-permute-start | bytes 294920 | tf_op jit(solution)/shard_map/ppermute | solution.py:572
  208.9 24.1 %collective-permute-start.33 = (bf16[256,192]{1,0:T(8,128)(2,1)S(1)}, bf16[256,192]{1,0:T(8,128)(2,1)S(1)}, u32[]{:S(2)}, u32[]{:S(2)}) collective-permute-start(bf16[256,192]{1,0:T(8,128)(2,1)S(1)} %copy-done.41), channel_id=1, source_target_pairs={{0,8},{8,0},{16,24},{24,16},{1,9},{9,1},{17,25},{25,17},{2,10},{10... | collective-permute-start | bytes 294920 | tf_op jit(solution)/shard_map/ppermute | solution.py:572
  209.0 26.0 %collective-permute-start.34 = (bf16[256,192]{1,0:T(8,128)(2,1)S(1)}, bf16[256,192]{1,0:T(8,128)(2,1)S(1)}, u32[]{:S(2)}, u32[]{:S(2)}) collective-permute-start(bf16[256,192]{1,0:T(8,128)(2,1)S(1)} %copy-done.40), channel_id=1, source_target_pairs={{0,16},{8,24},{16,0},{24,8},{1,17},{9,25},{17,1},{25,9},{2,18},{10... | collective-permute-start | bytes 294920 | tf_op jit(solution)/shard_map/ppermute | solution.py:572
  209.1 26.0 %collective-permute-start.35 = (bf16[256,192]{1,0:T(8,128)(2,1)S(1)}, bf16[256,192]{1,0:T(8,128)(2,1)S(1)}, u32[]{:S(2)}, u32[]{:S(2)}) collective-permute-start(bf16[256,192]{1,0:T(8,128)(2,1)S(1)} %copy-done.39), channel_id=1, source_target_pairs={{0,24},{8,16},{16,8},{24,0},{1,25},{9,17},{17,9},{25,1},{2,26},{10... | collective-permute-start | bytes 294920 | tf_op jit(solution)/shard_map/ppermute | solution.py:572
  211.1 49.9 %collective-permute-start.39 = (bf16[256,192]{1,0:T(8,128)(2,1)S(1)}, bf16[256,192]{1,0:T(8,128)(2,1)S(1)}, u32[]{:S(2)}, u32[]{:S(2)}) collective-permute-start(bf16[256,192]{1,0:T(8,128)(2,1)S(1)} %copy-done.38), channel_id=1, source_target_pairs={{0,8},{8,0},{16,24},{24,16},{1,9},{9,1},{17,25},{25,17},{2,10},{10... | collective-permute-start | bytes 294920 | tf_op jit(solution)/shard_map/ppermute | solution.py:572
  211.1 50.0 %collective-permute-start.40 = (bf16[256,192]{1,0:T(8,128)(2,1)S(1)}, bf16[256,192]{1,0:T(8,128)(2,1)S(1)}, u32[]{:S(2)}, u32[]{:S(2)}) collective-permute-start(bf16[256,192]{1,0:T(8,128)(2,1)S(1)} %copy-done.37), channel_id=1, source_target_pairs={{0,16},{8,24},{16,0},{24,8},{1,17},{9,25},{17,1},{25,9},{2,18},{10... | collective-permute-start | bytes 294920 | tf_op jit(solution)/shard_map/ppermute | solution.py:572
  233.1 28.5 %collective-permute-start.41 = (bf16[256,192]{1,0:T(8,128)(2,1)S(1)}, bf16[256,192]{1,0:T(8,128)(2,1)S(1)}, u32[]{:S(2)}, u32[]{:S(2)}) collective-permute-start(bf16[256,192]{1,0:T(8,128)(2,1)S(1)} %copy-done.36), channel_id=1, source_target_pairs={{0,24},{8,16},{16,8},{24,0},{1,25},{9,17},{17,9},{25,1},{2,26},{10... | collective-permute-start | bytes 294920 | tf_op jit(solution)/shard_map/ppermute | solution.py:572
  235.1 26.4 %collective-permute-start.30 = (bf16[256,768]{1,0:T(8,128)(2,1)}, bf16[256,768]{1,0:T(8,128)(2,1)S(1)}, u32[]{:S(2)}, u32[]{:S(2)}) collective-permute-start(bf16[256,768]{1,0:T(8,128)(2,1)} %get-tuple-element.158), channel_id=1, source_target_pairs={{0,8},{8,0},{16,24},{24,16},{1,9},{9,1},{17,25},{25,17},{2,10},{10... | collective-permute-start | bytes 1179656 | tf_op jit(solution)/shard_map/ppermute | solution.py:572
  235.2 26.4 %collective-permute-start.31 = (bf16[256,768]{1,0:T(8,128)(2,1)}, bf16[256,768]{1,0:T(8,128)(2,1)S(1)}, u32[]{:S(2)}, u32[]{:S(2)}) collective-permute-start(bf16[256,768]{1,0:T(8,128)(2,1)} %get-tuple-element.160), channel_id=1, source_target_pairs={{0,8},{8,0},{16,24},{24,16},{1,9},{9,1},{17,25},{25,17},{2,10},{10... | collective-permute-start | bytes 1179656 | tf_op jit(solution)/shard_map/ppermute | solution.py:572
  261.0 49.2 %collective-permute-start.37 = (bf16[256,768]{1,0:T(8,128)(2,1)}, bf16[256,768]{1,0:T(8,128)(2,1)S(1)}, u32[]{:S(2)}, u32[]{:S(2)}) collective-permute-start(bf16[256,768]{1,0:T(8,128)(2,1)} %get-tuple-element.177), channel_id=1, source_target_pairs={{0,8},{8,0},{16,24},{24,16},{1,9},{9,1},{17,25},{25,17},{2,10},{10... | collective-permute-start | bytes 1179656 | tf_op jit(solution)/shard_map/ppermute | solution.py:572
  261.0 57.5 %collective-permute-start.36 = (bf16[256,768]{1,0:T(8,128)(2,1)}, bf16[256,768]{1,0:T(8,128)(2,1)}, u32[]{:S(2)}, u32[]{:S(2)}) collective-permute-start(bf16[256,768]{1,0:T(8,128)(2,1)} %get-tuple-element.175), channel_id=1, source_target_pairs={{0,8},{8,0},{16,24},{24,16},{1,9},{9,1},{17,25},{25,17},{2,10},{10... | collective-permute-start | bytes 1179656 | tf_op jit(solution)/shard_map/ppermute | solution.py:572
  276.2 28.3 %all-to-all-start.1 = ((f32[8,32,96]{2,1,0:T(8,128)}), f32[8,32,96]{2,1,0:T(8,128)S(1)}, u32[]{:S(2)}, u32[]{:S(2)}) async-start(f32[8,32,96]{2,1,0:T(8,128)} %pad.9.clone), calls=%async_computation.2 | async-start | bytes 262144 | tf_op jit(solution)/shard_map/all_to_all | solution.py:597
  300.6 16.6 %collective-permute-start.32 = (bf16[256,768]{1,0:T(8,128)(2,1)}, bf16[256,768]{1,0:T(8,128)(2,1)}, u32[]{:S(2)}, u32[]{:S(2)}) collective-permute-start(bf16[256,768]{1,0:T(8,128)(2,1)} %add_convert_fusion.3), channel_id=1, source_target_pairs={{0,16},{8,24},{16,0},{24,8},{1,17},{9,25},{17,1},{25,9},{2,18},{10... | collective-permute-start | bytes 1179656 | tf_op jit(solution)/shard_map/ppermute | solution.py:572
  304.5 32.4 %all-to-all-start = ((bf16[8,96,576]{2,1,0:T(8,128)(2,1)}), bf16[8,96,576]{2,1,0:T(8,128)(2,1)}, u32[]{:S(2)}, u32[]{:S(2)}) async-start(bf16[8,96,576]{2,1,0:T(8,128)(2,1)} %bitcast.50), calls=%async_computation | async-start | bytes 1966080 | tf_op jit(solution)/shard_map/all_to_all | solution.py:597
  311.3 10.7 %collective-permute-start.38 = (bf16[256,768]{1,0:T(8,128)(2,1)S(1)}, bf16[256,768]{1,0:T(8,128)(2,1)}, u32[]{:S(2)}, u32[]{:S(2)}) collective-permute-start(bf16[256,768]{1,0:T(8,128)(2,1)S(1)} %add_convert_fusion.2), channel_id=1, source_target_pairs={{0,16},{8,24},{16,0},{24,8},{1,17},{9,25},{17,1},{25,9},{2,18},{10... | collective-permute-start | bytes 1179656 | tf_op jit(solution)/shard_map/ppermute | solution.py:572
  313.8 9.4 %collective-permute-start.42 = (bf16[256,768]{1,0:T(8,128)(2,1)}, bf16[256,768]{1,0:T(8,128)(2,1)}, u32[]{:S(2)}, u32[]{:S(2)}) collective-permute-start(bf16[256,768]{1,0:T(8,128)(2,1)} %get-tuple-element.192), channel_id=1, source_target_pairs={{0,8},{8,0},{16,24},{24,16},{1,9},{9,1},{17,25},{25,17},{2,10},{10... | collective-permute-start | bytes 1179656 | tf_op jit(solution)/shard_map/ppermute | solution.py:572
  316.4 14.0 %collective-permute-start.44 = (bf16[256,768]{1,0:T(8,128)(2,1)S(1)}, bf16[256,768]{1,0:T(8,128)(2,1)S(1)}, u32[]{:S(2)}, u32[]{:S(2)}) collective-permute-start(bf16[256,768]{1,0:T(8,128)(2,1)S(1)} %add_convert_fusion.1), channel_id=1, source_target_pairs={{0,16},{8,24},{16,0},{24,8},{1,17},{9,25},{17,1},{25,9},{2,18},{10... | collective-permute-start | bytes 1179656 | tf_op jit(solution)/shard_map/ppermute | solution.py:572
  338.9 16.2 %collective-permute-start.48 = (bf16[432,768]{1,0:T(8,128)(2,1)}, bf16[432,768]{1,0:T(8,128)(2,1)S(1)}, u32[]{:S(2)}, u32[]{:S(2)}) collective-permute-start(bf16[432,768]{1,0:T(8,128)(2,1)} %reduce-scatter.2.cloned.1.call-done), channel_id=1, source_target_pairs={{0,16},{8,24},{16,0},{24,8},{1,17},{9,25},{17,1},{25,9},{2,18},{10... | collective-permute-start | bytes 1990664 | tf_op jit(solution)/shard_map/ppermute | solution.py:572
  340.7 19.9 %collective-permute-start.45 = (bf16[96,576]{1,0:T(8,128)(2,1)S(1)}, bf16[96,576]{1,0:T(8,128)(2,1)S(1)}, u32[]{:S(2)}, u32[]{:S(2)}) collective-permute-start(bf16[96,576]{1,0:T(8,128)(2,1)S(1)} %copy-done.9), channel_id=1, source_target_pairs={{0,8},{8,0},{16,24},{24,16},{1,9},{9,1},{17,25},{25,17},{2,10},{10... | collective-permute-start | bytes 331784 | tf_op jit(solution)/shard_map/ppermute | solution.py:572
  341.7 18.9 %collective-permute-start.46 = (bf16[96,576]{1,0:T(8,128)(2,1)S(1)}, bf16[96,576]{1,0:T(8,128)(2,1)S(1)}, u32[]{:S(2)}, u32[]{:S(2)}) collective-permute-start(bf16[96,576]{1,0:T(8,128)(2,1)S(1)} %copy-done.9), channel_id=1, source_target_pairs={{0,16},{8,24},{16,0},{24,8},{1,17},{9,25},{17,1},{25,9},{2,18},{10... | collective-permute-start | bytes 331784 | tf_op jit(solution)/shard_map/ppermute | solution.py:572
  342.0 18.9 %collective-permute-start.47 = (bf16[96,576]{1,0:T(8,128)(2,1)S(1)}, bf16[96,576]{1,0:T(8,128)(2,1)S(1)}, u32[]{:S(2)}, u32[]{:S(2)}) collective-permute-start(bf16[96,576]{1,0:T(8,128)(2,1)S(1)} %copy-done.9), channel_id=1, source_target_pairs={{0,24},{8,16},{16,8},{24,0},{1,25},{9,17},{17,9},{25,1},{2,26},{10... | collective-permute-start | bytes 331784 | tf_op jit(solution)/shard_map/ppermute | solution.py:572
  (84 other events, 487.1 us)
Sparse Core Ops, SparseCore 0:
  11.2 90.2 all-gather.2
  206.9 110.5 reduce-scatter.1

commit v2 on v1

--- a/solution.py
+++ b/solution.py
@@ -9,6 +9,7 @@
 
 
 HD = 64
+SHORTEST = 512
 eps = 1e-05
 F32 = jnp.float32
 BF16 = jnp.bfloat16
@@ -111,7 +112,7 @@
         lax.fori_loop(0, heads * parts, step, 0)
 
     blocks = (live + rows - 1) // rows
-    for count in range(1, parts + 1):
+    for count in range(max(1, SHORTEST // rows), parts + 1):
         pl.when(blocks == count)(functools.partial(variant, count))
     for j in range(parts):
         stacked = jnp.concatenate([ot[h * parts + j] for h in range(heads)], axis=0)
@@ -210,7 +211,7 @@
         lax.fori_loop(0, heads * parts, step, 0)
 
     blocks = (live + rows - 1) // rows
-    for count in range(1, parts + 1):
+    for count in range(max(1, SHORTEST // rows), parts + 1):
         pl.when(blocks == count)(functools.partial(variant, count))
     shift_sum, gain_sum, col_sum = 0.0, 0.0, 0.0
     for j in range(parts):
@@ -593,8 +594,23 @@
     return whole
 
 
-def sum_blocks(blocks, axis, kind):
-    blocks = lax.all_to_all(blocks.astype(kind), axis, split_axis=0, concat_axis=0, tiled=True)
+def sum_blocks(blocks, small, axis):
+    count, mine = lax.axis_size(axis), lax.axis_index(axis) % 2
+    sums = []
+    for values, kind in ((blocks, BF16), (small, F32)):
+        pairs = values.reshape((count // 2, 2) + values.shape[1:])
+        sent = swap(pick(pairs, 1 - mine, 1).astype(kind), axis, 1)
+        sums.append((pick(pairs, mine, 1) + sent.astype(F32)).astype(BF16))
+    sums[1] = jnp.pad(sums[1], ((0, 0), (0, 0), (0, blocks.shape[2] - small.shape[2])))
+    groups = [list(range(g, count, 2)) for g in range(2)]
+    blocks = lax.all_to_all(
+        jnp.concatenate(sums, axis=1),
+        axis,
+        split_axis=0,
+        concat_axis=0,
+        axis_index_groups=groups,
+        tiled=True,
+    )
     return jnp.sum(blocks.astype(F32), axis=0)
 
 
@@ -622,6 +638,18 @@
     ff_half = half_ff * owners
     quarter = own_ff // own_rows
 
+    fc1_half = lax.dynamic_slice(w_fc1, (0, core * ff_half), (own_rows, ff_half))
+    columns = range(0, ff_half, width)
+    rest = jnp.concatenate(
+        [pick(w_out.reshape(2, half_rows, width), core, 0)]
+        + [fc1_half[:, c : c + width] for c in columns]
+        + [pick(w_fc2.reshape(2, half_ff, width), core, 0)],
+        axis=0,
+    )
+    rest_rows = rest.shape[0]
+    w_qkv = after(w_qkv, rest)
+    rest = lax.all_gather(rest, "fsdp", axis=0, tiled=False)
+
     own_w = pick(w_qkv.reshape(own_rows, 3, parts, span), s, 2).reshape(own_rows, 3 * span)
     ff_small = jnp.concatenate([ff_gain[:, None], ff_biases], axis=1).T.reshape(
         3 * quarter, own_rows
@@ -637,18 +665,6 @@
     d_small = small[:, :10].transpose(1, 0, 2).reshape(10, width)
     gains, biases = d_small[:3], d_small[3:]
     ff_small = small[:, 10:].reshape(owners, 3, own_ff).transpose(1, 0, 2).reshape(3, 2 * ff_half)
-
-    w_out, w_fc1, w_fc2 = after((w_out, w_fc1, w_fc2), block)
-    fc1_half = lax.dynamic_slice(w_fc1, (0, core * ff_half), (own_rows, ff_half))
-    columns = range(0, ff_half, width)
-    rest = jnp.concatenate(
-        [pick(w_out.reshape(2, half_rows, width), core, 0)]
-        + [fc1_half[:, c : c + width] for c in columns]
-        + [pick(w_fc2.reshape(2, half_ff, width), core, 0)],
-        axis=0,
-    )
-    rest_rows = rest.shape[0]
-    rest = lax.all_gather(rest, "fsdp", axis=0, tiled=False)
 
     qkv_bias = pick(
         jnp.stack([biases[1], jnp.zeros_like(biases[1]), biases[2]]).reshape(3, parts, span), s, 1
@@ -726,8 +742,9 @@
         ]
         pieces.append(pick(grad_fc2, turn, 1))
         grads.append(jnp.concatenate([p.astype(BF16) for p in pieces], axis=1))
-    rest_sum = grads[1].astype(F32) + swap(grads[0], "seq", 1).astype(F32)
-    rest_sum = rest_sum.astype(BF16).reshape(owners * rest_rows, width)
+    other_grads = swap(grads[0], "seq", 1)
+    rest_sum = (grads[1].astype(F32) + other_grads.astype(F32)).astype(BF16)
+    rest_sum = rest_sum.reshape(owners * rest_rows, width)
     mixed_grads[0], rest_sum = lax.optimization_barrier((mixed_grads[0], rest_sum))
     rest_sum = lax.psum_scatter(rest_sum, "fsdp", scatter_dimension=0, tiled=True)
 
@@ -779,13 +796,16 @@
         axis=1,
     )
     small_blocks = jnp.pad(small_blocks, ((0, 0), (0, small_rows - kinds), (0, 0)))
-    small_sum = sum_blocks(small_blocks, "fsdp", F32)
-    own_sum = sum_blocks(grad_own.reshape(owners, own_rows, 3 * span), "fsdp", BF16).astype(BF16)
-    rest_sum = after(rest_sum, own_sum)
-    rest_sum = rest_sum.astype(F32) + swap(rest_sum, "seq", 2).astype(F32)
+    own_sum = sum_blocks(
+        grad_own.reshape(owners, own_rows, 3 * span), small_blocks, "fsdp"
+    )
+    small_sum = own_sum[own_rows:, :own_rows]
+    own_sum = own_sum[:own_rows].astype(BF16)
+    across = swap(rest_sum, "seq", 2)
     small_sum = [small_sum] + [swap(small_sum, "seq", j) for j in range(1, parts)]
     small_sum = (small_sum[0] + small_sum[1]) + (small_sum[2] + small_sum[3])
     feed_sum = small_sum[10:kinds].reshape(3, own_ff)
+    small_outs = (small_sum[:3].T, small_sum[3:10].T, feed_sum[0], feed_sum[1:].T)
     group = jnp.stack([own_sum] + [swap(own_sum, "seq", j) for j in range(1, parts)])
     w_qkv_grad = jnp.concatenate(
         [
@@ -796,6 +816,8 @@
         axis=1,
     ).astype(F32)
 
+    across = after(across, [w_qkv_grad, small_outs, input_grad])
+    rest_sum = rest_sum.astype(F32) + across.astype(F32)
     other_sum = swap(rest_sum, "seq", 1)
     pair = [
         jnp.where(core == 0, rest_sum, other_sum),
@@ -818,10 +840,7 @@
         w_out_grad,
         w_fc1_grad,
         w_fc2_grad,
-        small_sum[:3].T,
-        small_sum[3:10].T,
-        feed_sum[0],
-        feed_sum[1:].T,
+        *small_outs,
     )
 
 

time: 382 us -> 401 us (1.050)
  the two profiles are of different devices: /device:TPU:1 before, /device:TPU:0 now
where the time goes in v2:
time: 401 us; the launch traced here: 393 us
  Pallas kernels  151 us (38%)
  waiting for transfers between devices  97.3 us (24%)
  starting transfers between devices  49.7 us (12%)
  local copies, waits for them, and re-layouts  33.7 us (8%)
  other arithmetic  25.7 us (6%)
  matrix products  19.7 us (5%)
  between operations  15.9 us (4%)
    ppermute x55, waiting for transfers between devices, swap(): return lax.ppermute(values, axis, [(i, i ^ mask) for i in range(count)])  87.9 us
    pallas_call x1, Pallas kernels, token_stage(): pl.pallas_call(functools.partial(token_kernel, plan, seqs, parts), grid=(...  57.3 us
    pallas_call x3, Pallas kernels, attend_backward(): pl.pallas_call(functools.partial(attend_back_kernel, parts, heads, rows),...  53.6 us
    pallas_call x3, Pallas kernels, attend_forward(): pl.pallas_call(functools.partial(attend_kernel, parts, heads, rows), grid...  40.4 us
    ppermute x55, starting transfers between devices, swap(): return lax.ppermute(values, axis, [(i, i ^ mask) for i in range(count)])  39.1 us
    dot_general x8, matrix products, mm_tn(): lax.dot_general(left, right, (((0,), (0,)), ((), ())), preferred_element_...  18.6 us
    all_to_all x1, starting transfers between devices, sum_blocks(): lax.all_to_all(jnp.concatenate(sums, axis=1), axis, split_axis=0, concat_...  10.5 us
    all_to_all x1, waiting for transfers between devices, sum_blocks(): lax.all_to_all(jnp.concatenate(sums, axis=1), axis, split_axis=0, concat_...  9.35 us
  transfers between devices with their start and end apart: 58, of which 17 were waited for; matrix products, arithmetic and copies ran while one was open for 13% of the time, Pallas kernels for 24%

profile of v2, /device:TPU:0, one launch (start us, length us, event | category | flops | bytes accessed | tf_op | source)
XLA Modules:
  0.0 393.4 jit_solution(17234833682484081227)
XLA Ops:
  12.7 4.1 %collective-permute-start.3 = (bf16[128,576]{0,1:T(8,128)(2,1)S(1)}, bf16[128,576]{0,1:T(8,128)(2,1)S(1)}, u32[]{:S(2)}, u32[]{:S(2)}) collective-permute-start(bf16[128,576]{0,1:T(8,128)(2,1)S(1)} %fusion.29), channel_id=1, source_target_pairs={{0,4},{1,5},{2,6},{3,7},{4,0},{5,1},{6,2},{7,3},{8,12},{9,13},{10,... | collective-permute-start | bytes 442376 | tf_op jit(solution)/shard_map/ppermute | solution.py:573
  16.8 1.6 collective-permute-start.4
  18.4 1.5 collective-permute-start.6
  20.0 1.6 collective-permute-start.1
  22.6 1.9 pad_add_fusion.2
  24.5 1.3 pad_add_fusion.1.info
  28.3 13.2 %collective-permute-done.5 = bf16[128,576]{0,1:T(8,128)(2,1)} collective-permute-done((bf16[128,576]{0,1:T(8,128)(2,1)S(1)}, bf16[128,576]{0,1:T(8,128)(2,1)}, u32[]{:S(2)}, u32[]{:S(2)}) %collective-permute-start.5) | collective-permute-done | bytes 147488 | tf_op jit(solution)/shard_map/ppermute | solution.py:573
  43.7 1.3 collective-permute-start.9
  45.0 3.3 collective-permute-done.8
  51.6 8.5 %collective-permute-done.14.refs_2_ = bf16[256,768]{1,0:T(8,128)(2,1)S(1)} collective-permute-done((bf16[256,768]{1,0:T(8,128)(2,1)S(1)}, bf16[256,768]{1,0:T(8,128)(2,1)S(1)}, u32[]{:S(2)}, u32[]{:S(2)}) %collective-permute-start.14) | collective-permute-done | bytes 393248 | tf_op jit(solution)/shard_map/ppermute | solution.py:573
  63.1 15.6 %attend_forward.3 = (bf16[4,256,768]{2,1,0:T(8,128)(2,1)}, bf16[3,1024,64]{2,1,0:T(8,128)(2,1)}, bf16[3,1024,64]{2,1,0:T(8,128)(2,1)}, bf16[3,1024,64]{2,1,0:T(8...) custom-call(s32[2]{0:T(128)} %pad_add_fusion.1.info, ...), custom_call_target="tpu_custom_call" | custom-call | flops 1711276032 | bytes 6389760 | tf_op jit(solution)/shard_map/attend_forward/pallas_call | solution.py:135
  80.8 15.5 %attend_forward.4 = (bf16[4,256,768]{2,1,0:T(8,128)(2,1)}, bf16[3,1024,64]{2,1,0:T(8,128)(2,1)}, bf16[3,1024,64]{2,1,0:T(8,128)(2,1)}, bf16[3,1024,64]{2,1,0:T(8...) custom-call(s32[2]{0:T(128)} %get-tuple-element.283.info, ...), custom_call_target="tpu_custom_call" | custom-call | flops 1711276032 | bytes 6389760 | tf_op jit(solution)/shard_map/attend_forward/pallas_call | solution.py:135
  97.1 9.3 %attend_forward.5 = (bf16[4,256,768]{2,1,0:T(8,128)(2,1)}, bf16[3,1024,64]{2,1,0:T(8,128)(2,1)}, bf16[3,1024,64]{2,1,0:T(8,128)(2,1)}, bf16[3,1024,64]{2,1,0:T(8...) custom-call(s32[2]{0:T(128)} %get-tuple-element.284.info, ...), custom_call_target="tpu_custom_call" | custom-call | flops 1711276032 | bytes 6389760 | tf_op jit(solution)/shard_map/attend_forward/pallas_call | solution.py:135
  112.4 3.5 collective-permute-done.20.refs_7_
  118.3 4.2 %collective-permute-done.24.refs_12_ = bf16[256,192]{1,0:T(8,128)(2,1)S(1)} collective-permute-done((bf16[256,192]{1,0:T(8,128)(2,1)}, bf16[256,192]{1,0:T(8,128)(2,1)S(1)}, u32[]{:S(2)}, u32[]{:S(2)}) %collective-permute-start.24) | collective-permute-done | bytes 98336 | tf_op jit(solution)/shard_map/ppermute | solution.py:573
  122.5 1.6 collective-permute-done.25.refs_13_
  124.8 57.3 %token_stage.1 = (bf16[3,256,768]{2,1,0:T(8,128)(2,1)}, f32[3,256,768]{2,1,0:T(8,128)}, bf16[768,768]{1,0:T(8,128)(2,1)}, bf16[768,768]{1,0:T(8,128)(2,1)}, bf16...) custom-call(s32[5]{0:T(128)} %pad_add_fusion.info, ...), custom_call_target="tpu_custom_call" | custom-call | flops 16307453952 | bytes 43646976 | tf_op jit(solution)/shard_map/token_stage/pallas_call | solution.py:511
  182.1 1.7 copy.138
  183.8 2.5 convolution_convert_fusion.1
  190.8 4.2 %fusion.41 = bf16[3072,768]{1,0:T(8,128)(2,1)S(1)} fusion(bf16[768,3072]{1,0:T(8,128)(2,1)S(1)} %bitcast.179, bf16[768,768]{1,0:T(8,128)(2,1)S(1)} %copy-done.73), kind=kOutput, calls=%fused_computation.148 | convolution fusion | flops 3623878656 | bytes 10616832 | tf_op jit(solution)/shard_map/dot_general | solution.py:28
  200.4 4.3 %collective-permute-done.29 = bf16[8,432,768]{2,1,0:T(8,128)(2,1)S(1)} collective-permute-done((bf16[8,432,768]{2,1,0:T(8,128)(2,1)S(1)}, bf16[8,432,768]{2,1,0:T(8,128)(2,1)S(1)}, u32[]{:S(2)}, u32[]{:S(2)}) %collective-permute-start.29) | collective-permute-done | bytes 5308448 | tf_op jit(solution)/shard_map/ppermute | solution.py:573
  204.8 3.6 add_convert_fusion
  214.6 21.1 %attend_backward.3 = (bf16[4,256,576]{2,1,0:T(8,128)(2,1)}, bf16[256,768]{1,0:T(8,128)(2,1)}, bf16[256,768]{1,0:T(8,128)(2,1)}, bf16[256,768]{1,0:T(8,128)(2,1)}...) custom-call(s32[2]{0:T(128)} %pad_add_fusion.1.info, bf16[256,768]{1,0:T(8,128)(2,1)} %copy-done.13, ...), custom_call_target="tpu_custom_call" | custom-call | flops 2919235584 | bytes 9142272 | tf_op jit(solution)/shard_map/attend_backward/pallas_call | solution.py:245
  237.3 21.1 %attend_backward.4 = (bf16[4,256,576]{2,1,0:T(8,128)(2,1)}, bf16[256,768]{1,0:T(8,128)(2,1)}, bf16[256,768]{1,0:T(8,128)(2,1)}, bf16[256,768]{1,0:T(8,128)(2,1)}...) custom-call(s32[2]{0:T(128)} %get-tuple-element.283.info, bf16[256,768]{1,0:T(8,128)(2,1)} %copy-done.12, ...), custom_call_target="tpu_custom_call" | custom-call | flops 2919235584 | bytes 9142272 | tf_op jit(solution)/shard_map/attend_backward/pallas_call | solution.py:245
  258.4 4.2 %fusion.42 = f32[768,576,1]{0,1,2:T(8,128)} fusion(bf16[4,256,768]{2,1,0:T(8,128)(2,1)} %get-tuple-element.193, bf16[4,256,576]{2,1,0:T(8,128)(2,1)} %get-tuple-element.194), kind=kOutput, calls=%fused_computation.149 | convolution fusion | flops 905969664 | bytes 4521984 | tf_op jit(solution)/shard_map/dot_general | solution.py:28
  263.9 11.5 %attend_backward.5 = (bf16[4,256,576]{2,1,0:T(8,128)(2,1)}, bf16[256,768]{1,0:T(8,128)(2,1)}, bf16[256,768]{1,0:T(8,128)(2,1)}, bf16[256,768]{1,0:T(8,128)(2,1)}...) custom-call(s32[2]{0:T(128)} %get-tuple-element.284.info, bf16[256,768]{1,0:T(8,128)(2,1)} %copy-done.11, ...), custom_call_target="tpu_custom_call" | custom-call | flops 2919235584 | bytes 9142272 | tf_op jit(solution)/shard_map/attend_backward/pallas_call | solution.py:245
  275.4 3.1 fusion.43
  278.5 1.3 bitcast_add_fusion
  279.9 1.9 copy.143
  281.8 2.2 fusion.27
  284.6 2.1 collective-permute-start.46
  289.0 16.7 %collective-permute-done.46 = f32[4,32,96]{2,1,0:T(8,128)S(1)} collective-permute-done((f32[4,32,96]{2,1,0:T(8,128)S(1)}, f32[4,32,96]{2,1,0:T(8,128)S(1)}, u32[]{:S(2)}, u32[]{:S(2)}) %collective-permute-start.46) | collective-permute-done | bytes 49184 | tf_op jit(solution)/shard_map/ppermute | solution.py:573
  307.2 1.5 collective-permute-start.44
  308.9 8.8 %collective-permute-done.38 = bf16[256,768]{1,0:T(8,128)(2,1)S(1)} collective-permute-done((bf16[256,768]{1,0:T(8,128)(2,1)S(1)}, bf16[256,768]{1,0:T(8,128)(2,1)S(1)}, u32[]{:S(2)}, u32[]{:S(2)}) %collective-permute-start.38) | collective-permute-done | bytes 393248 | tf_op jit(solution)/shard_map/ppermute | solution.py:573
  318.8 1.1 fusion.22
  320.9 2.1 copy.146
  323.0 10.5 %all-to-all-start = ((bf16[4,128,576]{1,2,0:T(8,128)(2,1)}), bf16[4,128,576]{1,2,0:T(8,128)(2,1)S(1)}, u32[]{:S(2)}, u32[]{:S(2)}) async-start(bf16[4,128,576]{1,2,0:T(8,128)(2,1)} %copy.146), calls=%async_computation | async-start | bytes 1179648 | tf_op jit(solution)/shard_map/all_to_all | solution.py:606
  333.5 1.4 add_bitcast_fusion
  336.6 1.9 fusion.7
  338.5 9.3 %all-to-all-done = bf16[4,128,576]{1,2,0:T(8,128)(2,1)S(1)} async-done(((bf16[4,128,576]{1,2,0:T(8,128)(2,1)}), bf16[4,128,576]{1,2,0:T(8,128)(2,1)S(1)}, u32[]{:S(2)}, u32[]{:S(2)}) %all-to-all-start) | async-done | bytes 589856 | tf_op jit(solution)/shard_map/all_to_all | solution.py:606
  348.0 1.7 collective-permute-start.52
  350.3 1.6 collective-permute-start.48
  352.2 1.2 collective-permute-done.53
  355.2 2.0 collective-permute-done.48
  357.2 2.5 collective-permute-done.49
  362.9 15.0 %collective-permute-done.50 = bf16[432,768]{1,0:T(8,128)(2,1)S(1)} collective-permute-done((bf16[432,768]{1,0:T(8,128)(2,1)}, bf16[432,768]{1,0:T(8,128)(2,1)S(1)}, u32[]{:S(2)}, u32[]{:S(2)}) %collective-permute-start.50) | collective-permute-done | bytes 663584 | tf_op jit(solution)/shard_map/ppermute | solution.py:573
  379.5 1.9 collective-permute-done.54
  381.3 1.6 broadcast_select_fusion.1
  (395 shorter events, 66.6 us)
Async XLA Ops:
  7.2 99.2 %all-gather.3.cloned.1.call-start = ((), (), s32[]{:S(2)}) async-start(), calls=%async_computation.3 | async-start | bytes 5971968 | tf_op jit(solution)/shard_map/all_gather | solution.py:651
  11.2 349.5 %reduce-scatter.2.cloned.1.call-start = ((), (), s32[]{:S(2)}) async-start(), calls=%async_computation.2 | async-start | bytes 5971968 | tf_op jit(solution)/shard_map/reduce_scatter | solution.py:749
  12.7 13.2 %collective-permute-start.3 = (bf16[128,576]{0,1:T(8,128)(2,1)S(1)}, bf16[128,576]{0,1:T(8,128)(2,1)S(1)}, u32[]{:S(2)}, u32[]{:S(2)}) collective-permute-start(bf16[128,576]{0,1:T(8,128)(2,1)S(1)} %fusion.29), channel_id=1, source_target_pairs={{0,4},{1,5},{2,6},{3,7},{4,0},{5,1},{6,2},{7,3},{8,12},{9,13},{10,... | collective-permute-start | bytes 442376 | tf_op jit(solution)/shard_map/ppermute | solution.py:573
  16.8 9.8 %collective-permute-start.4 = (bf16[128,576]{0,1:T(8,128)(2,1)S(1)}, bf16[128,576]{0,1:T(8,128)(2,1)S(1)}, u32[]{:S(2)}, u32[]{:S(2)}) collective-permute-start(bf16[128,576]{0,1:T(8,128)(2,1)S(1)} %fusion.29), channel_id=1, source_target_pairs={{0,2},{1,3},{2,0},{3,1},{4,6},{5,7},{6,4},{7,5},{8,10},{9,11},{10,... | collective-permute-start | bytes 442376 | tf_op jit(solution)/shard_map/ppermute | solution.py:573
  18.4 9.0 %collective-permute-start.6 = (bf16[128,576]{0,1:T(8,128)(2,1)S(1)}, bf16[128,576]{0,1:T(8,128)(2,1)S(1)}, u32[]{:S(2)}, u32[]{:S(2)}) collective-permute-start(bf16[128,576]{0,1:T(8,128)(2,1)S(1)} %fusion.29), channel_id=1, source_target_pairs={{0,1},{1,0},{2,3},{3,2},{4,5},{5,4},{6,7},{7,6},{8,9},{9,8},{10,11... | collective-permute-start | bytes 442376 | tf_op jit(solution)/shard_map/ppermute | solution.py:573
  20.0 28.4 %collective-permute-start.1 = (bf16[256,768]{1,0:T(8,128)(2,1)S(1)}, bf16[256,768]{1,0:T(8,128)(2,1)}, u32[]{:S(2)}, u32[]{:S(2)}) collective-permute-start(bf16[256,768]{1,0:T(8,128)(2,1)S(1)} %get-tuple-element.258.refs_0_), channel_id=1, source_target_pairs={{0,16},{8,24},{16,0},{24,8},{1,17},{9,25},{17,1},{25,9},{2,18},{10... | collective-permute-start | bytes 1179656 | tf_op jit(solution)/shard_map/ppermute | solution.py:573
  21.6 29.4 %collective-permute-start = (bf16[256,768]{1,0:T(8,128)(2,1)S(1)}, bf16[256,768]{1,0:T(8,128)(2,1)}, u32[]{:S(2)}, u32[]{:S(2)}) collective-permute-start(bf16[256,768]{1,0:T(8,128)(2,1)S(1)} %get-tuple-element.258.refs_0_), channel_id=1, source_target_pairs={{0,8},{8,0},{16,24},{24,16},{1,9},{9,1},{17,25},{25,17},{2,10},{10... | collective-permute-start | bytes 1179656 | tf_op jit(solution)/shard_map/ppermute | solution.py:573
  26.1 15.5 %collective-permute-start.5 = (bf16[128,576]{0,1:T(8,128)(2,1)S(1)}, bf16[128,576]{0,1:T(8,128)(2,1)}, u32[]{:S(2)}, u32[]{:S(2)}) collective-permute-start(bf16[128,576]{0,1:T(8,128)(2,1)S(1)} %collective-permute-done.3), channel_id=1, source_target_pairs={{0,2},{1,3},{2,0},{3,1},{4,6},{5,7},{6,4},{7,5},{8,10},{9,11},{10,... | collective-permute-start | bytes 442376 | tf_op jit(solution)/shard_map/ppermute | solution.py:573
  26.6 22.7 %collective-permute-start.11 = (bf16[256,768]{1,0:T(8,128)(2,1)S(1)}, bf16[256,768]{1,0:T(8,128)(2,1)}, u32[]{:S(2)}, u32[]{:S(2)}) collective-permute-start(bf16[256,768]{1,0:T(8,128)(2,1)S(1)} %get-tuple-element.110.refs_0_), channel_id=1, source_target_pairs={{0,16},{8,24},{16,0},{24,8},{1,17},{9,25},{17,1},{25,9},{2,18},{10... | collective-permute-start | bytes 1179656 | tf_op jit(solution)/shard_map/ppermute | solution.py:573
  27.5 16.0 %collective-permute-start.7 = (bf16[128,576]{0,1:T(8,128)(2,1)S(1)}, bf16[128,576]{0,1:T(8,128)(2,1)S(1)}, u32[]{:S(2)}, u32[]{:S(2)}) collective-permute-start(bf16[128,576]{0,1:T(8,128)(2,1)S(1)} %collective-permute-done.3), channel_id=1, source_target_pairs={{0,1},{1,0},{2,3},{3,2},{4,5},{5,4},{6,7},{7,6},{8,9},{9,8},{10,11... | collective-permute-start | bytes 442376 | tf_op jit(solution)/shard_map/ppermute | solution.py:573
  48.2 30.6 %collective-permute-start.10 = (bf16[256,768]{1,0:T(8,128)(2,1)S(1)}, bf16[256,768]{1,0:T(8,128)(2,1)}, u32[]{:S(2)}, u32[]{:S(2)}) collective-permute-start(bf16[256,768]{1,0:T(8,128)(2,1)S(1)} %get-tuple-element.110.refs_0_), channel_id=1, source_target_pairs={{0,8},{8,0},{16,24},{24,16},{1,9},{9,1},{17,25},{25,17},{2,10},{10... | collective-permute-start | bytes 1179656 | tf_op jit(solution)/shard_map/ppermute | solution.py:573
  48.4 11.6 %collective-permute-start.14 = (bf16[256,768]{1,0:T(8,128)(2,1)S(1)}, bf16[256,768]{1,0:T(8,128)(2,1)S(1)}, u32[]{:S(2)}, u32[]{:S(2)}) collective-permute-start(bf16[256,768]{1,0:T(8,128)(2,1)S(1)} %get-tuple-element.119.refs_0_), channel_id=1, source_target_pairs={{0,16},{8,24},{16,0},{24,8},{1,17},{9,25},{17,1},{25,9},{2,18},{10... | collective-permute-start | bytes 1179656 | tf_op jit(solution)/shard_map/ppermute | solution.py:573
  49.3 13.8 %collective-permute-start.2 = (bf16[256,768]{1,0:T(8,128)(2,1)}, bf16[256,768]{1,0:T(8,128)(2,1)}, u32[]{:S(2)}, u32[]{:S(2)}) collective-permute-start(bf16[256,768]{1,0:T(8,128)(2,1)} %collective-permute-done.1.refs_2_), channel_id=1, source_target_pairs={{0,8},{8,0},{16,24},{24,16},{1,9},{9,1},{17,25},{25,17},{2,10},{10... | collective-permute-start | bytes 1179656 | tf_op jit(solution)/shard_map/ppermute | solution.py:573
  50.5 28.3 %collective-permute-start.12 = (bf16[256,768]{1,0:T(8,128)(2,1)}, bf16[256,768]{1,0:T(8,128)(2,1)}, u32[]{:S(2)}, u32[]{:S(2)}) collective-permute-start(bf16[256,768]{1,0:T(8,128)(2,1)} %collective-permute-done.11.refs_2_), channel_id=1, source_target_pairs={{0,8},{8,0},{16,24},{24,16},{1,9},{9,1},{17,25},{25,17},{2,10},{10... | collective-permute-start | bytes 1179656 | tf_op jit(solution)/shard_map/ppermute | solution.py:573
  51.0 45.3 %collective-permute-start.13 = (bf16[256,768]{1,0:T(8,128)(2,1)S(1)}, bf16[256,768]{1,0:T(8,128)(2,1)S(1)}, u32[]{:S(2)}, u32[]{:S(2)}) collective-permute-start(bf16[256,768]{1,0:T(8,128)(2,1)S(1)} %get-tuple-element.119.refs_0_), channel_id=1, source_target_pairs={{0,8},{8,0},{16,24},{24,16},{1,9},{9,1},{17,25},{25,17},{2,10},{10... | collective-permute-start | bytes 1179656 | tf_op jit(solution)/shard_map/ppermute | solution.py:573
  60.0 36.3 %collective-permute-start.15 = (bf16[256,768]{1,0:T(8,128)(2,1)S(1)}, bf16[256,768]{1,0:T(8,128)(2,1)}, u32[]{:S(2)}, u32[]{:S(2)}) collective-permute-start(bf16[256,768]{1,0:T(8,128)(2,1)S(1)} %collective-permute-done.14.refs_2_), channel_id=1, source_target_pairs={{0,8},{8,0},{16,24},{24,16},{1,9},{9,1},{17,25},{25,17},{2,10},{10... | collective-permute-start | bytes 1179656 | tf_op jit(solution)/shard_map/ppermute | solution.py:573
  78.8 17.5 %collective-permute-start.16 = (bf16[256,192]{1,0:T(8,128)(2,1)}, bf16[256,192]{1,0:T(8,128)(2,1)S(1)}, u32[]{:S(2)}, u32[]{:S(2)}) collective-permute-start(bf16[256,192]{1,0:T(8,128)(2,1)} %get-tuple-element.116), channel_id=1, source_target_pairs={{0,8},{8,0},{16,24},{24,16},{1,9},{9,1},{17,25},{25,17},{2,10},{10... | collective-permute-start | bytes 294920 | tf_op jit(solution)/shard_map/ppermute | solution.py:573
  79.4 17.0 %collective-permute-start.17 = (bf16[256,192]{1,0:T(8,128)(2,1)}, bf16[256,192]{1,0:T(8,128)(2,1)S(1)}, u32[]{:S(2)}, u32[]{:S(2)}) collective-permute-start(bf16[256,192]{1,0:T(8,128)(2,1)} %get-tuple-element.117), channel_id=1, source_target_pairs={{0,16},{8,24},{16,0},{24,8},{1,17},{9,25},{17,1},{25,9},{2,18},{10... | collective-permute-start | bytes 294920 | tf_op jit(solution)/shard_map/ppermute | solution.py:573
  80.2 16.2 %collective-permute-start.18 = (bf16[256,192]{1,0:T(8,128)(2,1)}, bf16[256,192]{1,0:T(8,128)(2,1)S(1)}, u32[]{:S(2)}, u32[]{:S(2)}) collective-permute-start(bf16[256,192]{1,0:T(8,128)(2,1)} %get-tuple-element.118), channel_id=1, source_target_pairs={{0,24},{8,16},{16,8},{24,0},{1,25},{9,17},{17,9},{25,1},{2,26},{10... | collective-permute-start | bytes 294920 | tf_op jit(solution)/shard_map/ppermute | solution.py:573
  106.4 17.7 %collective-permute-start.19 = (bf16[8,432,768]{2,1,0:T(8,128)(2,1)}, bf16[8,432,768]{2,1,0:T(8,128)(2,1)}, u32[]{:S(2)}, u32[]{:S(2)}) collective-permute-start(bf16[8,432,768]{2,1,0:T(8,128)(2,1)} %bitcast.176), channel_id=1, source_target_pairs={{0,8},{8,0},{16,24},{24,16},{1,9},{9,1},{17,25},{25,17},{2,10},{10... | collective-permute-start | bytes 15925256 | tf_op jit(solution)/shard_map/ppermute | solution.py:573
  107.1 8.8 %collective-permute-start.20 = (bf16[256,192]{1,0:T(8,128)(2,1)S(1)}, bf16[256,192]{1,0:T(8,128)(2,1)S(1)}, u32[]{:S(2)}, u32[]{:S(2)}) collective-permute-start(bf16[256,192]{1,0:T(8,128)(2,1)S(1)} %copy-done.65), channel_id=1, source_target_pairs={{0,8},{8,0},{16,24},{24,16},{1,9},{9,1},{17,25},{25,17},{2,10},{10... | collective-permute-start | bytes 294920 | tf_op jit(solution)/shard_map/ppermute | solution.py:573
  107.2 9.5 %collective-permute-start.21 = (bf16[256,192]{1,0:T(8,128)(2,1)S(1)}, bf16[256,192]{1,0:T(8,128)(2,1)S(1)}, u32[]{:S(2)}, u32[]{:S(2)}) collective-permute-start(bf16[256,192]{1,0:T(8,128)(2,1)S(1)} %copy-done.60), channel_id=1, source_target_pairs={{0,16},{8,24},{16,0},{24,8},{1,17},{9,25},{17,1},{25,9},{2,18},{10... | collective-permute-start | bytes 294920 | tf_op jit(solution)/shard_map/ppermute | solution.py:573
  111.0 7.2 %collective-permute-start.22 = (bf16[256,192]{1,0:T(8,128)(2,1)S(1)}, bf16[256,192]{1,0:T(8,128)(2,1)S(1)}, u32[]{:S(2)}, u32[]{:S(2)}) collective-permute-start(bf16[256,192]{1,0:T(8,128)(2,1)S(1)} %copy-done.54), channel_id=1, source_target_pairs={{0,24},{8,16},{16,8},{24,0},{1,25},{9,17},{17,9},{25,1},{2,26},{10... | collective-permute-start | bytes 294920 | tf_op jit(solution)/shard_map/ppermute | solution.py:573
  116.7 7.4 %collective-permute-start.25 = (bf16[256,192]{1,0:T(8,128)(2,1)}, bf16[256,192]{1,0:T(8,128)(2,1)S(1)}, u32[]{:S(2)}, u32[]{:S(2)}) collective-permute-start(bf16[256,192]{1,0:T(8,128)(2,1)} %get-tuple-element.132), channel_id=1, source_target_pairs={{0,24},{8,16},{16,8},{24,0},{1,25},{9,17},{17,9},{25,1},{2,26},{10... | collective-permute-start | bytes 294920 | tf_op jit(solution)/shard_map/ppermute | solution.py:573
  195.9 8.9 %collective-permute-start.29 = (bf16[8,432,768]{2,1,0:T(8,128)(2,1)S(1)}, bf16[8,432,768]{2,1,0:T(8,128)(2,1)S(1)}, u32[]{:S(2)}, u32[]{:S(2)}) collective-permute-start(bf16[8,432,768]{2,1,0:T(8,128)(2,1)S(1)} %pad_maximum_fusion), channel_id=1, source_target_pairs={{0,8},{8,0},{16,24},{24,16},{1,9},{9,1},{17,25},{25,17},{2,10},{10... | collective-permute-start | bytes 15925256 | tf_op jit(solution)/shard_map/ppermute | solution.py:573
  196.4 12.0 %collective-permute-start.26 = (bf16[256,192]{1,0:T(8,128)(2,1)S(1)}, bf16[256,192]{1,0:T(8,128)(2,1)S(1)}, u32[]{:S(2)}, u32[]{:S(2)}) collective-permute-start(bf16[256,192]{1,0:T(8,128)(2,1)S(1)} %copy-done.63), channel_id=1, source_target_pairs={{0,8},{8,0},{16,24},{24,16},{1,9},{9,1},{17,25},{25,17},{2,10},{10... | collective-permute-start | bytes 294920 | tf_op jit(solution)/shard_map/ppermute | solution.py:573
  196.8 11.6 %collective-permute-start.27 = (bf16[256,192]{1,0:T(8,128)(2,1)S(1)}, bf16[256,192]{1,0:T(8,128)(2,1)S(1)}, u32[]{:S(2)}, u32[]{:S(2)}) collective-permute-start(bf16[256,192]{1,0:T(8,128)(2,1)S(1)} %copy-done.62), channel_id=1, source_target_pairs={{0,16},{8,24},{16,0},{24,8},{1,17},{9,25},{17,1},{25,9},{2,18},{10... | collective-permute-start | bytes 294920 | tf_op jit(solution)/shard_map/ppermute | solution.py:573
  197.6 10.8 %collective-permute-start.28 = (bf16[256,192]{1,0:T(8,128)(2,1)S(1)}, bf16[256,192]{1,0:T(8,128)(2,1)S(1)}, u32[]{:S(2)}, u32[]{:S(2)}) collective-permute-start(bf16[256,192]{1,0:T(8,128)(2,1)S(1)} %copy-done.59), channel_id=1, source_target_pairs={{0,24},{8,16},{16,8},{24,0},{1,25},{9,17},{17,9},{25,1},{2,26},{10... | collective-permute-start | bytes 294920 | tf_op jit(solution)/shard_map/ppermute | solution.py:573
  210.6 25.2 %collective-permute-start.33 = (bf16[256,192]{1,0:T(8,128)(2,1)S(1)}, bf16[256,192]{1,0:T(8,128)(2,1)S(1)}, u32[]{:S(2)}, u32[]{:S(2)}) collective-permute-start(bf16[256,192]{1,0:T(8,128)(2,1)S(1)} %copy-done.45), channel_id=1, source_target_pairs={{0,8},{8,0},{16,24},{24,16},{1,9},{9,1},{17,25},{25,17},{2,10},{10... | collective-permute-start | bytes 294920 | tf_op jit(solution)/shard_map/ppermute | solution.py:573
  211.0 25.5 %collective-permute-start.34 = (bf16[256,192]{1,0:T(8,128)(2,1)S(1)}, bf16[256,192]{1,0:T(8,128)(2,1)S(1)}, u32[]{:S(2)}, u32[]{:S(2)}) collective-permute-start(bf16[256,192]{1,0:T(8,128)(2,1)S(1)} %copy-done.44), channel_id=1, source_target_pairs={{0,16},{8,24},{16,0},{24,8},{1,17},{9,25},{17,1},{25,9},{2,18},{10... | collective-permute-start | bytes 294920 | tf_op jit(solution)/shard_map/ppermute | solution.py:573
  211.8 24.6 %collective-permute-start.35 = (bf16[256,192]{1,0:T(8,128)(2,1)S(1)}, bf16[256,192]{1,0:T(8,128)(2,1)S(1)}, u32[]{:S(2)}, u32[]{:S(2)}) collective-permute-start(bf16[256,192]{1,0:T(8,128)(2,1)S(1)} %copy-done.43), channel_id=1, source_target_pairs={{0,24},{8,16},{16,8},{24,0},{1,25},{9,17},{17,9},{25,1},{2,26},{10... | collective-permute-start | bytes 294920 | tf_op jit(solution)/shard_map/ppermute | solution.py:573
  212.5 50.1 %collective-permute-start.39 = (bf16[256,192]{1,0:T(8,128)(2,1)S(1)}, bf16[256,192]{1,0:T(8,128)(2,1)S(1)}, u32[]{:S(2)}, u32[]{:S(2)}) collective-permute-start(bf16[256,192]{1,0:T(8,128)(2,1)S(1)} %copy-done.42), channel_id=1, source_target_pairs={{0,8},{8,0},{16,24},{24,16},{1,9},{9,1},{17,25},{25,17},{2,10},{10... | collective-permute-start | bytes 294920 | tf_op jit(solution)/shard_map/ppermute | solution.py:573
  213.1 50.0 %collective-permute-start.40 = (bf16[256,192]{1,0:T(8,128)(2,1)S(1)}, bf16[256,192]{1,0:T(8,128)(2,1)S(1)}, u32[]{:S(2)}, u32[]{:S(2)}) collective-permute-start(bf16[256,192]{1,0:T(8,128)(2,1)S(1)} %copy-done.41), channel_id=1, source_target_pairs={{0,16},{8,24},{16,0},{24,8},{1,17},{9,25},{17,1},{25,9},{2,18},{10... | collective-permute-start | bytes 294920 | tf_op jit(solution)/shard_map/ppermute | solution.py:573
  235.8 27.5 %collective-permute-start.41 = (bf16[256,192]{1,0:T(8,128)(2,1)S(1)}, bf16[256,192]{1,0:T(8,128)(2,1)S(1)}, u32[]{:S(2)}, u32[]{:S(2)}) collective-permute-start(bf16[256,192]{1,0:T(8,128)(2,1)S(1)} %copy-done.40), channel_id=1, source_target_pairs={{0,24},{8,16},{16,8},{24,0},{1,25},{9,17},{17,9},{25,1},{2,26},{10... | collective-permute-start | bytes 294920 | tf_op jit(solution)/shard_map/ppermute | solution.py:573
  236.4 26.8 %collective-permute-start.30 = (bf16[256,768]{1,0:T(8,128)(2,1)}, bf16[256,768]{1,0:T(8,128)(2,1)S(1)}, u32[]{:S(2)}, u32[]{:S(2)}) collective-permute-start(bf16[256,768]{1,0:T(8,128)(2,1)} %get-tuple-element.154), channel_id=1, source_target_pairs={{0,8},{8,0},{16,24},{24,16},{1,9},{9,1},{17,25},{25,17},{2,10},{10... | collective-permute-start | bytes 1179656 | tf_op jit(solution)/shard_map/ppermute | solution.py:573
  237.2 26.0 %collective-permute-start.31 = (bf16[256,768]{1,0:T(8,128)(2,1)}, bf16[256,768]{1,0:T(8,128)(2,1)S(1)}, u32[]{:S(2)}, u32[]{:S(2)}) collective-permute-start(bf16[256,768]{1,0:T(8,128)(2,1)} %get-tuple-element.156), channel_id=1, source_target_pairs={{0,8},{8,0},{16,24},{24,16},{1,9},{9,1},{17,25},{25,17},{2,10},{10... | collective-permute-start | bytes 1179656 | tf_op jit(solution)/shard_map/ppermute | solution.py:573
  262.6 25.3 %collective-permute-start.37 = (bf16[256,768]{1,0:T(8,128)(2,1)}, bf16[256,768]{1,0:T(8,128)(2,1)}, u32[]{:S(2)}, u32[]{:S(2)}) collective-permute-start(bf16[256,768]{1,0:T(8,128)(2,1)} %get-tuple-element.173), channel_id=1, source_target_pairs={{0,8},{8,0},{16,24},{24,16},{1,9},{9,1},{17,25},{25,17},{2,10},{10... | collective-permute-start | bytes 1179656 | tf_op jit(solution)/shard_map/ppermute | solution.py:573
  263.1 45.7 %collective-permute-start.36 = (bf16[256,768]{1,0:T(8,128)(2,1)}, bf16[256,768]{1,0:T(8,128)(2,1)}, u32[]{:S(2)}, u32[]{:S(2)}) collective-permute-start(bf16[256,768]{1,0:T(8,128)(2,1)} %get-tuple-element.171), channel_id=1, source_target_pairs={{0,8},{8,0},{16,24},{24,16},{1,9},{9,1},{17,25},{25,17},{2,10},{10... | collective-permute-start | bytes 1179656 | tf_op jit(solution)/shard_map/ppermute | solution.py:573
  284.0 34.9 %collective-permute-start.45 = (bf16[4,96,576]{2,1,0:T(8,128)(2,1)}, bf16[4,96,576]{2,1,0:T(8,128)(2,1)}, u32[]{:S(2)}, u32[]{:S(2)}) collective-permute-start(bf16[4,96,576]{2,1,0:T(8,128)(2,1)} %fusion.27), channel_id=1, source_target_pairs={{0,1},{1,0},{2,3},{3,2},{4,5},{5,4},{6,7},{7,6},{8,9},{9,8},{10,11... | collective-permute-start | bytes 1327112 | tf_op jit(solution)/shard_map/ppermute | solution.py:573
  284.6 21.1 %collective-permute-start.46 = (f32[4,32,96]{2,1,0:T(8,128)S(1)}, f32[4,32,96]{2,1,0:T(8,128)S(1)}, u32[]{:S(2)}, u32[]{:S(2)}) collective-permute-start(f32[4,32,96]{2,1,0:T(8,128)S(1)} %dynamic-slice_bitcast_fusion.2), channel_id=1, source_target_pairs={{0,1},{1,0},{2,3},{3,2},{4,5},{5,4},{6,7},{7,6},{8,9},{9,8},{10,11... | collective-permute-start | bytes 147464 | tf_op jit(solution)/shard_map/ppermute | solution.py:573
  286.8 20.3 %collective-permute-start.32 = (bf16[256,768]{1,0:T(8,128)(2,1)S(1)}, bf16[256,768]{1,0:T(8,128)(2,1)S(1)}, u32[]{:S(2)}, u32[]{:S(2)}) collective-permute-start(bf16[256,768]{1,0:T(8,128)(2,1)S(1)} %add_convert_fusion.3), channel_id=1, source_target_pairs={{0,16},{8,24},{16,0},{24,8},{1,17},{9,25},{17,1},{25,9},{2,18},{10... | collective-permute-start | bytes 1179656 | tf_op jit(solution)/shard_map/ppermute | solution.py:573
  287.9 18.3 %collective-permute-start.43 = (bf16[256,768]{1,0:T(8,128)(2,1)S(1)}, bf16[256,768]{1,0:T(8,128)(2,1)S(1)}, u32[]{:S(2)}, u32[]{:S(2)}) collective-permute-start(bf16[256,768]{1,0:T(8,128)(2,1)S(1)} %copy-done.39), channel_id=1, source_target_pairs={{0,8},{8,0},{16,24},{24,16},{1,9},{9,1},{17,25},{25,17},{2,10},{10... | collective-permute-start | bytes 1179656 | tf_op jit(solution)/shard_map/ppermute | solution.py:573
  305.7 12.0 %collective-permute-start.38 = (bf16[256,768]{1,0:T(8,128)(2,1)S(1)}, bf16[256,768]{1,0:T(8,128)(2,1)S(1)}, u32[]{:S(2)}, u32[]{:S(2)}) collective-permute-start(bf16[256,768]{1,0:T(8,128)(2,1)S(1)} %add_convert_fusion.2), channel_id=1, source_target_pairs={{0,16},{8,24},{16,0},{24,8},{1,17},{9,25},{17,1},{25,9},{2,18},{10... | collective-permute-start | bytes 1179656 | tf_op jit(solution)/shard_map/ppermute | solution.py:573
  306.2 27.3 %collective-permute-start.42 = (bf16[256,768]{1,0:T(8,128)(2,1)}, bf16[256,768]{1,0:T(8,128)(2,1)}, u32[]{:S(2)}, u32[]{:S(2)}) collective-permute-start(bf16[256,768]{1,0:T(8,128)(2,1)} %get-tuple-element.188), channel_id=1, source_target_pairs={{0,8},{8,0},{16,24},{24,16},{1,9},{9,1},{17,25},{25,17},{2,10},{10... | collective-permute-start | bytes 1179656 | tf_op jit(solution)/shard_map/ppermute | solution.py:573
  307.2 26.4 %collective-permute-start.44 = (bf16[256,768]{1,0:T(8,128)(2,1)}, bf16[256,768]{1,0:T(8,128)(2,1)}, u32[]{:S(2)}, u32[]{:S(2)}) collective-permute-start(bf16[256,768]{1,0:T(8,128)(2,1)} %add_convert_fusion.1), channel_id=1, source_target_pairs={{0,16},{8,24},{16,0},{24,8},{1,17},{9,25},{17,1},{25,9},{2,18},{10... | collective-permute-start | bytes 1179656 | tf_op jit(solution)/shard_map/ppermute | solution.py:573
  323.0 24.8 %all-to-all-start = ((bf16[4,128,576]{1,2,0:T(8,128)(2,1)}), bf16[4,128,576]{1,2,0:T(8,128)(2,1)S(1)}, u32[]{:S(2)}, u32[]{:S(2)}) async-start(bf16[4,128,576]{1,2,0:T(8,128)(2,1)} %copy.146), calls=%async_computation | async-start | bytes 1179648 | tf_op jit(solution)/shard_map/all_to_all | solution.py:606
  351.9 7.8 %collective-permute-start.49 = (bf16[96,576]{0,1:T(8,128)(2,1)S(1)}, bf16[96,576]{0,1:T(8,128)(2,1)S(1)}, u32[]{:S(2)}, u32[]{:S(2)}) collective-permute-start(bf16[96,576]{0,1:T(8,128)(2,1)S(1)} %slice.394), channel_id=1, source_target_pairs={{0,24},{8,16},{16,8},{24,0},{1,25},{9,17},{17,9},{25,1},{2,26},{10... | collective-permute-start | bytes 331784 | tf_op jit(solution)/shard_map/ppermute | solution.py:573
  360.6 17.2 %collective-permute-start.50 = (bf16[432,768]{1,0:T(8,128)(2,1)}, bf16[432,768]{1,0:T(8,128)(2,1)S(1)}, u32[]{:S(2)}, u32[]{:S(2)}) collective-permute-start(bf16[432,768]{1,0:T(8,128)(2,1)} %reduce-scatter.2.cloned.1.call-done), channel_id=1, source_target_pairs={{0,16},{8,24},{16,0},{24,8},{1,17},{9,25},{17,1},{25,9},{2,18},{10... | collective-permute-start | bytes 1990664 | tf_op jit(solution)/shard_map/ppermute | solution.py:573
  (86 other events, 520.7 us)
Sparse Core Ops, SparseCore 0:
  11.3 92.5 all-gather.2
  208.5 108.6 reduce-scatter.1

commit v3 on v2

--- a/solution.py
+++ b/solution.py
@@ -802,11 +802,12 @@
     small_sum = own_sum[own_rows:, :own_rows]
     own_sum = own_sum[:own_rows].astype(BF16)
     across = swap(rest_sum, "seq", 2)
-    small_sum = [small_sum] + [swap(small_sum, "seq", j) for j in range(1, parts)]
-    small_sum = (small_sum[0] + small_sum[1]) + (small_sum[2] + small_sum[3])
+    small_sum = small_sum + swap(small_sum, "seq", 1)
+    small_sum = small_sum + swap(small_sum, "seq", 2)
     feed_sum = small_sum[10:kinds].reshape(3, own_ff)
     small_outs = (small_sum[:3].T, small_sum[3:10].T, feed_sum[0], feed_sum[1:].T)
-    group = jnp.stack([own_sum] + [swap(own_sum, "seq", j) for j in range(1, parts)])
+    group = jnp.stack([own_sum, swap(own_sum, "seq", 2)])
+    group = jnp.stack([group, swap(group, "seq", 1)], axis=1).reshape((parts,) + own_sum.shape)
     w_qkv_grad = jnp.concatenate(
         [
             pick(group, s ^ g, 0)[:, p * span : (p + 1) * span]

time: 401 us -> 401 us (level)
    ppermute x55 -> x53, starting transfers between devices: 39.1 us -> 37.1 us  [swap(): return lax.ppermute(values, axis, [(i, i ^ mask) for i in range(count)])]
    ppermute x55 -> x53, waiting for transfers between devices: 87.9 us -> 87.2 us  [swap(): return lax.ppermute(values, axis, [(i, i ^ mask) for i in range(count)])]
  transfers between devices with their start and end apart: 58 -> 56, of which waited for: 17 -> 16; matrix products, arithmetic and copies ran while one was open for 13% -> 13% of each run, Pallas kernels for 24% -> 24%
where the time goes in v3:
time: 401 us; the launch traced here: 394 us
  Pallas kernels  151 us (38%)
  waiting for transfers between devices  99.7 us (25%)
  starting transfers between devices  48.8 us (12%)
  local copies, waits for them, and re-layouts  30.3 us (8%)
  other arithmetic  27.8 us (7%)
  matrix products  19.7 us (5%)
  between operations  15.9 us (4%)
    ppermute x53, waiting for transfers between devices, swap(): return lax.ppermute(values, axis, [(i, i ^ mask) for i in range(count)])  87.2 us
    pallas_call x1, Pallas kernels, token_stage(): pl.pallas_call(functools.partial(token_kernel, plan, seqs, parts), grid=(...  57.3 us
    pallas_call x3, Pallas kernels, attend_backward(): pl.pallas_call(functools.partial(attend_back_kernel, parts, heads, rows),...  53.6 us
    pallas_call x3, Pallas kernels, attend_forward(): pl.pallas_call(functools.partial(attend_kernel, parts, heads, rows), grid...  40.4 us
    ppermute x53, starting transfers between devices, swap(): return lax.ppermute(values, axis, [(i, i ^ mask) for i in range(count)])  37.1 us
    dot_general x8, matrix products, mm_tn(): lax.dot_general(left, right, (((0,), (0,)), ((), ())), preferred_element_...  18.6 us
    all_to_all x1, waiting for transfers between devices, sum_blocks(): lax.all_to_all(jnp.concatenate(sums, axis=1), axis, split_axis=0, concat_...  12.5 us
    all_to_all x1, starting transfers between devices, sum_blocks(): lax.all_to_all(jnp.concatenate(sums, axis=1), axis, split_axis=0, concat_...  11.6 us
  transfers between devices with their start and end apart: 56, of which 16 were waited for; matrix products, arithmetic and copies ran while one was open for 13% of the time, Pallas kernels for 24%

profile of v3, /device:TPU:0, one launch (start us, length us, event | category | flops | bytes accessed | tf_op | source)
XLA Modules:
  0.0 393.6 jit_solution(5164235972915925207)
XLA Ops:
  12.7 4.1 %collective-permute-start.3 = (bf16[128,576]{0,1:T(8,128)(2,1)S(1)}, bf16[128,576]{0,1:T(8,128)(2,1)S(1)}, u32[]{:S(2)}, u32[]{:S(2)}) collective-permute-start(bf16[128,576]{0,1:T(8,128)(2,1)S(1)} %fusion.29), channel_id=1, source_target_pairs={{0,4},{1,5},{2,6},{3,7},{4,0},{5,1},{6,2},{7,3},{8,12},{9,13},{10,... | collective-permute-start | bytes 442376 | tf_op jit(solution)/shard_map/ppermute | solution.py:573
  16.8 1.6 collective-permute-start.4
  18.4 1.5 collective-permute-start.6
  20.0 1.6 collective-permute-start.1
  22.6 1.9 pad_add_fusion.2
  24.5 1.2 pad_add_fusion.1.info
  28.6 13.3 %collective-permute-done.5 = bf16[128,576]{0,1:T(8,128)(2,1)S(1)} collective-permute-done((bf16[128,576]{0,1:T(8,128)(2,1)S(1)}, bf16[128,576]{0,1:T(8,128)(2,1)S(1)}, u32[]{:S(2)}, u32[]{:S(2)}) %collective-permute-start.5) | collective-permute-done | bytes 147488 | tf_op jit(solution)/shard_map/ppermute | solution.py:573
  42.9 1.6 collective-permute-start.9
  44.5 4.2 %collective-permute-done.8 = bf16[128,576]{0,1:T(8,128)(2,1)S(1)} collective-permute-done((bf16[128,576]{0,1:T(8,128)(2,1)S(1)}, bf16[128,576]{0,1:T(8,128)(2,1)S(1)}, u32[]{:S(2)}, u32[]{:S(2)}) %collective-permute-start.8) | collective-permute-done | bytes 147488 | tf_op jit(solution)/shard_map/ppermute | solution.py:573
  49.7 1.3 collective-permute-done.9
  52.1 8.3 %collective-permute-done.14.refs_2_ = bf16[256,768]{1,0:T(8,128)(2,1)S(1)} collective-permute-done((bf16[256,768]{1,0:T(8,128)(2,1)S(1)}, bf16[256,768]{1,0:T(8,128)(2,1)S(1)}, u32[]{:S(2)}, u32[]{:S(2)}) %collective-permute-start.14) | collective-permute-done | bytes 393248 | tf_op jit(solution)/shard_map/ppermute | solution.py:573
  63.6 15.6 %attend_forward.3 = (bf16[4,256,768]{2,1,0:T(8,128)(2,1)}, bf16[3,1024,64]{2,1,0:T(8,128)(2,1)}, bf16[3,1024,64]{2,1,0:T(8,128)(2,1)}, bf16[3,1024,64]{2,1,0:T(8...) custom-call(s32[2]{0:T(128)} %pad_add_fusion.1.info, ...), custom_call_target="tpu_custom_call" | custom-call | flops 1711276032 | bytes 6389760 | tf_op jit(solution)/shard_map/attend_forward/pallas_call | solution.py:135
  81.3 15.5 %attend_forward.4 = (bf16[4,256,768]{2,1,0:T(8,128)(2,1)}, bf16[3,1024,64]{2,1,0:T(8,128)(2,1)}, bf16[3,1024,64]{2,1,0:T(8,128)(2,1)}, bf16[3,1024,64]{2,1,0:T(8...) custom-call(s32[2]{0:T(128)} %get-tuple-element.285.info, ...), custom_call_target="tpu_custom_call" | custom-call | flops 1711276032 | bytes 6389760 | tf_op jit(solution)/shard_map/attend_forward/pallas_call | solution.py:135
  97.5 9.3 %attend_forward.5 = (bf16[4,256,768]{2,1,0:T(8,128)(2,1)}, bf16[3,1024,64]{2,1,0:T(8,128)(2,1)}, bf16[3,1024,64]{2,1,0:T(8,128)(2,1)}, bf16[3,1024,64]{2,1,0:T(8...) custom-call(s32[2]{0:T(128)} %get-tuple-element.286.info, ...), custom_call_target="tpu_custom_call" | custom-call | flops 1711276032 | bytes 6389760 | tf_op jit(solution)/shard_map/attend_forward/pallas_call | solution.py:135
  111.2 1.3 collective-permute-start.22
  112.9 3.5 collective-permute-done.20.refs_7_
  118.8 4.2 %collective-permute-done.24.refs_12_ = bf16[256,192]{1,0:T(8,128)(2,1)S(1)} collective-permute-done((bf16[256,192]{1,0:T(8,128)(2,1)}, bf16[256,192]{1,0:T(8,128)(2,1)S(1)}, u32[]{:S(2)}, u32[]{:S(2)}) %collective-permute-start.24) | collective-permute-done | bytes 98336 | tf_op jit(solution)/shard_map/ppermute | solution.py:573
  123.0 1.6 collective-permute-done.25.refs_13_
  125.3 57.3 %token_stage.1 = (bf16[3,256,768]{2,1,0:T(8,128)(2,1)}, f32[3,256,768]{2,1,0:T(8,128)}, bf16[768,768]{1,0:T(8,128)(2,1)}, bf16[768,768]{1,0:T(8,128)(2,1)}, bf16...) custom-call(s32[5]{0:T(128)} %pad_add_fusion.info, ...), custom_call_target="tpu_custom_call" | custom-call | flops 16307453952 | bytes 43646976 | tf_op jit(solution)/shard_map/token_stage/pallas_call | solution.py:511
  182.6 1.7 copy.142
  184.4 2.5 convolution_convert_fusion.1
  191.3 4.3 %fusion.42 = bf16[3072,768]{1,0:T(8,128)(2,1)S(1)} fusion(bf16[768,3072]{1,0:T(8,128)(2,1)S(1)} %bitcast.182, bf16[768,768]{1,0:T(8,128)(2,1)S(1)} %copy-done.73), kind=kOutput, calls=%fused_computation.150 | convolution fusion | flops 3623878656 | bytes 10616832 | tf_op jit(solution)/shard_map/dot_general | solution.py:28
  201.0 4.3 %collective-permute-done.29 = bf16[8,432,768]{2,1,0:T(8,128)(2,1)S(1)} collective-permute-done((bf16[8,432,768]{2,1,0:T(8,128)(2,1)S(1)}, bf16[8,432,768]{2,1,0:T(8,128)(2,1)S(1)}, u32[]{:S(2)}, u32[]{:S(2)}) %collective-permute-start.29) | collective-permute-done | bytes 5308448 | tf_op jit(solution)/shard_map/ppermute | solution.py:573
  205.3 3.5 add_convert_fusion
  214.8 21.1 %attend_backward.3 = (bf16[4,256,576]{2,1,0:T(8,128)(2,1)}, bf16[256,768]{1,0:T(8,128)(2,1)}, bf16[256,768]{1,0:T(8,128)(2,1)}, bf16[256,768]{1,0:T(8,128)(2,1)}...) custom-call(s32[2]{0:T(128)} %pad_add_fusion.1.info, bf16[256,768]{1,0:T(8,128)(2,1)} %copy-done.12, ...), custom_call_target="tpu_custom_call" | custom-call | flops 2919235584 | bytes 9142272 | tf_op jit(solution)/shard_map/attend_backward/pallas_call | solution.py:245
  237.8 21.0 %attend_backward.4 = (bf16[4,256,576]{2,1,0:T(8,128)(2,1)}, bf16[256,768]{1,0:T(8,128)(2,1)}, bf16[256,768]{1,0:T(8,128)(2,1)}, bf16[256,768]{1,0:T(8,128)(2,1)}...) custom-call(s32[2]{0:T(128)} %get-tuple-element.285.info, bf16[256,768]{1,0:T(8,128)(2,1)} %copy-done.11, ...), custom_call_target="tpu_custom_call" | custom-call | flops 2919235584 | bytes 9142272 | tf_op jit(solution)/shard_map/attend_backward/pallas_call | solution.py:245
  258.9 4.2 %fusion.43 = f32[768,576,1]{0,1,2:T(8,128)} fusion(bf16[4,256,768]{2,1,0:T(8,128)(2,1)} %get-tuple-element.193, bf16[4,256,576]{2,1,0:T(8,128)(2,1)} %get-tuple-element.194), kind=kOutput, calls=%fused_computation.151 | convolution fusion | flops 905969664 | bytes 4521984 | tf_op jit(solution)/shard_map/dot_general | solution.py:28
  264.3 11.4 %attend_backward.5 = (bf16[4,256,576]{2,1,0:T(8,128)(2,1)}, bf16[256,768]{1,0:T(8,128)(2,1)}, bf16[256,768]{1,0:T(8,128)(2,1)}, bf16[256,768]{1,0:T(8,128)(2,1)}...) custom-call(s32[2]{0:T(128)} %get-tuple-element.286.info, bf16[256,768]{1,0:T(8,128)(2,1)} %copy-done.10, ...), custom_call_target="tpu_custom_call" | custom-call | flops 2919235584 | bytes 9142272 | tf_op jit(solution)/shard_map/attend_backward/pallas_call | solution.py:245
  275.8 3.1 fusion.44
  279.0 1.3 bitcast_add_fusion
  280.3 1.9 copy.147
  282.2 1.4 fusion.27
  284.3 2.0 collective-permute-start.46
  288.3 16.0 %collective-permute-done.46 = f32[4,32,96]{2,1,0:T(8,128)S(1)} collective-permute-done((f32[4,32,96]{2,1,0:T(8,128)S(1)}, f32[4,32,96]{2,1,0:T(8,128)S(1)}, u32[]{:S(2)}, u32[]{:S(2)}) %collective-permute-start.46) | collective-permute-done | bytes 49184 | tf_op jit(solution)/shard_map/ppermute | solution.py:573
  305.3 2.0 collective-permute-start.44
  307.5 8.8 %collective-permute-done.38 = bf16[256,768]{1,0:T(8,128)(2,1)S(1)} collective-permute-done((bf16[256,768]{1,0:T(8,128)(2,1)S(1)}, bf16[256,768]{1,0:T(8,128)(2,1)S(1)}, u32[]{:S(2)}, u32[]{:S(2)}) %collective-permute-start.38) | collective-permute-done | bytes 393248 | tf_op jit(solution)/shard_map/ppermute | solution.py:573
  319.7 11.6 %all-to-all-start = ((bf16[4,128,576]{1,2,0:T(8,128)(2,1)}), bf16[4,128,576]{1,2,0:T(8,128)(2,1)}, u32[]{:S(2)}, u32[]{:S(2)}) async-start(bf16[4,128,576]{1,2,0:T(8,128)(2,1)} %copy.150), calls=%async_computation | async-start | bytes 1179648 | tf_op jit(solution)/shard_map/all_to_all | solution.py:606
  331.3 1.4 add_bitcast_fusion
  334.1 12.5 %all-to-all-done = bf16[4,128,576]{1,2,0:T(8,128)(2,1)} async-done(((bf16[4,128,576]{1,2,0:T(8,128)(2,1)}), bf16[4,128,576]{1,2,0:T(8,128)(2,1)}, u32[]{:S(2)}, u32[]{:S(2)}) %all-to-all-start) | async-done | bytes 589856 | tf_op jit(solution)/shard_map/all_to_all | solution.py:606
  347.9 3.2 fusion.7
  351.2 1.3 collective-permute-start.51
  353.4 2.0 collective-permute-done.51
  357.1 1.5 collective-permute-done.47
  358.7 1.6 collective-permute-done.48
  360.9 1.3 collective-permute-start.49
  363.6 14.5 %collective-permute-done.49 = bf16[432,768]{1,0:T(8,128)(2,1)S(1)} collective-permute-done((bf16[432,768]{1,0:T(8,128)(2,1)}, bf16[432,768]{1,0:T(8,128)(2,1)S(1)}, u32[]{:S(2)}, u32[]{:S(2)}) %collective-permute-start.49) | collective-permute-done | bytes 663584 | tf_op jit(solution)/shard_map/ppermute | solution.py:573
  379.7 1.9 collective-permute-done.52
  381.5 1.6 broadcast_select_fusion.1
  (390 shorter events, 63.8 us)
Async XLA Ops:
  7.2 99.7 %all-gather.3.cloned.1.call-start = ((), (), s32[]{:S(2)}) async-start(), calls=%async_computation.3 | async-start | bytes 5971968 | tf_op jit(solution)/shard_map/all_gather | solution.py:651
  11.2 349.7 %reduce-scatter.2.cloned.1.call-start = ((), (), s32[]{:S(2)}) async-start(), calls=%async_computation.2 | async-start | bytes 5971968 | tf_op jit(solution)/shard_map/reduce_scatter | solution.py:749
  12.7 13.6 %collective-permute-start.3 = (bf16[128,576]{0,1:T(8,128)(2,1)S(1)}, bf16[128,576]{0,1:T(8,128)(2,1)S(1)}, u32[]{:S(2)}, u32[]{:S(2)}) collective-permute-start(bf16[128,576]{0,1:T(8,128)(2,1)S(1)} %fusion.29), channel_id=1, source_target_pairs={{0,4},{1,5},{2,6},{3,7},{4,0},{5,1},{6,2},{7,3},{8,12},{9,13},{10,... | collective-permute-start | bytes 442376 | tf_op jit(solution)/shard_map/ppermute | solution.py:573
  16.8 10.2 %collective-permute-start.4 = (bf16[128,576]{0,1:T(8,128)(2,1)S(1)}, bf16[128,576]{0,1:T(8,128)(2,1)S(1)}, u32[]{:S(2)}, u32[]{:S(2)}) collective-permute-start(bf16[128,576]{0,1:T(8,128)(2,1)S(1)} %fusion.29), channel_id=1, source_target_pairs={{0,2},{1,3},{2,0},{3,1},{4,6},{5,7},{6,4},{7,5},{8,10},{9,11},{10,... | collective-permute-start | bytes 442376 | tf_op jit(solution)/shard_map/ppermute | solution.py:573
  18.4 9.4 %collective-permute-start.6 = (bf16[128,576]{0,1:T(8,128)(2,1)S(1)}, bf16[128,576]{0,1:T(8,128)(2,1)S(1)}, u32[]{:S(2)}, u32[]{:S(2)}) collective-permute-start(bf16[128,576]{0,1:T(8,128)(2,1)S(1)} %fusion.29), channel_id=1, source_target_pairs={{0,1},{1,0},{2,3},{3,2},{4,5},{5,4},{6,7},{7,6},{8,9},{9,8},{10,11... | collective-permute-start | bytes 442376 | tf_op jit(solution)/shard_map/ppermute | solution.py:573
  20.0 28.8 %collective-permute-start.1 = (bf16[256,768]{1,0:T(8,128)(2,1)S(1)}, bf16[256,768]{1,0:T(8,128)(2,1)}, u32[]{:S(2)}, u32[]{:S(2)}) collective-permute-start(bf16[256,768]{1,0:T(8,128)(2,1)S(1)} %get-tuple-element.258.refs_0_), channel_id=1, source_target_pairs={{0,16},{8,24},{16,0},{24,8},{1,17},{9,25},{17,1},{25,9},{2,18},{10... | collective-permute-start | bytes 1179656 | tf_op jit(solution)/shard_map/ppermute | solution.py:573
  21.6 30.0 %collective-permute-start = (bf16[256,768]{1,0:T(8,128)(2,1)S(1)}, bf16[256,768]{1,0:T(8,128)(2,1)}, u32[]{:S(2)}, u32[]{:S(2)}) collective-permute-start(bf16[256,768]{1,0:T(8,128)(2,1)S(1)} %get-tuple-element.258.refs_0_), channel_id=1, source_target_pairs={{0,8},{8,0},{16,24},{24,16},{1,9},{9,1},{17,25},{25,17},{2,10},{10... | collective-permute-start | bytes 1179656 | tf_op jit(solution)/shard_map/ppermute | solution.py:573
  26.5 15.4 %collective-permute-start.5 = (bf16[128,576]{0,1:T(8,128)(2,1)S(1)}, bf16[128,576]{0,1:T(8,128)(2,1)S(1)}, u32[]{:S(2)}, u32[]{:S(2)}) collective-permute-start(bf16[128,576]{0,1:T(8,128)(2,1)S(1)} %collective-permute-done.3), channel_id=1, source_target_pairs={{0,2},{1,3},{2,0},{3,1},{4,6},{5,7},{6,4},{7,5},{8,10},{9,11},{10,... | collective-permute-start | bytes 442376 | tf_op jit(solution)/shard_map/ppermute | solution.py:573
  27.1 22.4 %collective-permute-start.11 = (bf16[256,768]{1,0:T(8,128)(2,1)S(1)}, bf16[256,768]{1,0:T(8,128)(2,1)}, u32[]{:S(2)}, u32[]{:S(2)}) collective-permute-start(bf16[256,768]{1,0:T(8,128)(2,1)S(1)} %get-tuple-element.110.refs_0_), channel_id=1, source_target_pairs={{0,16},{8,24},{16,0},{24,8},{1,17},{9,25},{17,1},{25,9},{2,18},{10... | collective-permute-start | bytes 1179656 | tf_op jit(solution)/shard_map/ppermute | solution.py:573
  28.0 14.7 %collective-permute-start.7 = (bf16[128,576]{0,1:T(8,128)(2,1)S(1)}, bf16[128,576]{0,1:T(8,128)(2,1)S(1)}, u32[]{:S(2)}, u32[]{:S(2)}) collective-permute-start(bf16[128,576]{0,1:T(8,128)(2,1)S(1)} %collective-permute-done.3), channel_id=1, source_target_pairs={{0,1},{1,0},{2,3},{3,2},{4,5},{5,4},{6,7},{7,6},{8,9},{9,8},{10,11... | collective-permute-start | bytes 442376 | tf_op jit(solution)/shard_map/ppermute | solution.py:573
  42.9 8.2 %collective-permute-start.9 = (bf16[128,576]{0,1:T(8,128)(2,1)S(1)}, bf16[128,576]{0,1:T(8,128)(2,1)S(1)}, u32[]{:S(2)}, u32[]{:S(2)}) collective-permute-start(bf16[128,576]{0,1:T(8,128)(2,1)S(1)} %collective-permute-done.5), channel_id=1, source_target_pairs={{0,1},{1,0},{2,3},{3,2},{4,5},{5,4},{6,7},{7,6},{8,9},{9,8},{10,11... | collective-permute-start | bytes 442376 | tf_op jit(solution)/shard_map/ppermute | solution.py:573
  48.7 30.6 %collective-permute-start.10 = (bf16[256,768]{1,0:T(8,128)(2,1)S(1)}, bf16[256,768]{1,0:T(8,128)(2,1)}, u32[]{:S(2)}, u32[]{:S(2)}) collective-permute-start(bf16[256,768]{1,0:T(8,128)(2,1)S(1)} %get-tuple-element.110.refs_0_), channel_id=1, source_target_pairs={{0,8},{8,0},{16,24},{24,16},{1,9},{9,1},{17,25},{25,17},{2,10},{10... | collective-permute-start | bytes 1179656 | tf_op jit(solution)/shard_map/ppermute | solution.py:573
  48.9 11.6 %collective-permute-start.14 = (bf16[256,768]{1,0:T(8,128)(2,1)S(1)}, bf16[256,768]{1,0:T(8,128)(2,1)S(1)}, u32[]{:S(2)}, u32[]{:S(2)}) collective-permute-start(bf16[256,768]{1,0:T(8,128)(2,1)S(1)} %get-tuple-element.119.refs_0_), channel_id=1, source_target_pairs={{0,16},{8,24},{16,0},{24,8},{1,17},{9,25},{17,1},{25,9},{2,18},{10... | collective-permute-start | bytes 1179656 | tf_op jit(solution)/shard_map/ppermute | solution.py:573
  49.5 14.1 %collective-permute-start.2 = (bf16[256,768]{1,0:T(8,128)(2,1)}, bf16[256,768]{1,0:T(8,128)(2,1)}, u32[]{:S(2)}, u32[]{:S(2)}) collective-permute-start(bf16[256,768]{1,0:T(8,128)(2,1)} %collective-permute-done.1.refs_2_), channel_id=1, source_target_pairs={{0,8},{8,0},{16,24},{24,16},{1,9},{9,1},{17,25},{25,17},{2,10},{10... | collective-permute-start | bytes 1179656 | tf_op jit(solution)/shard_map/ppermute | solution.py:573
  51.0 28.2 %collective-permute-start.12 = (bf16[256,768]{1,0:T(8,128)(2,1)}, bf16[256,768]{1,0:T(8,128)(2,1)}, u32[]{:S(2)}, u32[]{:S(2)}) collective-permute-start(bf16[256,768]{1,0:T(8,128)(2,1)} %collective-permute-done.11.refs_2_), channel_id=1, source_target_pairs={{0,8},{8,0},{16,24},{24,16},{1,9},{9,1},{17,25},{25,17},{2,10},{10... | collective-permute-start | bytes 1179656 | tf_op jit(solution)/shard_map/ppermute | solution.py:573
  51.6 45.2 %collective-permute-start.13 = (bf16[256,768]{1,0:T(8,128)(2,1)S(1)}, bf16[256,768]{1,0:T(8,128)(2,1)S(1)}, u32[]{:S(2)}, u32[]{:S(2)}) collective-permute-start(bf16[256,768]{1,0:T(8,128)(2,1)S(1)} %get-tuple-element.119.refs_0_), channel_id=1, source_target_pairs={{0,8},{8,0},{16,24},{24,16},{1,9},{9,1},{17,25},{25,17},{2,10},{10... | collective-permute-start | bytes 1179656 | tf_op jit(solution)/shard_map/ppermute | solution.py:573
  60.5 36.3 %collective-permute-start.15 = (bf16[256,768]{1,0:T(8,128)(2,1)S(1)}, bf16[256,768]{1,0:T(8,128)(2,1)}, u32[]{:S(2)}, u32[]{:S(2)}) collective-permute-start(bf16[256,768]{1,0:T(8,128)(2,1)S(1)} %collective-permute-done.14.refs_2_), channel_id=1, source_target_pairs={{0,8},{8,0},{16,24},{24,16},{1,9},{9,1},{17,25},{25,17},{2,10},{10... | collective-permute-start | bytes 1179656 | tf_op jit(solution)/shard_map/ppermute | solution.py:573
  79.3 17.5 %collective-permute-start.16 = (bf16[256,192]{1,0:T(8,128)(2,1)}, bf16[256,192]{1,0:T(8,128)(2,1)S(1)}, u32[]{:S(2)}, u32[]{:S(2)}) collective-permute-start(bf16[256,192]{1,0:T(8,128)(2,1)} %get-tuple-element.116), channel_id=1, source_target_pairs={{0,8},{8,0},{16,24},{24,16},{1,9},{9,1},{17,25},{25,17},{2,10},{10... | collective-permute-start | bytes 294920 | tf_op jit(solution)/shard_map/ppermute | solution.py:573
  79.9 16.9 %collective-permute-start.17 = (bf16[256,192]{1,0:T(8,128)(2,1)}, bf16[256,192]{1,0:T(8,128)(2,1)S(1)}, u32[]{:S(2)}, u32[]{:S(2)}) collective-permute-start(bf16[256,192]{1,0:T(8,128)(2,1)} %get-tuple-element.117), channel_id=1, source_target_pairs={{0,16},{8,24},{16,0},{24,8},{1,17},{9,25},{17,1},{25,9},{2,18},{10... | collective-permute-start | bytes 294920 | tf_op jit(solution)/shard_map/ppermute | solution.py:573
  80.4 16.5 %collective-permute-start.18 = (bf16[256,192]{1,0:T(8,128)(2,1)}, bf16[256,192]{1,0:T(8,128)(2,1)S(1)}, u32[]{:S(2)}, u32[]{:S(2)}) collective-permute-start(bf16[256,192]{1,0:T(8,128)(2,1)} %get-tuple-element.118), channel_id=1, source_target_pairs={{0,24},{8,16},{16,8},{24,0},{1,25},{9,17},{17,9},{25,1},{2,26},{10... | collective-permute-start | bytes 294920 | tf_op jit(solution)/shard_map/ppermute | solution.py:573
  106.9 17.8 %collective-permute-start.19 = (bf16[8,432,768]{2,1,0:T(8,128)(2,1)}, bf16[8,432,768]{2,1,0:T(8,128)(2,1)}, u32[]{:S(2)}, u32[]{:S(2)}) collective-permute-start(bf16[8,432,768]{2,1,0:T(8,128)(2,1)} %bitcast.179), channel_id=1, source_target_pairs={{0,8},{8,0},{16,24},{24,16},{1,9},{9,1},{17,25},{25,17},{2,10},{10... | collective-permute-start | bytes 15925256 | tf_op jit(solution)/shard_map/ppermute | solution.py:573
  107.7 8.8 %collective-permute-start.20 = (bf16[256,192]{1,0:T(8,128)(2,1)S(1)}, bf16[256,192]{1,0:T(8,128)(2,1)S(1)}, u32[]{:S(2)}, u32[]{:S(2)}) collective-permute-start(bf16[256,192]{1,0:T(8,128)(2,1)S(1)} %copy-done.65), channel_id=1, source_target_pairs={{0,8},{8,0},{16,24},{24,16},{1,9},{9,1},{17,25},{25,17},{2,10},{10... | collective-permute-start | bytes 294920 | tf_op jit(solution)/shard_map/ppermute | solution.py:573
  107.7 9.2 %collective-permute-start.21 = (bf16[256,192]{1,0:T(8,128)(2,1)S(1)}, bf16[256,192]{1,0:T(8,128)(2,1)S(1)}, u32[]{:S(2)}, u32[]{:S(2)}) collective-permute-start(bf16[256,192]{1,0:T(8,128)(2,1)S(1)} %copy-done.60), channel_id=1, source_target_pairs={{0,16},{8,24},{16,0},{24,8},{1,17},{9,25},{17,1},{25,9},{2,18},{10... | collective-permute-start | bytes 294920 | tf_op jit(solution)/shard_map/ppermute | solution.py:573
  111.2 7.5 %collective-permute-start.22 = (bf16[256,192]{1,0:T(8,128)(2,1)S(1)}, bf16[256,192]{1,0:T(8,128)(2,1)S(1)}, u32[]{:S(2)}, u32[]{:S(2)}) collective-permute-start(bf16[256,192]{1,0:T(8,128)(2,1)S(1)} %copy-done.54), channel_id=1, source_target_pairs={{0,24},{8,16},{16,8},{24,0},{1,25},{9,17},{17,9},{25,1},{2,26},{10... | collective-permute-start | bytes 294920 | tf_op jit(solution)/shard_map/ppermute | solution.py:573
  116.9 7.7 %collective-permute-start.25 = (bf16[256,192]{1,0:T(8,128)(2,1)}, bf16[256,192]{1,0:T(8,128)(2,1)S(1)}, u32[]{:S(2)}, u32[]{:S(2)}) collective-permute-start(bf16[256,192]{1,0:T(8,128)(2,1)} %get-tuple-element.132), channel_id=1, source_target_pairs={{0,24},{8,16},{16,8},{24,0},{1,25},{9,17},{17,9},{25,1},{2,26},{10... | collective-permute-start | bytes 294920 | tf_op jit(solution)/shard_map/ppermute | solution.py:573
  196.5 8.9 %collective-permute-start.29 = (bf16[8,432,768]{2,1,0:T(8,128)(2,1)S(1)}, bf16[8,432,768]{2,1,0:T(8,128)(2,1)S(1)}, u32[]{:S(2)}, u32[]{:S(2)}) collective-permute-start(bf16[8,432,768]{2,1,0:T(8,128)(2,1)S(1)} %pad_maximum_fusion), channel_id=1, source_target_pairs={{0,8},{8,0},{16,24},{24,16},{1,9},{9,1},{17,25},{25,17},{2,10},{10... | collective-permute-start | bytes 15925256 | tf_op jit(solution)/shard_map/ppermute | solution.py:573
  197.0 11.9 %collective-permute-start.26 = (bf16[256,192]{1,0:T(8,128)(2,1)S(1)}, bf16[256,192]{1,0:T(8,128)(2,1)S(1)}, u32[]{:S(2)}, u32[]{:S(2)}) collective-permute-start(bf16[256,192]{1,0:T(8,128)(2,1)S(1)} %copy-done.63), channel_id=1, source_target_pairs={{0,8},{8,0},{16,24},{24,16},{1,9},{9,1},{17,25},{25,17},{2,10},{10... | collective-permute-start | bytes 294920 | tf_op jit(solution)/shard_map/ppermute | solution.py:573
  197.3 11.5 %collective-permute-start.27 = (bf16[256,192]{1,0:T(8,128)(2,1)S(1)}, bf16[256,192]{1,0:T(8,128)(2,1)S(1)}, u32[]{:S(2)}, u32[]{:S(2)}) collective-permute-start(bf16[256,192]{1,0:T(8,128)(2,1)S(1)} %copy-done.62), channel_id=1, source_target_pairs={{0,16},{8,24},{16,0},{24,8},{1,17},{9,25},{17,1},{25,9},{2,18},{10... | collective-permute-start | bytes 294920 | tf_op jit(solution)/shard_map/ppermute | solution.py:573
  197.8 11.0 %collective-permute-start.28 = (bf16[256,192]{1,0:T(8,128)(2,1)S(1)}, bf16[256,192]{1,0:T(8,128)(2,1)S(1)}, u32[]{:S(2)}, u32[]{:S(2)}) collective-permute-start(bf16[256,192]{1,0:T(8,128)(2,1)S(1)} %copy-done.59), channel_id=1, source_target_pairs={{0,24},{8,16},{16,8},{24,0},{1,25},{9,17},{17,9},{25,1},{2,26},{10... | collective-permute-start | bytes 294920 | tf_op jit(solution)/shard_map/ppermute | solution.py:573
  211.1 24.8 %collective-permute-start.33 = (bf16[256,192]{1,0:T(8,128)(2,1)S(1)}, bf16[256,192]{1,0:T(8,128)(2,1)S(1)}, u32[]{:S(2)}, u32[]{:S(2)}) collective-permute-start(bf16[256,192]{1,0:T(8,128)(2,1)S(1)} %copy-done.45), channel_id=1, source_target_pairs={{0,8},{8,0},{16,24},{24,16},{1,9},{9,1},{17,25},{25,17},{2,10},{10... | collective-permute-start | bytes 294920 | tf_op jit(solution)/shard_map/ppermute | solution.py:573
  211.5 25.5 %collective-permute-start.34 = (bf16[256,192]{1,0:T(8,128)(2,1)S(1)}, bf16[256,192]{1,0:T(8,128)(2,1)S(1)}, u32[]{:S(2)}, u32[]{:S(2)}) collective-permute-start(bf16[256,192]{1,0:T(8,128)(2,1)S(1)} %copy-done.44), channel_id=1, source_target_pairs={{0,16},{8,24},{16,0},{24,8},{1,17},{9,25},{17,1},{25,9},{2,18},{10... | collective-permute-start | bytes 294920 | tf_op jit(solution)/shard_map/ppermute | solution.py:573
  212.0 25.0 %collective-permute-start.35 = (bf16[256,192]{1,0:T(8,128)(2,1)S(1)}, bf16[256,192]{1,0:T(8,128)(2,1)S(1)}, u32[]{:S(2)}, u32[]{:S(2)}) collective-permute-start(bf16[256,192]{1,0:T(8,128)(2,1)S(1)} %copy-done.43), channel_id=1, source_target_pairs={{0,24},{8,16},{16,8},{24,0},{1,25},{9,17},{17,9},{25,1},{2,26},{10... | collective-permute-start | bytes 294920 | tf_op jit(solution)/shard_map/ppermute | solution.py:573
  213.0 50.1 %collective-permute-start.39 = (bf16[256,192]{1,0:T(8,128)(2,1)S(1)}, bf16[256,192]{1,0:T(8,128)(2,1)S(1)}, u32[]{:S(2)}, u32[]{:S(2)}) collective-permute-start(bf16[256,192]{1,0:T(8,128)(2,1)S(1)} %copy-done.42), channel_id=1, source_target_pairs={{0,8},{8,0},{16,24},{24,16},{1,9},{9,1},{17,25},{25,17},{2,10},{10... | collective-permute-start | bytes 294920 | tf_op jit(solution)/shard_map/ppermute | solution.py:573
  213.6 49.9 %collective-permute-start.40 = (bf16[256,192]{1,0:T(8,128)(2,1)S(1)}, bf16[256,192]{1,0:T(8,128)(2,1)S(1)}, u32[]{:S(2)}, u32[]{:S(2)}) collective-permute-start(bf16[256,192]{1,0:T(8,128)(2,1)S(1)} %copy-done.41), channel_id=1, source_target_pairs={{0,16},{8,24},{16,0},{24,8},{1,17},{9,25},{17,1},{25,9},{2,18},{10... | collective-permute-start | bytes 294920 | tf_op jit(solution)/shard_map/ppermute | solution.py:573
  236.0 27.7 %collective-permute-start.41 = (bf16[256,192]{1,0:T(8,128)(2,1)S(1)}, bf16[256,192]{1,0:T(8,128)(2,1)S(1)}, u32[]{:S(2)}, u32[]{:S(2)}) collective-permute-start(bf16[256,192]{1,0:T(8,128)(2,1)S(1)} %copy-done.40), channel_id=1, source_target_pairs={{0,24},{8,16},{16,8},{24,0},{1,25},{9,17},{17,9},{25,1},{2,26},{10... | collective-permute-start | bytes 294920 | tf_op jit(solution)/shard_map/ppermute | solution.py:573
  237.0 26.7 %collective-permute-start.30 = (bf16[256,768]{1,0:T(8,128)(2,1)}, bf16[256,768]{1,0:T(8,128)(2,1)S(1)}, u32[]{:S(2)}, u32[]{:S(2)}) collective-permute-start(bf16[256,768]{1,0:T(8,128)(2,1)} %get-tuple-element.154), channel_id=1, source_target_pairs={{0,8},{8,0},{16,24},{24,16},{1,9},{9,1},{17,25},{25,17},{2,10},{10... | collective-permute-start | bytes 1179656 | tf_op jit(solution)/shard_map/ppermute | solution.py:573
  237.8 25.9 %collective-permute-start.31 = (bf16[256,768]{1,0:T(8,128)(2,1)}, bf16[256,768]{1,0:T(8,128)(2,1)S(1)}, u32[]{:S(2)}, u32[]{:S(2)}) collective-permute-start(bf16[256,768]{1,0:T(8,128)(2,1)} %get-tuple-element.156), channel_id=1, source_target_pairs={{0,8},{8,0},{16,24},{24,16},{1,9},{9,1},{17,25},{25,17},{2,10},{10... | collective-permute-start | bytes 1179656 | tf_op jit(solution)/shard_map/ppermute | solution.py:573
  263.0 24.2 %collective-permute-start.37 = (bf16[256,768]{1,0:T(8,128)(2,1)}, bf16[256,768]{1,0:T(8,128)(2,1)}, u32[]{:S(2)}, u32[]{:S(2)}) collective-permute-start(bf16[256,768]{1,0:T(8,128)(2,1)} %get-tuple-element.173), channel_id=1, source_target_pairs={{0,8},{8,0},{16,24},{24,16},{1,9},{9,1},{17,25},{25,17},{2,10},{10... | collective-permute-start | bytes 1179656 | tf_op jit(solution)/shard_map/ppermute | solution.py:573
  263.6 43.9 %collective-permute-start.36 = (bf16[256,768]{1,0:T(8,128)(2,1)}, bf16[256,768]{1,0:T(8,128)(2,1)}, u32[]{:S(2)}, u32[]{:S(2)}) collective-permute-start(bf16[256,768]{1,0:T(8,128)(2,1)} %get-tuple-element.171), channel_id=1, source_target_pairs={{0,8},{8,0},{16,24},{24,16},{1,9},{9,1},{17,25},{25,17},{2,10},{10... | collective-permute-start | bytes 1179656 | tf_op jit(solution)/shard_map/ppermute | solution.py:573
  283.6 33.9 %collective-permute-start.45 = (bf16[4,96,576]{2,1,0:T(8,128)(2,1)S(1)}, bf16[4,96,576]{2,1,0:T(8,128)(2,1)}, u32[]{:S(2)}, u32[]{:S(2)}) collective-permute-start(bf16[4,96,576]{2,1,0:T(8,128)(2,1)S(1)} %fusion.27), channel_id=1, source_target_pairs={{0,1},{1,0},{2,3},{3,2},{4,5},{5,4},{6,7},{7,6},{8,9},{9,8},{10,11... | collective-permute-start | bytes 1327112 | tf_op jit(solution)/shard_map/ppermute | solution.py:573
  284.3 20.0 %collective-permute-start.46 = (f32[4,32,96]{2,1,0:T(8,128)S(1)}, f32[4,32,96]{2,1,0:T(8,128)S(1)}, u32[]{:S(2)}, u32[]{:S(2)}) collective-permute-start(f32[4,32,96]{2,1,0:T(8,128)S(1)} %dynamic-slice_bitcast_fusion.6), channel_id=1, source_target_pairs={{0,1},{1,0},{2,3},{3,2},{4,5},{5,4},{6,7},{7,6},{8,9},{9,8},{10,11... | collective-permute-start | bytes 147464 | tf_op jit(solution)/shard_map/ppermute | solution.py:573
  286.5 18.8 %collective-permute-start.32 = (bf16[256,768]{1,0:T(8,128)(2,1)S(1)}, bf16[256,768]{1,0:T(8,128)(2,1)S(1)}, u32[]{:S(2)}, u32[]{:S(2)}) collective-permute-start(bf16[256,768]{1,0:T(8,128)(2,1)S(1)} %add_convert_fusion.3), channel_id=1, source_target_pairs={{0,16},{8,24},{16,0},{24,8},{1,17},{9,25},{17,1},{25,9},{2,18},{10... | collective-permute-start | bytes 1179656 | tf_op jit(solution)/shard_map/ppermute | solution.py:573
  287.2 17.1 %collective-permute-start.43 = (bf16[256,768]{1,0:T(8,128)(2,1)}, bf16[256,768]{1,0:T(8,128)(2,1)S(1)}, u32[]{:S(2)}, u32[]{:S(2)}) collective-permute-start(bf16[256,768]{1,0:T(8,128)(2,1)} %get-tuple-element.190), channel_id=1, source_target_pairs={{0,8},{8,0},{16,24},{24,16},{1,9},{9,1},{17,25},{25,17},{2,10},{10... | collective-permute-start | bytes 1179656 | tf_op jit(solution)/shard_map/ppermute | solution.py:573
  304.3 12.0 %collective-permute-start.38 = (bf16[256,768]{1,0:T(8,128)(2,1)S(1)}, bf16[256,768]{1,0:T(8,128)(2,1)S(1)}, u32[]{:S(2)}, u32[]{:S(2)}) collective-permute-start(bf16[256,768]{1,0:T(8,128)(2,1)S(1)} %add_convert_fusion.2), channel_id=1, source_target_pairs={{0,16},{8,24},{16,0},{24,8},{1,17},{9,25},{17,1},{25,9},{2,18},{10... | collective-permute-start | bytes 1179656 | tf_op jit(solution)/shard_map/ppermute | solution.py:573
  304.3 27.0 %collective-permute-start.42 = (bf16[256,768]{1,0:T(8,128)(2,1)}, bf16[256,768]{1,0:T(8,128)(2,1)}, u32[]{:S(2)}, u32[]{:S(2)}) collective-permute-start(bf16[256,768]{1,0:T(8,128)(2,1)} %get-tuple-element.188), channel_id=1, source_target_pairs={{0,8},{8,0},{16,24},{24,16},{1,9},{9,1},{17,25},{25,17},{2,10},{10... | collective-permute-start | bytes 1179656 | tf_op jit(solution)/shard_map/ppermute | solution.py:573
  305.3 26.0 %collective-permute-start.44 = (bf16[256,768]{1,0:T(8,128)(2,1)}, bf16[256,768]{1,0:T(8,128)(2,1)}, u32[]{:S(2)}, u32[]{:S(2)}) collective-permute-start(bf16[256,768]{1,0:T(8,128)(2,1)} %add_convert_fusion.1), channel_id=1, source_target_pairs={{0,16},{8,24},{16,0},{24,8},{1,17},{9,25},{17,1},{25,9},{2,18},{10... | collective-permute-start | bytes 1179656 | tf_op jit(solution)/shard_map/ppermute | solution.py:573
  319.7 26.9 %all-to-all-start = ((bf16[4,128,576]{1,2,0:T(8,128)(2,1)}), bf16[4,128,576]{1,2,0:T(8,128)(2,1)}, u32[]{:S(2)}, u32[]{:S(2)}) async-start(bf16[4,128,576]{1,2,0:T(8,128)(2,1)} %copy.150), calls=%async_computation | async-start | bytes 1179648 | tf_op jit(solution)/shard_map/all_to_all | solution.py:606
  360.9 17.2 %collective-permute-start.49 = (bf16[432,768]{1,0:T(8,128)(2,1)}, bf16[432,768]{1,0:T(8,128)(2,1)S(1)}, u32[]{:S(2)}, u32[]{:S(2)}) collective-permute-start(bf16[432,768]{1,0:T(8,128)(2,1)} %reduce-scatter.2.cloned.1.call-done), channel_id=1, source_target_pairs={{0,16},{8,24},{16,0},{24,8},{1,17},{9,25},{17,1},{25,9},{2,18},{10... | collective-permute-start | bytes 1990664 | tf_op jit(solution)/shard_map/ppermute | solution.py:573
  (84 other events, 515.4 us)
Sparse Core Ops, SparseCore 0:
  11.3 92.7 all-gather.2
  209.1 107.5 reduce-scatter.1
